TPU v7x, 32 devices: a whole 2x2x4 slice. The times are simulated.
32 devices in a mesh: dp: 8 (over z, y), tensor: 4 (over x, core).
Axes of the slice: x: 2, y: 2, z: 4, core: 2. Of those that a mesh axis runs over, the one named last changes fastest.
Arguments:
- tokens: bfloat16 [8192, 2048], P(('dp', 'tensor')), may hold values from -6 to 6
- prefix: int32 [8], P('dp'), may hold values from 102 to 512
- query_weight: bfloat16 [2048, 2048], P('dp', 'tensor'), may hold values from -0.125 to 0.125
- key_weight: bfloat16 [2048, 2048], P('dp', 'tensor'), may hold values from -0.25 to 0.25
- value_weight: bfloat16 [2048, 2048], P('dp', 'tensor'), may hold values from -0.125 to 0.125
- out_weight: bfloat16 [2048, 2048], P('tensor', 'dp'), may hold values from -1 to 1
- query_bias: bfloat16 [16, 128], P('tensor', 'dp'), may hold values from -1.75 to 1.75
- value_bias: bfloat16 [16, 128], P('tensor', 'dp'), may hold values from -1.75 to 1.75
- up_weight: bfloat16 [2048, 8192], P('dp', 'tensor'), may hold values from -0.125 to 0.125
- down_weight: bfloat16 [8192, 2048], P('tensor', 'dp'), may hold values from -0.0625 to 0.0625
- up_bias: bfloat16 [64, 128], P('tensor', 'dp'), may hold values from -3 to 3
- norm1_gain: bfloat16 [2048], P('dp'), may hold values from 0.5 to 1.5
- norm1_bias: bfloat16 [2048], P('dp'), may hold values from -1.75 to 1.75
- norm2_gain: bfloat16 [2048], P('dp'), may hold values from 0.5 to 1.5
- norm2_bias: bfloat16 [2048], P('dp'), may hold values from -1.75 to 1.75
- out_bias: bfloat16 [2048], P('dp'), may hold values from -1.75 to 1.75
- down_bias: bfloat16 [2048], P('dp'), may hold values from -1.75 to 1.75
- cotangent: bfloat16 [8192, 2048], P(('dp', 'tensor')), may hold values from -12 to 12
Outputs:
- layer_out: bfloat16 [8192, 2048], P(('dp', 'tensor'))
- input_grad: float32 [8192, 2048], P(('dp', 'tensor'))
- query_weight_grad: float32 [2048, 2048], P('dp', 'tensor')
- key_weight_grad: float32 [2048, 2048], P('dp', 'tensor')
- value_weight_grad: float32 [2048, 2048], P('dp', 'tensor')
- out_weight_grad: float32 [2048, 2048], P('tensor', 'dp')
- query_bias_grad: float32 [16, 128], P('tensor', 'dp')
- value_bias_grad: float32 [16, 128], P('tensor', 'dp')
- up_weight_grad: float32 [2048, 8192], P('dp', 'tensor')
- down_weight_grad: float32 [8192, 2048], P('tensor', 'dp')
- up_bias_grad: float32 [64, 128], P('tensor', 'dp')
- norm1_gain_grad: float32 [2048], P(('dp', 'tensor'))
- norm1_bias_grad: float32 [2048], P(('dp', 'tensor'))
- norm2_gain_grad: float32 [2048], P(('dp', 'tensor'))
- norm2_bias_grad: float32 [2048], P(('dp', 'tensor'))
- out_bias_grad: float32 [2048], P(('dp', 'tensor'))
- down_bias_grad: float32 [2048], P(('dp', 'tensor'))
Inputs may be any that keep to these rules, and one draw needn't show every extreme that they name: Token j of a sequence is seen by token i when j <= i or j lies in the sequence's first prefix tokens.
All inputs are finite; a program needn't handle non-finite values.
Results may differ from a plain program's by a relative error of at most 0.012.
The roundings to bfloat16 on the way count: a program that leaves them out, or rounds other values in their place, can miss the bound.
Values may be sent and summed in bfloat16 or wider, within the bound.
A program may use at most 192 MiB of HBM per device.

v0:
```python
import jax
import jax.numpy as jnp
from jax import lax
from jax.sharding import PartitionSpec as P


def layer_norm(rows, gain, shift):
    center = rows - jnp.mean(rows, axis=-1, keepdims=True)
    spread = jnp.mean(center * center, axis=-1, keepdims=True)
    return center * lax.rsqrt(spread + 1e-05) * gain + shift


def gelu_exact(values):
    return jax.nn.gelu(values, approximate=False)


def head_major(matrix, heads):
    return matrix.reshape(matrix.shape[0], heads, -1).transpose(1, 0, 2)


def row_major(stacked):
    return stacked.transpose(1, 0, 2).reshape(stacked.shape[1], -1)


def masked_scores(q_block, keys, start, prefix_len):
    scores = jnp.einsum("hqd,hkd->hqk", q_block, keys, preferred_element_type=jnp.float32)
    rows = start + lax.broadcasted_iota(jnp.int32, scores.shape[1:], 0)
    cols = lax.broadcasted_iota(jnp.int32, scores.shape[1:], 1)
    seen = (cols <= rows) | (cols < prefix_len)
    return jnp.where(seen[None], scores, -1e30)


def to_blocks(stacked, count):
    heads, length = (stacked.shape[0], stacked.shape[1])
    return stacked.reshape((heads, count, length // count) + stacked.shape[2:]).swapaxes(0, 1)


def from_blocks(blocked):
    count, heads, block = (blocked.shape[0], blocked.shape[1], blocked.shape[2])
    return blocked.swapaxes(0, 1).reshape((heads, count * block) + blocked.shape[3:])


def contract_rows(left, right):
    return jnp.einsum("ld,le->de", left, right, preferred_element_type=jnp.float32)


def times_transpose(left, right):
    return jnp.einsum("le,de->ld", left, right, preferred_element_type=jnp.float32)


def local(
    tokens,
    prefix,
    query_weight,
    key_weight,
    value_weight,
    out_weight,
    query_bias,
    value_bias,
    up_weight,
    down_weight,
    up_bias,
    norm1_gain,
    norm1_bias,
    norm2_gain,
    norm2_bias,
    out_bias,
    down_bias,
    cotangent,
):
    f32 = jnp.float32
    bf16 = jnp.bfloat16
    wq, wk, wv, wo, bq, bv, g1, n1, g2, n2, bo, b2 = (
        lax.all_gather(query_weight, "dp", axis=0, tiled=True),
        lax.all_gather(key_weight, "dp", axis=0, tiled=True),
        lax.all_gather(value_weight, "dp", axis=0, tiled=True),
        lax.all_gather(out_weight, "dp", axis=1, tiled=True),
        lax.all_gather(query_bias, "dp", axis=1, tiled=True),
        lax.all_gather(value_bias, "dp", axis=1, tiled=True),
        lax.all_gather(norm1_gain, "dp", axis=0, tiled=True),
        lax.all_gather(norm1_bias, "dp", axis=0, tiled=True),
        lax.all_gather(norm2_gain, "dp", axis=0, tiled=True),
        lax.all_gather(norm2_bias, "dp", axis=0, tiled=True),
        lax.all_gather(out_bias, "dp", axis=0, tiled=True),
        lax.all_gather(down_bias, "dp", axis=0, tiled=True),
    )
    w1, w2, b1 = (
        lax.all_gather(up_weight, "dp", axis=0, tiled=True),
        lax.all_gather(down_weight, "dp", axis=1, tiled=True),
        lax.all_gather(up_bias, "dp", axis=1, tiled=True),
    )
    g1f, n1f, g2f, n2f = (g1.astype(f32), n1.astype(f32), g2.astype(f32), n2.astype(f32))
    bof, b2f = (bo.astype(f32), b2.astype(f32))
    heads = bq.shape[0]
    head_size = bq.shape[1]
    scale = head_size ** (-0.5)
    prefix_len = prefix[0]
    xf = tokens.astype(f32)
    h1 = layer_norm(xf, g1f, n1f).astype(bf16)
    rows1 = lax.all_gather(h1, "tensor", axis=0, tiled=True)
    length = rows1.shape[0]
    block = min(512, length)
    count = length // block
    query = (
        (jnp.dot(rows1, wq, preferred_element_type=f32) + bq.astype(f32).reshape(-1)) * scale
    ).astype(bf16)
    keyed = jnp.dot(rows1, wk, preferred_element_type=f32).astype(bf16)
    valued = (jnp.dot(rows1, wv, preferred_element_type=f32) + bv.astype(f32).reshape(-1)).astype(
        bf16
    )
    q_heads = head_major(query, heads)
    k_heads = head_major(keyed, heads)
    v_heads = head_major(valued, heads)
    q_blocks = to_blocks(q_heads, count)
    starts = jnp.arange(count, dtype=jnp.int32) * block

    def forward_block(item):
        q_block, start = item
        scores = masked_scores(q_block, k_heads, start, prefix_len)
        top = jnp.max(scores, axis=-1, keepdims=True)
        expd = jnp.exp(scores - top)
        total = jnp.sum(expd, axis=-1, keepdims=True)
        probs = (expd / total).astype(bf16)
        outv = jnp.einsum("hqk,hkd->hqd", probs, v_heads, preferred_element_type=f32)
        return (outv.astype(bf16), (top + jnp.log(total))[..., 0])

    o_blocks, lse_blocks = lax.map(forward_block, (q_blocks, starts))
    mixed = row_major(from_blocks(o_blocks))
    attn_part = jnp.dot(mixed, wo, preferred_element_type=f32)
    attn_total = lax.psum_scatter(attn_part, "tensor", scatter_dimension=0, tiled=True)
    second = xf + attn_total + bof
    h2 = layer_norm(second, g2f, n2f).astype(bf16)
    rows2 = lax.all_gather(h2, "tensor", axis=0, tiled=True)
    hidden = jnp.dot(rows2, w1, preferred_element_type=f32) + b1.astype(f32).reshape(-1)
    gated = gelu_exact(hidden).astype(bf16)
    mlp_part = jnp.dot(gated, w2, preferred_element_type=f32)
    mlp_total = lax.psum_scatter(
        mlp_part.astype(jnp.bfloat16), "tensor", scatter_dimension=0, tiled=True
    ).astype(jnp.float32)
    layer_out = (second + mlp_total + b2f).astype(bf16)
    d_out = cotangent.astype(f32)
    g_b2 = jnp.sum(d_out, axis=0)
    d_rows = lax.all_gather(cotangent, "tensor", axis=0, tiled=True)
    d_gated = times_transpose(d_rows, w2)
    d_hidden = jax.vjp(gelu_exact, hidden)[1](d_gated)[0]
    g_b1 = jnp.sum(d_hidden, axis=0).reshape(b1.shape)
    d_hidden_low = d_hidden.astype(bf16)
    d_h2_part = times_transpose(d_hidden_low, w1)
    g_w2 = contract_rows(gated, d_rows)
    g_w1 = contract_rows(rows2, d_hidden_low)
    d_h2 = lax.psum_scatter(d_h2_part, "tensor", scatter_dimension=0, tiled=True)
    norm2_back = jax.vjp(layer_norm, second, g2f, n2f)[1]
    d_second_ln, g_g2, g_n2 = norm2_back(d_h2)
    d_second = d_out + d_second_ln
    g_bo = jnp.sum(d_second, axis=0)
    d_second_low = d_second.astype(bf16)
    back_rows = lax.all_gather(d_second_low, "tensor", axis=0, tiled=True)
    g_wo = contract_rows(mixed, back_rows)
    d_mixed = times_transpose(back_rows, wo).astype(bf16)
    do_blocks = to_blocks(head_major(d_mixed, heads), count)

    def backward_block(carry, item):
        d_keys, d_vals = carry
        q_block, do_block, lse_block, start = item
        scores = masked_scores(q_block, k_heads, start, prefix_len)
        probs = jnp.exp(scores - lse_block[..., None])
        d_probs = jnp.einsum("hqd,hkd->hqk", do_block, v_heads, preferred_element_type=f32)
        d_vals = d_vals + jnp.einsum(
            "hqk,hqd->hkd", probs.astype(bf16), do_block, preferred_element_type=f32
        )
        inner = jnp.sum(probs * d_probs, axis=-1, keepdims=True)
        d_scores = (probs * (d_probs - inner)).astype(bf16)
        d_query = jnp.einsum("hqk,hkd->hqd", d_scores, k_heads, preferred_element_type=f32)
        d_keys = d_keys + jnp.einsum("hqk,hqd->hkd", d_scores, q_block, preferred_element_type=f32)
        return ((d_keys, d_vals), d_query)

    empty = jnp.zeros(k_heads.shape, f32)
    (d_keys, d_vals), dq_blocks = lax.scan(
        backward_block, (empty, empty), (q_blocks, do_blocks, lse_blocks, starts)
    )
    d_query = row_major(from_blocks(dq_blocks)) * scale
    d_keys = row_major(d_keys)
    d_vals = row_major(d_vals)
    g_bq = jnp.sum(d_query, axis=0).reshape(bq.shape)
    g_bv = jnp.sum(d_vals, axis=0).reshape(bv.shape)
    dq_low, dk_low, dv_low = (d_query.astype(bf16), d_keys.astype(bf16), d_vals.astype(bf16))
    g_wq = contract_rows(rows1, dq_low)
    g_wk = contract_rows(rows1, dk_low)
    g_wv = contract_rows(rows1, dv_low)
    d_h1_part = (
        times_transpose(dq_low, wq) + times_transpose(dk_low, wk) + times_transpose(dv_low, wv)
    )
    d_h1 = lax.psum_scatter(d_h1_part, "tensor", scatter_dimension=0, tiled=True)
    norm1_back = jax.vjp(layer_norm, xf, g1f, n1f)[1]
    d_input_ln, g_g1, g_n1 = norm1_back(d_h1)
    input_grad = d_second + d_input_ln
    s_wq, s_wk, s_wv, s_wo, s_bq, s_bv, s_w1, s_w2, s_b1 = (
        lax.psum_scatter(g_wq, "dp", scatter_dimension=0, tiled=True),
        lax.psum_scatter(g_wk, "dp", scatter_dimension=0, tiled=True),
        lax.psum_scatter(g_wv, "dp", scatter_dimension=0, tiled=True),
        lax.psum_scatter(g_wo, "dp", scatter_dimension=1, tiled=True),
        lax.psum_scatter(g_bq, "dp", scatter_dimension=1, tiled=True),
        lax.psum_scatter(g_bv, "dp", scatter_dimension=1, tiled=True),
        lax.psum_scatter(g_w1, "dp", scatter_dimension=0, tiled=True),
        lax.psum_scatter(g_w2, "dp", scatter_dimension=1, tiled=True),
        lax.psum_scatter(g_b1, "dp", scatter_dimension=1, tiled=True),
    )
    s_g1, s_n1, s_g2, s_n2, s_bo, s_b2 = (
        lax.psum_scatter(g_g1, ("dp", "tensor"), scatter_dimension=0, tiled=True),
        lax.psum_scatter(g_n1, ("dp", "tensor"), scatter_dimension=0, tiled=True),
        lax.psum_scatter(g_g2, ("dp", "tensor"), scatter_dimension=0, tiled=True),
        lax.psum_scatter(g_n2, ("dp", "tensor"), scatter_dimension=0, tiled=True),
        lax.psum_scatter(g_bo, ("dp", "tensor"), scatter_dimension=0, tiled=True),
        lax.psum_scatter(g_b2, ("dp", "tensor"), scatter_dimension=0, tiled=True),
    )
    return (
        layer_out,
        input_grad,
        s_wq,
        s_wk,
        s_wv,
        s_wo,
        s_bq,
        s_bv,
        s_w1,
        s_w2,
        s_b1,
        s_g1,
        s_n1,
        s_g2,
        s_n2,
        s_bo,
        s_b2,
    )


def solution(mesh):
    in_specs = (
        P(("dp", "tensor"), None),
        P("dp"),
        P("dp", "tensor"),
        P("dp", "tensor"),
        P("dp", "tensor"),
        P("tensor", "dp"),
        P("tensor", "dp"),
        P("tensor", "dp"),
        P("dp", "tensor"),
        P("tensor", "dp"),
        P("tensor", "dp"),
        P("dp"),
        P("dp"),
        P("dp"),
        P("dp"),
        P("dp"),
        P("dp"),
        P(("dp", "tensor"), None),
    )
    out_specs = (
        P(("dp", "tensor"), None),
        P(("dp", "tensor"), None),
        P("dp", "tensor"),
        P("dp", "tensor"),
        P("dp", "tensor"),
        P("tensor", "dp"),
        P("tensor", "dp"),
        P("tensor", "dp"),
        P("dp", "tensor"),
        P("tensor", "dp"),
        P("tensor", "dp"),
        P(("dp", "tensor")),
        P(("dp", "tensor")),
        P(("dp", "tensor")),
        P(("dp", "tensor")),
        P(("dp", "tensor")),
        P(("dp", "tensor")),
    )
    return jax.shard_map(local, mesh=mesh, in_specs=in_specs, out_specs=out_specs, check_vma=False)
```

profile of v0, /device:TPU:9, one launch (start us, length us, event | category | flops | bytes accessed | tf_op | source)
XLA Modules:
  0.0 2068.3 jit_solution(7735939592882901301)
XLA Ops:
  8.6 14.3 all-gather
  23.6 12.8 all-gather.1
  40.6 2.7 fusion.49
  45.3 15.3 all-gather.2
  60.7 12.4 all-gather.3
  73.2 23.1 %all-gather.19.cloned.1.call-done = bf16[1024,2048]{1,0:T(8,128)(2,1)} async-done(((bf16[256,2048]{1,0:T(8,128)(2,1)}), bf16[1024,2048]{1,0:T(8,128)(2,1)}) %all-gather.19.cloned.1.call-update) | async-done | bytes 4194320 | tf_op jit(solution)/shard_map/all_gather | solution.py:100
  96.3 5.2 multiply_convert_fusion.2
  102.8 43.4 %all-gather.25.cloned.1.call-done = bf16[2048,512]{1,0:T(8,128)(2,1)} async-done(((bf16[256,512]{1,0:T(8,128)(2,1)}), bf16[2048,512]{1,0:T(8,128)(2,1)}) %all-gather.25.cloned.1.call-update) | async-done | bytes 2097168 | tf_op jit(solution)/shard_map/all_gather | solution.py:76
  146.1 5.2 add_convert_fusion.2
  152.0 43.7 %all-gather.23.cloned.1.call-done = bf16[2048,512]{1,0:T(8,128)(2,1)} async-done(((bf16[256,512]{1,0:T(8,128)(2,1)}), bf16[2048,512]{1,0:T(8,128)(2,1)}) %all-gather.23.cloned.1.call-update) | async-done | bytes 2097168 | tf_op jit(solution)/shard_map/all_gather | solution.py:75
  195.8 6.2 convolution_convert_fusion.2
  203.6 18.7 while.27
  209.6 3.4 fusion.142
  218.9 3.4 fusion.142
  222.3 3.0 copy.102
  225.3 19.7 all-gather.27.cloned.1.call-done
  245.0 7.6 fusion.69
  253.7 14.0 all-gather.4
  267.7 13.0 all-gather.5
  280.7 15.5 all-gather.6
  296.3 28.5 %reduce-scatter.20.cloned.1.call-done = f32[256,2048]{1,0:T(8,128)} async-done(((f32[1024,2048]{1,0:T(8,128)}), f32[256,2048]{1,0:T(8,128)}) %reduce-scatter.20.cloned.1.call-update) | async-done | bytes 2097168 | tf_op jit(solution)/shard_map/reduce_scatter | solution.py:130
  331.0 22.7 %all_gather.71 = bf16[16,128]{0,1:T(8,128)(2,1)S(1)} all-gather(bf16[16,16]{0,1:T(8,128)(2,1)S(1)} %copy.103), channel_id=1, replica_groups=mesh['dp'=8,'tensor'=4] {'dp'}, dimensions={1}, use_global_device_ids=true | all-gather | bytes 4608 | tf_op jit(solution)/shard_map/all_gather | solution.py:90
  353.8 95.5 %all-gather.31.cloned.1.call-done = bf16[2048,2048]{1,0:T(8,128)(2,1)} async-done(((bf16[256,2048]{1,0:T(8,128)(2,1)}), bf16[2048,2048]{1,0:T(8,128)(2,1)}) %all-gather.31.cloned.1.call-update) | async-done | bytes 8388624 | tf_op jit(solution)/shard_map/all_gather | solution.py:88
  449.3 37.8 %all-gather.29.cloned.1.call-done = bf16[1024,2048]{1,0:T(8,128)(2,1)} async-done(((bf16[256,2048]{1,0:T(8,128)(2,1)}), bf16[1024,2048]{1,0:T(8,128)(2,1)}) %all-gather.29.cloned.1.call-update) | async-done | bytes 4194320 | tf_op jit(solution)/shard_map/all_gather | solution.py:133
  487.1 14.4 fusion.70
  501.5 21.6 %all-gather.35.cloned.1.call-done = bf16[1024,2048]{1,0:T(8,128)(2,1)} async-done(((bf16[256,2048]{1,0:T(8,128)(2,1)}), bf16[1024,2048]{1,0:T(8,128)(2,1)}) %all-gather.35.cloned.1.call-update) | async-done | bytes 4194320 | tf_op jit(solution)/shard_map/all_gather | solution.py:143
  523.1 123.9 %all-gather.33.cloned.1.call-done = bf16[2048,2048]{1,0:T(8,128)(2,1)} async-done(((bf16[2048,256]{1,0:T(8,128)(2,1)}), bf16[2048,2048]{1,0:T(8,128)(2,1)}) %all-gather.33.cloned.1.call-update) | async-done | bytes 8388624 | tf_op jit(solution)/shard_map/all_gather | solution.py:89
  647.0 32.9 %fusion.64 = (f32[2048]{0:T(1024)S(1)}, bf16[1024,2048]{1,0:T(8,128)(2,1)S(1)}, f32[1024,2048]{1,0:T(8,128)}) fusion(f32[1024,2048]{1,0:T(8,128)} %fusion.70, f32[2048]{0:T(1024)S(1)} %bitcast_convert_fusion.1, bf16[1024,2048]{1,0:T(8,128)(2,1)} %all-gather.35.cloned.1.call-done, bf16[2048,2048]{1,0:T(8,128)(2,1)} %all-gather.33.cloned.1.call-done), kind=kOutput, calls=%fused_computation.124 | convolution fusion | flops 8745121792 | bytes 33570816 | tf_op jit(solution)/shard_map/le,de->ld/dot_general | solution.py:48
  682.0 13.4 fusion.56
  695.5 8.0 multiply_convert_fusion.1
  705.7 13.8 convolution_convert_fusion
  720.2 15.0 all-gather.7
  735.3 32.3 %reduce-scatter.24.cloned.1.call-done = f32[256,2048]{1,0:T(8,128)} async-done(((f32[1024,2048]{1,0:T(8,128)}), f32[256,2048]{1,0:T(8,128)}) %reduce-scatter.24.cloned.1.call-update) | async-done | bytes 2097168 | tf_op jit(solution)/shard_map/reduce_scatter | solution.py:151
  767.6 2.9 multiply_reduce_fusion.1
  770.5 44.1 %reduce-scatter.22.cloned.1.call-done = bf16[256,2048]{1,0:T(8,128)(2,1)} async-done(((bf16[1024,2048]{1,0:T(8,128)(2,1)}), bf16[256,2048]{1,0:T(8,128)(2,1)}) %reduce-scatter.22.cloned.1.call-update) | async-done | bytes 1048592 | tf_op jit(solution)/shard_map/reduce_scatter | solution.py:137
  814.6 3.7 fusion.66
  822.2 33.9 %all-gather.37.cloned.1.call-done = bf16[1024,2048]{1,0:T(8,128)(2,1)} async-done(((bf16[256,2048]{1,0:T(8,128)(2,1)}), bf16[1024,2048]{1,0:T(8,128)(2,1)}) %all-gather.37.cloned.1.call-update) | async-done | bytes 4194320 | tf_op jit(solution)/shard_map/all_gather | solution.py:157
  856.0 5.2 convolution_convert_fusion.1
  862.6 48.7 %while.28 = (s32[]{:T(128)}, f32[4,1024,128]{2,1,0:T(8,128)}, f32[4,1024,128]{2,1,0:T(8,128)}, f32[2,4,512,128]{3,2,0,1:T(8,128)}, s32[2]{0:T(128)S(1)}, /*index...) while((s32[]{:T(128)}, f32[4,1024,128]{2,1,0:T(8,128)}, ...), condition=%wide.region_15.16_spmd.clone, body=%wide.region_13.15_spmd.clone.sunk | while | flops 2712665600 | bytes 172031280 | solution.py:178
  866.4 3.1 multiply_reduce_fusion.6
  875.9 5.2 select_add_fusion.4
  881.0 5.2 select_add_fusion.5
  890.0 3.1 multiply_reduce_fusion.6
  899.5 5.8 select_add_fusion.4
  905.3 5.9 select_add_fusion.5
  917.6 2.8 multiply_reduce_fusion.4
  924.9 4.5 fusion.71
  931.8 5.8 add_add_fusion
  937.6 6.6 fusion.75
  945.5 6.5 fusion.76
  953.2 6.6 fusion.73
  959.9 6.6 fusion.74
  966.6 15.2 fusion.54
  982.1 15.3 fusion.77
  1000.3 48.4 %reduce-scatter.40.cloned.1.call-done = f32[16,4]{1,0:T(8,128)} async-done(((f32[128,4]{1,0:T(8,128)}), f32[16,4]{1,0:T(8,128)}) %reduce-scatter.40.cloned.1.call-update) | async-done | bytes 272
  1050.1 73.5 %reduce-scatter.26.cloned.1.call-done = f32[256,2048]{1,0:T(8,128)} async-done(((f32[1024,2048]{1,0:T(8,128)}), f32[256,2048]{1,0:T(8,128)}) %reduce-scatter.26.cloned.1.call-update) | async-done | bytes 2097168 | tf_op jit(solution)/shard_map/reduce_scatter | solution.py:193
  1128.5 2.6 convert_reduce_fusion.1
  1131.1 43.2 %all-reduce.6 = (f32[2048]{0:T(1024)S(1)}, f32[2048]{0:T(1024)S(1)}, f32[2048]{0:T(1024)S(1)}, f32[2048]{0:T(1024)S(1)}, f32[2048]{0:T(1024)S(1)}, /*index=5*/f32[2048]{0:T(1024)S(1)}) all-reduce(f32[2048]{0:T(1024)S(1)} %get-tuple-element.238, ...), channel_id=15, replica_groups=mesh['dp'=8,'tensor'=4] {'dp','tensor'}, use_global_device_ids=true, to_apply=%region_32.33.clone | all-reduce | flops 12288 | bytes 98304
  1177.7 39.9 %reduce-scatter.32.cloned.1.call-done = f32[256,512]{1,0:T(8,128)} async-done(((f32[2048,512]{1,0:T(8,128)}), f32[256,512]{1,0:T(8,128)}) %reduce-scatter.32.cloned.1.call-update) | async-done | bytes 524304 | tf_op jit(solution)/shard_map/reduce_scatter | solution.py:200
  1217.6 92.6 %reduce-scatter.34.cloned.1.call-done = f32[512,256]{1,0:T(8,128)} async-done(((f32[512,2048]{1,0:T(8,128)}), f32[512,256]{1,0:T(8,128)}) %reduce-scatter.34.cloned.1.call-update) | async-done | bytes 524304 | tf_op jit(solution)/shard_map/reduce_scatter | solution.py:201
  1310.1 92.0 %reduce-scatter.28.cloned.1.call-done = f32[256,512]{1,0:T(8,128)} async-done(((f32[2048,512]{1,0:T(8,128)}), f32[256,512]{1,0:T(8,128)}) %reduce-scatter.28.cloned.1.call-update) | async-done | bytes 524304 | tf_op jit(solution)/shard_map/reduce_scatter | solution.py:198
  1402.2 92.1 %reduce-scatter.30.cloned.1.call-done = f32[256,512]{1,0:T(8,128)} async-done(((f32[2048,512]{1,0:T(8,128)}), f32[256,512]{1,0:T(8,128)}) %reduce-scatter.30.cloned.1.call-update) | async-done | bytes 524304 | tf_op jit(solution)/shard_map/reduce_scatter | solution.py:199
  1494.3 283.5 %reduce-scatter.36.cloned.1.call-done = f32[256,2048]{1,0:T(8,128)} async-done(((f32[2048,2048]{1,0:T(8,128)}), f32[256,2048]{1,0:T(8,128)}) %reduce-scatter.36.cloned.1.call-update) | async-done | bytes 2097168 | tf_op jit(solution)/shard_map/reduce_scatter | solution.py:204
  1777.8 283.7 %reduce-scatter.38.cloned.1.call-done = f32[2048,256]{1,0:T(8,128)} async-done(((f32[2048,2048]{1,0:T(8,128)}), f32[2048,256]{1,0:T(8,128)}) %reduce-scatter.38.cloned.1.call-update) | async-done | bytes 2097168 | tf_op jit(solution)/shard_map/reduce_scatter | solution.py:205
  (271 shorter events, 89.8 us)
Async XLA Ops:
  7.2 38.1 %copy-start.49 = (bf16[4,16]{1,0:T(4,128)(2,1)S(1)}, bf16[4,16]{1,0:T(4,128)(2,1)}, u32[]{:S(2)}) copy-start(bf16[4,16]{1,0:T(4,128)(2,1)} %param.28) | copy-start | bytes 388
  7.2 53.5 %copy-start.50 = (bf16[4,16]{1,0:T(4,128)(2,1)S(1)}, bf16[4,16]{1,0:T(4,128)(2,1)}, u32[]{:S(2)}) copy-start(bf16[4,16]{1,0:T(4,128)(2,1)} %param.29) | copy-start | bytes 388
  7.2 66.0 %all-gather.21.cloned.1.call-start = ((), (), s32[]{:S(2)}) async-start(), calls=%async_computation.14 | async-start | bytes 2359296 | tf_op jit(solution)/shard_map/all_gather | solution.py:74
  7.9 88.4 %all-gather.19.cloned.1.call-start = ((), (), s32[]{:S(2)}) async-start(), calls=%async_computation.13 | async-start | bytes 5242880 | tf_op jit(solution)/shard_map/all_gather | solution.py:100
  23.0 17.1 copy-start.26
  43.3 102.8 %all-gather.25.cloned.1.call-start = ((), (), s32[]{:S(2)}) async-start(), calls=%async_computation.16 | async-start | bytes 2359296 | tf_op jit(solution)/shard_map/all_gather | solution.py:76
  44.1 151.7 %all-gather.23.cloned.1.call-start = ((), (), s32[]{:S(2)}) async-start(), calls=%async_computation.15 | async-start | bytes 2359296 | tf_op jit(solution)/shard_map/all_gather | solution.py:75
  44.6 200.4 %all-gather.27.cloned.1.call-start = ((), (), s32[]{:S(2)}) async-start(), calls=%async_computation.17 | async-start | bytes 2359296 | tf_op jit(solution)/shard_map/all_gather | solution.py:77
  45.2 279.6 %reduce-scatter.20.cloned.1.call-start = ((), (), s32[]{:S(2)}) async-start(), calls=%async_computation.18 | async-start | bytes 10485760 | tf_op jit(solution)/shard_map/reduce_scatter | solution.py:130
  222.2 30.3 %copy-start.3 = (bf16[4,1024,128]{2,1,0:T(8,128)(2,1)}, bf16[4,1024,128]{2,1,0:T(8,128)(2,1)S(1)}, u32[]{:S(2)}) copy-start(bf16[4,1024,128]{2,1,0:T(8,128)(2,1)S(1)} %get-tuple-element.520) | copy-start | bytes 3145732
  222.2 30.3 %copy-start.5 = (bf16[2,4,512,128]{3,2,1,0:T(8,128)(2,1)}, bf16[2,4,512,128]{3,2,1,0:T(8,128)(2,1)S(1)}, u32[]{:S(2)}) copy-start(bf16[2,4,512,128]{3,2,1,0:T(8,128)(2,1)S(1)} %get-tuple-element.521) | copy-start | bytes 3145732
  222.2 30.3 %copy-start.12 = (bf16[4,1024,128]{2,1,0:T(8,128)(2,1)}, bf16[4,1024,128]{2,1,0:T(8,128)(2,1)S(1)}, u32[]{:S(2)}) copy-start(bf16[4,1024,128]{2,1,0:T(8,128)(2,1)S(1)} %get-tuple-element.522) | copy-start | bytes 3145732
  222.2 30.3 %copy-start.30 = (f32[2,4,512]{2,1,0:T(4,128)}, f32[2,4,512]{2,1,0:T(4,128)S(1)}, u32[]{:S(2)}) copy-start(f32[2,4,512]{2,1,0:T(4,128)S(1)} %get-tuple-element.466) | copy-start | bytes 49156
  222.3 30.4 %copy-start.56 = (s32[2]{0:T(128)}, s32[2]{0:T(128)S(1)}, u32[]{:S(2)}) copy-start(s32[2]{0:T(128)S(1)} %get-tuple-element.592) | copy-start | bytes 28
  252.6 15.1 copy-start.53
  252.6 28.1 %copy-start.54 = (bf16[256]{0:T(256)(128)(2,1)S(1)}, bf16[256]{0:T(256)(128)(2,1)}, u32[]{:S(2)}) copy-start(bf16[256]{0:T(256)(128)(2,1)} %param.36) | copy-start | bytes 1540
  252.6 72.2 %copy-start.10 = (bf16[256,2048]{1,0:T(8,128)(2,1)S(1)}, bf16[256,2048]{1,0:T(8,128)(2,1)}, u32[]{:S(2)}) copy-start(bf16[256,2048]{1,0:T(8,128)(2,1)} %param.22) | copy-start | bytes 3145732
  252.7 196.6 %all-gather.31.cloned.1.call-start = ((), (), s32[]{:S(2)}) async-start(), calls=%async_computation.20 | async-start | bytes 9437184 | tf_op jit(solution)/shard_map/all_gather | solution.py:88
  253.4 233.6 %all-gather.29.cloned.1.call-start = ((), (), s32[]{:S(2)}) async-start(), calls=%async_computation.19 | async-start | bytes 5242880 | tf_op jit(solution)/shard_map/all_gather | solution.py:133
  280.7 48.8 %copy-start.28 = (f32[8,1,256]{2,1,0:T(1,128)}, f32[8,1,256]{2,1,0:T(1,128)S(1)}, u32[]{:S(2)}) copy-start(f32[8,1,256]{2,1,0:T(1,128)S(1)} %convert_element_type.131) | copy-start | bytes 24580
  326.8 4.1 copy-start.36
  326.8 4.1 copy-start.48
  328.1 173.5 %copy-start.40 = (f32[256]{0:T(256)}, f32[256]{0:T(256)S(1)}, u32[]{:S(2)}) copy-start(f32[256]{0:T(256)S(1)} %fusion.59) | copy-start | bytes 3076
  329.6 193.6 %all-gather.35.cloned.1.call-start = ((), (), s32[]{:S(2)}) async-start(), calls=%async_computation.23 | async-start | bytes 5242880 | tf_op jit(solution)/shard_map/all_gather | solution.py:143
  330.3 316.7 %all-gather.33.cloned.1.call-start = ((), (), s32[]{:S(2)}) async-start(), calls=%async_computation.21 | async-start | bytes 9437184 | tf_op jit(solution)/shard_map/all_gather | solution.py:89
  330.9 436.7 %reduce-scatter.24.cloned.1.call-start = ((), (), s32[]{:S(2)}) async-start(), calls=%async_computation.24 | async-start | bytes 10485760 | tf_op jit(solution)/shard_map/reduce_scatter | solution.py:151
  695.4 119.1 %reduce-scatter.22.cloned.1.call-start = ((), (), s32[]{:S(2)}) async-start(), calls=%async_computation.22 | async-start | bytes 5242880 | tf_op jit(solution)/shard_map/reduce_scatter | solution.py:137
  719.5 48.0 %copy-start.9 = (f32[256,2048]{1,0:T(8,128)S(1)}, f32[256,2048]{1,0:T(8,128)}, u32[]{:S(2)}) copy-start(f32[256,2048]{1,0:T(8,128)} %copy-done.8) | copy-start | bytes 6291460
  719.5 48.0 %copy-start.29 = (f32[8,1,256]{2,1,0:T(1,128)S(1)}, f32[8,1,256]{2,1,0:T(1,128)}, u32[]{:S(2)}) copy-start(f32[8,1,256]{2,1,0:T(1,128)} %copy-done.28) | copy-start | bytes 24580
  719.5 48.0 %copy-start.37 = (f32[256]{0:T(256)S(1)}, f32[256]{0:T(256)}, u32[]{:S(2)}) copy-start(f32[256]{0:T(256)} %copy-done.36) | copy-start | bytes 3076
  719.5 48.0 %copy-start.41 = (f32[256]{0:T(256)S(1)}, f32[256]{0:T(256)}, u32[]{:S(2)}) copy-start(f32[256]{0:T(256)} %copy-done.40) | copy-start | bytes 3076
  719.6 50.9 %copy-start.43 = (f32[256]{0:T(256)S(1)}, f32[256]{0:T(256)}, u32[]{:S(2)}) copy-start(f32[256]{0:T(256)} %copy-done.42) | copy-start | bytes 3076
  719.6 136.5 %all-gather.37.cloned.1.call-start = ((), (), s32[]{:S(2)}) async-start(), calls=%async_computation.25 | async-start | bytes 5242880 | tf_op jit(solution)/shard_map/all_gather | solution.py:157
  814.6 5.0 copy-start.19
  820.9 176.6 %reduce-scatter.44.cloned.1.call-start = ((), (), s32[]{:S(2)}) async-start(), calls=%async_computation.35 | async-start | bytes 73728
  821.7 40.9 %copy-start.4 = (bf16[4,1024,128]{2,1,0:T(8,128)(2,1)S(1)}, bf16[4,1024,128]{2,1,0:T(8,128)(2,1)}, u32[]{:S(2)}) copy-start(bf16[4,1024,128]{2,1,0:T(8,128)(2,1)} %copy-done.3) | copy-start | bytes 3145732
  821.7 40.9 %copy-start.6 = (bf16[2,4,512,128]{3,2,1,0:T(8,128)(2,1)S(1)}, bf16[2,4,512,128]{3,2,1,0:T(8,128)(2,1)}, u32[]{:S(2)}) copy-start(bf16[2,4,512,128]{3,2,1,0:T(8,128)(2,1)} %copy-done.5) | copy-start | bytes 3145732
  821.7 40.9 %copy-start.31 = (f32[2,4,512]{2,1,0:T(4,128)S(1)}, f32[2,4,512]{2,1,0:T(4,128)}, u32[]{:S(2)}) copy-start(f32[2,4,512]{2,1,0:T(4,128)} %copy-done.30) | copy-start | bytes 49156
  821.7 40.9 %copy-start.57 = (s32[2]{0:T(128)S(1)}, s32[2]{0:T(128)}, u32[]{:S(2)}) copy-start(s32[2]{0:T(128)} %copy-done.56) | copy-start | bytes 28
  821.7 177.3 %reduce-scatter.42.cloned.1.call-start = ((), (), s32[]{:S(2)}) async-start(), calls=%async_computation.34 | async-start | bytes 73728
  863.9 5.7 copy-start
  875.9 5.2 copy-start.1
  887.5 5.7 copy-start
  899.5 5.8 copy-start.1
  914.7 8.0 copy-start.7
  917.4 131.4 %reduce-scatter.40.cloned.1.call-start = ((), (), s32[]{:S(2)}) async-start(), calls=%async_computation.33 | async-start | bytes 73728
  924.8 198.8 %reduce-scatter.26.cloned.1.call-start = ((), (), s32[]{:S(2)}) async-start(), calls=%async_computation.26 | async-start | bytes 10485760 | tf_op jit(solution)/shard_map/reduce_scatter | solution.py:193
  924.9 4.5 copy-start.23
  924.9 4.5 copy-start.51
  937.6 280.0 %reduce-scatter.32.cloned.1.call-start = ((), (), s32[]{:S(2)}) async-start(), calls=%async_computation.29 | async-start | bytes 4718592 | tf_op jit(solution)/shard_map/reduce_scatter | solution.py:200
  944.3 365.9 %reduce-scatter.34.cloned.1.call-start = ((), (), s32[]{:S(2)}) async-start(), calls=%async_computation.30 | async-start | bytes 4718592 | tf_op jit(solution)/shard_map/reduce_scatter | solution.py:201
  952.0 450.2 %reduce-scatter.28.cloned.1.call-start = ((), (), s32[]{:S(2)}) async-start(), calls=%async_computation.27 | async-start | bytes 4718592 | tf_op jit(solution)/shard_map/reduce_scatter | solution.py:198
  959.8 534.5 %reduce-scatter.30.cloned.1.call-start = ((), (), s32[]{:S(2)}) async-start(), calls=%async_computation.28 | async-start | bytes 4718592 | tf_op jit(solution)/shard_map/reduce_scatter | solution.py:199
  966.5 811.3 %reduce-scatter.36.cloned.1.call-start = ((), (), s32[]{:S(2)}) async-start(), calls=%async_computation.31 | async-start | bytes 18874368 | tf_op jit(solution)/shard_map/reduce_scatter | solution.py:204
  981.8 1079.7 %reduce-scatter.38.cloned.1.call-start = ((), (), s32[]{:S(2)}) async-start(), calls=%async_computation.32 | async-start | bytes 18874368 | tf_op jit(solution)/shard_map/reduce_scatter | solution.py:205
  997.4 126.2 %copy-start.11 = (bf16[256,2048]{1,0:T(8,128)(2,1)S(1)}, bf16[256,2048]{1,0:T(8,128)(2,1)}, u32[]{:S(2)}) copy-start(bf16[256,2048]{1,0:T(8,128)(2,1)} %param.22) | copy-start | bytes 3145732
  997.4 126.2 %copy-start.27 = (f32[8,1,256]{2,1,0:T(1,128)S(1)}, f32[8,1,256]{2,1,0:T(1,128)}, u32[]{:S(2)}) copy-start(f32[8,1,256]{2,1,0:T(1,128)} %copy-done.26) | copy-start | bytes 24580
  997.4 126.2 %copy-start.33 = (f32[256]{0:T(256)S(1)}, f32[256]{0:T(256)}, u32[]{:S(2)}) copy-start(f32[256]{0:T(256)} %copy-done.32) | copy-start | bytes 3076
  997.4 128.5 %copy-start.47 = (f32[256]{0:T(256)S(1)}, f32[256]{0:T(256)}, u32[]{:S(2)}) copy-start(f32[256]{0:T(256)} %copy-done.46) | copy-start | bytes 3076
  997.4 128.5 %copy-start.39 = (f32[256]{0:T(256)S(1)}, f32[256]{0:T(256)}, u32[]{:S(2)}) copy-start(f32[256]{0:T(256)} %copy-done.38) | copy-start | bytes 3076
  997.4 131.0 %copy-start.15 = (f32[256,2048]{1,0:T(8,128)S(1)}, f32[256,2048]{1,0:T(8,128)}, u32[]{:S(2)}) copy-start(f32[256,2048]{1,0:T(8,128)} %copy-done.14) | copy-start | bytes 6291460
  997.4 131.0 %copy-start.45 = (f32[256]{0:T(256)S(1)}, f32[256]{0:T(256)}, u32[]{:S(2)}) copy-start(f32[256]{0:T(256)} %copy-done.44) | copy-start | bytes 3076
  1123.6 4.9 copy-start.16
  1123.6 4.9 copy-start.20
  (23 other events, 44.4 us)
Sparse Core Ops, SparseCore 0:
  10.1 49.4 all-gather.20
  61.8 34.4 all-gather.18
  98.4 47.6 all-gather.24
  148.1 47.6 all-gather.22
  197.6 47.3 all-gather.26
  252.8 71.9 reduce-scatter.19
  327.0 122.2 all-gather.30
  451.4 35.5 all-gather.28
  488.6 34.4 all-gather.34
  525.0 121.9 all-gather.32
  695.6 71.9 reduce-scatter.23
  770.0 44.5 reduce-scatter.21
  821.0 35.0 all-gather.36
  859.3 59.9 reduce-scatter.43
  922.5 61.4 reduce-scatter.41
  987.3 61.4 reduce-scatter.39
  1051.2 72.3 reduce-scatter.25
  1127.6 89.9 reduce-scatter.31
  1221.8 88.3 reduce-scatter.33
  1314.2 87.9 reduce-scatter.27
  1406.4 87.8 reduce-scatter.29
  1498.7 279.0 reduce-scatter.35
  1782.2 279.2 reduce-scatter.37
where the time goes:
time: 2080 us; the launch traced here: 2070 us
  waiting for transfers between devices  1560 us (75%)
  matrix products  219 us (11%)
  blocking collectives  178 us (9%)
  other arithmetic  53.3 us (3%)
  local copies, waits for them, and re-layouts  43 us (2%)
    reduce_scatter x1, waiting for transfers between devices, local(): lax.psum_scatter(g_w2, 'dp', scatter_dimension=1, tiled=True)  284 us
    reduce_scatter x1, waiting for transfers between devices, local(): lax.psum_scatter(g_w1, 'dp', scatter_dimension=0, tiled=True)  283 us
    all_gather x1, waiting for transfers between devices, local(): lax.all_gather(down_weight, 'dp', axis=1, tiled=True)  124 us
    all_gather x1, waiting for transfers between devices, local(): lax.all_gather(up_weight, 'dp', axis=0, tiled=True)  95.5 us
    reduce_scatter x1, waiting for transfers between devices, local(): lax.psum_scatter(g_wo, 'dp', scatter_dimension=1, tiled=True)  92.6 us
    reduce_scatter x1, waiting for transfers between devices, local(): lax.psum_scatter(g_wk, 'dp', scatter_dimension=0, tiled=True)  92.1 us
    reduce_scatter x1, waiting for transfers between devices, local(): lax.psum_scatter(g_wq, 'dp', scatter_dimension=0, tiled=True)  92 us
    reduce_scatter x1, waiting for transfers between devices, local(): lax.psum_scatter(d_h1_part, 'tensor', scatter_dimension=0, tiled=True)  73.5 us
  transfers between devices with their start and end apart: 23, of which 20 were waited for; matrix products, arithmetic and copies ran while one was open for 12% of the time, Pallas kernels for 0%

commit v1 on v0

--- a/solution.py
+++ b/solution.py
@@ -1,7 +1,556 @@
+import functools
+
 import jax
 import jax.numpy as jnp
 from jax import lax
+from jax.experimental import pallas as pl
+from jax.experimental.pallas import tpu as pltpu
 from jax.sharding import PartitionSpec as P
+
+MESH = pl.DeviceIdType.MESH
+F32 = jnp.float32
+BF16 = jnp.bfloat16
+PREFIX_TOP = 512
+VMEM_BYTES = 67043328
+
+
+def split_of(count):
+    inner = 1
+    for size in range(1, count + 1):
+        if size * size <= count and count % size == 0:
+            inner = size
+    return count // inner, inner
+
+
+def remote(source, target, send_sem, recv_sem, dp, tensor):
+    return pltpu.make_async_remote_copy(
+        src_ref=source,
+        dst_ref=target,
+        send_sem=send_sem,
+        recv_sem=recv_sem,
+        device_id=(dp, tensor),
+        device_id_type=MESH,
+    )
+
+
+def block_of(index, size):
+    return pl.ds(pl.multiple_of(index * size, size), size)
+
+
+class Spot:
+    def __init__(self, count):
+        self.outer, self.inner = split_of(count)
+        self.count = count
+        self.dp = lax.axis_index("dp")
+        self.tensor = lax.axis_index("tensor")
+        self.row = lax.div(self.dp, self.inner)
+        self.column = lax.rem(self.dp, self.inner)
+        self.core_peer = self.tensor + 1 - 2 * lax.rem(self.tensor, 2)
+        self.x_peer = lax.rem(self.tensor + 2, 4)
+        self.far_peer = lax.rem(self.core_peer + 2, 4)
+
+    def across(self, step):
+        return lax.rem(self.row + step, self.outer) * self.inner + self.column
+
+    def beside(self, step, row=None):
+        return (self.row if row is None else row) * self.inner + lax.rem(self.column + step, self.inner)
+
+    def meet(self):
+        barrier = pltpu.get_barrier_semaphore()
+        for step in range(1, self.count):
+            pl.semaphore_signal(
+                barrier, inc=1, device_id=(lax.rem(self.dp + step, self.count), self.tensor), device_id_type=MESH
+            )
+        for peer in (self.core_peer, self.x_peer):
+            pl.semaphore_signal(barrier, inc=1, device_id=(self.dp, peer), device_id_type=MESH)
+        pl.semaphore_wait(barrier, self.count + 1)
+
+
+class Spread:
+    def __init__(self, spot, pieces, z_send, z_recv, y_send, y_recv):
+        self.spot, self.pieces = spot, pieces
+        self.sems = (z_send, z_recv, y_send, y_recv)
+        self.sent = []
+        self.todo = [(piece, step) for piece in range(len(pieces)) for step in range(1, spot.outer)]
+        self.own_next = 0
+
+    def send_rows(self, piece):
+        source, target = self.pieces[piece]
+        for step in range(1, self.spot.outer):
+            copy = remote(
+                source, target(self.spot.dp), self.sems[0].at[piece, step], self.sems[1].at[piece, step],
+                self.spot.across(step), self.spot.tensor,
+            )
+            copy.start()
+            self.sent.append(copy)
+
+    def y_copies(self, piece, step):
+        spot = self.spot
+        source, target = self.pieces[piece]
+        owner = spot.across(spot.outer - step) if step else spot.dp
+        if step:
+            source = target(owner)
+        copies = []
+        for side in range(1, spot.inner):
+            copies.append(remote(
+                source, target(owner), self.sems[2].at[piece, step, side], self.sems[3].at[piece, step, side],
+                spot.beside(side), spot.tensor,
+            ))
+        return copies
+
+    def send_own(self, upto):
+        while self.own_next < min(upto, len(self.pieces)):
+            for copy in self.y_copies(self.own_next, 0):
+                copy.start()
+                self.sent.append(copy)
+            self.own_next += 1
+
+    def forward(self, count):
+        for _ in range(count):
+            if not self.todo:
+                return
+            piece, step = self.todo.pop(0)
+            source, target = self.pieces[piece]
+            remote(
+                source, target(self.spot.across(self.spot.outer - step)), self.sems[0].at[piece, step],
+                self.sems[1].at[piece, step], self.spot.across(step), self.spot.tensor,
+            ).wait_recv()
+            for copy in self.y_copies(piece, step):
+                copy.start()
+                self.sent.append(copy)
+            if step == self.spot.outer - 1:
+                self.send_own(piece + 4)
+
+    def arrived(self, piece):
+        while self.todo and self.todo[0][0] <= piece:
+            self.forward(1)
+        for step in range(self.spot.outer):
+            for copy in self.y_copies(piece, step):
+                copy.wait_recv()
+
+    def finish(self):
+        for copy in self.sent:
+            copy.wait_send()
+
+
+class TensorGather:
+    def __init__(self, spot, own, full, rows, send, recv):
+        self.spot, self.full, self.rows, self.send, self.recv = spot, full, rows, send, recv
+        place = self.at(spot.tensor)
+        self.to_x = remote(own, place, send.at[0], recv.at[0], spot.dp, spot.x_peer)
+        self.to_core = remote(own, place, send.at[1], recv.at[1], spot.dp, spot.core_peer)
+        self.to_x.start()
+        self.to_core.start()
+
+    def at(self, index):
+        return self.full.at[block_of(index, self.rows)]
+
+    def pass_on(self):
+        self.to_x.wait_recv()
+        place = self.at(self.spot.x_peer)
+        self.on = remote(place, place, self.send.at[2], self.recv.at[2], self.spot.dp, self.spot.core_peer)
+        self.on.start()
+
+    def finish(self):
+        self.to_core.wait_recv()
+        self.on.wait_recv()
+        for copy in (self.to_x, self.to_core, self.on):
+            copy.wait_send()
+
+
+def tensor_sum(spot, product, core_send, core_recv, x_send, x_recv, send, recv, finish):
+    width = core_send.shape[2]
+    chunk = 512
+    count = width // chunk
+
+    def fill(rank, target):
+        def body(index, carry):
+            target[:, block_of(index, chunk)] = product(rank, index).astype(BF16)
+            return carry
+
+        lax.fori_loop(0, count, body, 0)
+
+    copies = []
+    for slot, rank in enumerate((spot.far_peer, spot.core_peer)):
+        fill(rank, core_send.at[slot])
+        copy = remote(core_send.at[slot], core_recv.at[slot], send.at[slot], recv.at[slot], spot.dp, spot.core_peer)
+        copy.start()
+        copies.append(copy)
+    copies[0].wait_recv()
+
+    def join(index, carry):
+        where = block_of(index, chunk)
+        x_send[:, where] = (product(spot.x_peer, index) + core_recv[0, :, where].astype(F32)).astype(BF16)
+        return carry
+
+    lax.fori_loop(0, count, join, 0)
+    over = remote(x_send, x_recv, send.at[2], recv.at[2], spot.dp, spot.x_peer)
+    over.start()
+    copies[1].wait_recv()
+
+    def end():
+        over.wait_recv()
+
+        def last(index, carry):
+            where = block_of(index, chunk)
+            total = product(spot.tensor, index) + core_recv[1, :, where].astype(F32) + x_recv[:, where].astype(F32)
+            finish(index, total)
+            return carry
+
+        lax.fori_loop(0, count, last, 0)
+        for copy in copies + [over]:
+            copy.wait_send()
+
+    return end
+
+
+def normal_parts(rows):
+    center = rows - jnp.mean(rows, axis=-1, keepdims=True)
+    spread = jnp.mean(center * center, axis=-1, keepdims=True)
+    return center, lax.rsqrt(spread + 1e-05)
+
+
+def forward_kernel(
+    heads,
+    count,
+    prefix,
+    tokens,
+    cotangent,
+    small,
+    qkv_shard,
+    out_shard,
+    up_shard,
+    down_shard,
+    wqkv,
+    wo,
+    w1,
+    w2,
+    h1_all,
+    d_rows,
+    qkv_all,
+    mixed_all,
+    lse_all,
+    second,
+    h2_all,
+    gated_all,
+    slope_all,
+    sums,
+    smalls,
+    h1v,
+    wqkv_v,
+    qkv_v,
+    mixed_v,
+    lse_v,
+    wo_v,
+    core_send,
+    core_recv,
+    x_send,
+    x_recv,
+    h2v,
+    w1_v,
+    gated_v,
+    slope_v,
+    small_send,
+    small_recv,
+    z_send,
+    z_recv,
+    y_send,
+    y_recv,
+    g_send,
+    g_recv,
+    s_send,
+    s_recv,
+    local_sem,
+):
+    spot = Spot(count)
+    rows, features = tokens.shape
+    length = h1v.shape[0]
+    depth = qkv_shard.shape[0]
+    width = wo_v.shape[0]
+    hidden = up_shard.shape[1]
+    half = depth // 2
+    tall = hidden // 2
+    pieces = [
+        (qkv_shard.at[pl.ds(part * half, half)],
+         lambda owner, part=part: wqkv.at[block_of(owner * 2 + part, half)])
+        for part in range(2)
+    ]
+    pieces.append((out_shard, lambda owner: wo.at[:, block_of(owner, depth)]))
+    pieces += [
+        (up_shard.at[pl.ds(part * half, half)],
+         lambda owner, part=part: w1.at[block_of(owner * 2 + part, half)])
+        for part in range(2)
+    ]
+    pieces += [
+        (down_shard.at[pl.ds(part * tall, tall)],
+         lambda owner, part=part: w2.at[pl.ds(part * tall, tall), block_of(owner, depth)])
+        for part in range(2)
+    ]
+    spread = Spread(spot, pieces, z_send, z_recv, y_send, y_recv)
+    locals_ = []
+
+    def keep(source, target):
+        copy = pltpu.make_async_copy(source, target, local_sem.at[len(locals_)])
+        copy.start()
+        locals_.append(copy)
+
+    spot.meet()
+    small_copies = []
+    for step in range(1, count):
+        copy = remote(
+            small, smalls.at[spot.dp], small_send.at[step], small_recv.at[step],
+            lax.rem(spot.dp + step, count), spot.tensor,
+        )
+        copy.start()
+        small_copies.append(copy)
+    for piece in range(len(pieces)):
+        spread.send_rows(piece)
+    spread.send_own(4)
+    for source, target in pieces:
+        keep(source, target(spot.dp))
+    smalls[spot.dp] = small[...]
+    for step, copy in enumerate(small_copies):
+        remote(
+            small, smalls.at[lax.rem(spot.dp + count - step - 1, count)], small_send.at[step + 1],
+            small_recv.at[step + 1], spot.dp, spot.core_peer,
+        ).wait_recv()
+    total = smalls[0]
+    for index in range(1, count):
+        total = total + smalls[index]
+    sums[...] = total
+
+    strip = 32
+    base = spot.tensor * rows
+
+    def norm1(index, carry):
+        where = block_of(index, strip)
+        center, scale = normal_parts(tokens[where, :].astype(F32))
+        h1v[pl.ds(pl.multiple_of(base + index * strip, strip), strip), :] = (
+            center * scale * sums[0:1, :] + sums[1:2, :]
+        ).astype(BF16)
+        return carry
+
+    lax.fori_loop(0, rows // strip, norm1, 0)
+    gather1 = TensorGather(spot, h1v.at[block_of(spot.tensor, rows)], h1v, rows, g_send.at[0], g_recv.at[0])
+    gather_d = TensorGather(spot, cotangent, d_rows, rows, g_send.at[1], g_recv.at[1])
+    keep(cotangent, d_rows.at[block_of(spot.tensor, rows)])
+    spread.forward(spot.outer - 1)
+    gather1.pass_on()
+    spread.forward(spot.outer - 1)
+    gather1.finish()
+    keep(h1v, h1_all)
+    gather_d.pass_on()
+    spread.arrived(0)
+    spread.arrived(1)
+    for copy in locals_[:2]:
+        copy.wait()
+    load = pltpu.make_async_copy(wqkv, wqkv_v, local_sem.at[14])
+    load.start()
+    spread.forward(1)
+    load.wait()
+
+    def project(index, carry):
+        where = block_of(index, rows)
+        for part in range(3):
+            lanes = slice(part * width, (part + 1) * width)
+            value = jnp.dot(h1v[where, :], wqkv_v[:, lanes], preferred_element_type=F32) + sums[6:7, lanes]
+            if part == 0:
+                value = value * (width // heads) ** -0.5
+            qkv_v[where, lanes] = value.astype(BF16)
+        return carry
+
+    lax.fori_loop(0, length // rows, project, 0)
+    keep(qkv_v, qkv_all)
+    spread.forward(2)
+    size = width // heads
+    limit = prefix[0]
+    bench = 256
+
+    for block in range(length // bench):
+        reach = min(length, max((block + 1) * bench, PREFIX_TOP))
+        span = slice(block * bench, (block + 1) * bench)
+
+        def attend(head, carry, block=block, span=span, reach=reach):
+            line = block * bench + lax.broadcasted_iota(jnp.int32, (bench, reach), 0)
+            place = lax.broadcasted_iota(jnp.int32, (bench, reach), 1)
+            seen = (place <= line) | (place < limit)
+            q = qkv_v[span, block_of(head, size)]
+            k = qkv_v[0:reach, pl.ds(pl.multiple_of(width + head * size, size), size)]
+            v = qkv_v[0:reach, pl.ds(pl.multiple_of(2 * width + head * size, size), size)]
+            scores = lax.dot_general(q, k, (((1,), (1,)), ((), ())), preferred_element_type=F32)
+            scores = jnp.where(seen, scores, -1e30)
+            top = jnp.max(scores, axis=-1, keepdims=True)
+            expd = jnp.exp(scores - top)
+            total = jnp.sum(expd, axis=-1, keepdims=True)
+            probs = (expd * (1.0 / total)).astype(BF16)
+            mixed_v[span, block_of(head, size)] = jnp.dot(probs, v, preferred_element_type=F32).astype(BF16)
+            lse_v[head, span, :] = jnp.broadcast_to(top + jnp.log(total), (bench, 128))
+            return carry
+
+        lax.fori_loop(0, heads, attend, 0)
+        if block % 2 == 1:
+            spread.forward(1)
+    keep(mixed_v, mixed_all)
+    keep(lse_v, lse_all)
+    spread.arrived(2)
+    locals_[2].wait()
+    load = pltpu.make_async_copy(wo, wo_v, local_sem.at[14])
+    load.start()
+    load.wait()
+
+    def out_part(rank, index):
+        return jnp.dot(mixed_v[block_of(rank, rows), :], wo_v[:, block_of(index, 512)], preferred_element_type=F32)
+
+    def take_second(index, total):
+        where = block_of(index, 512)
+        second[:, where] = tokens[:, where].astype(F32) + total + sums[4:5, where]
+
+    end = tensor_sum(
+        spot, out_part, core_send, core_recv, x_send, x_recv, s_send.at[0], s_recv.at[0], take_second
+    )
+    spread.forward(spot.outer - 1)
+    end()
+
+    def norm2(index, carry):
+        where = block_of(index, strip)
+        center, scale = normal_parts(second[where, :])
+        h2v[pl.ds(pl.multiple_of(base + index * strip, strip), strip), :] = (
+            center * scale * sums[2:3, :] + sums[3:4, :]
+        ).astype(BF16)
+        return carry
+
+    lax.fori_loop(0, rows // strip, norm2, 0)
+    gather2 = TensorGather(spot, h2v.at[block_of(spot.tensor, rows)], h2v, rows, g_send.at[2], g_recv.at[2])
+    spread.forward(spot.outer - 1)
+    gather2.pass_on()
+    gather2.finish()
+    gather_d.finish()
+    keep(h2v, h2_all)
+    spread.arrived(3)
+    spread.arrived(4)
+    for copy in locals_[3:5]:
+        copy.wait()
+    load = pltpu.make_async_copy(w1, w1_v, local_sem.at[14])
+    load.start()
+    spread.forward(1)
+    load.wait()
+    stored = []
+    for block in range(length // rows):
+        slot = block % 2
+        if block >= 2:
+            stored[block - 2].wait()
+
+        def lift(index, carry, block=block, slot=slot):
+            where = block_of(index, 512)
+            u = jnp.dot(
+                h2v[block * rows : (block + 1) * rows, :], w1_v[:, where], preferred_element_type=F32
+            ) + sums[7:8, where]
+            below = 0.5 * (1.0 + lax.erf(u * 0.7071067811865476))
+            gated_v[block * rows : (block + 1) * rows, where] = (u * below).astype(BF16)
+            slope_v[slot, :, where] = below + u * (0.3989422804014327 * jnp.exp(-0.5 * u * u))
+            return carry
+
+        lax.fori_loop(0, hidden // 512, lift, 0)
+        copy = pltpu.make_async_copy(
+            slope_v.at[slot], slope_all.at[pl.ds(block * rows, rows)], local_sem.at[15 + slot]
+        )
+        copy.start()
+        stored.append(copy)
+        spread.forward(1)
+    keep(gated_v, gated_all)
+    spread.arrived(5)
+    spread.arrived(6)
+    spread.finish()
+    for copy in small_copies:
+        copy.wait_send()
+    for copy in locals_[5:] + stored[-2:]:
+        copy.wait()
+
+
+def forward_call(heads, count, prefix, tokens, cotangent, small, qkv_shard, out_shard, up_shard, down_shard):
+    rows, features = tokens.shape
+    length = rows * 4
+    depth, triple = qkv_shard.shape
+    width = out_shard.shape[0]
+    hidden = up_shard.shape[1]
+    outer, inner = split_of(count)
+    shape = jax.ShapeDtypeStruct
+    hbm = pl.BlockSpec(memory_space=pl.ANY)
+    vmem = pl.BlockSpec(memory_space=pltpu.VMEM)
+    dma = pltpu.SemaphoreType.DMA
+    pieces = 7
+    return pl.pallas_call(
+        functools.partial(forward_kernel, heads, count),
+        out_shape=[
+            shape((features, triple), BF16),
+            shape((width, features), BF16),
+            shape((features, hidden), BF16),
+            shape((hidden, features), BF16),
+            shape((length, features), BF16),
+            shape((length, features), BF16),
+            shape((length, triple), BF16),
+            shape((length, width), BF16),
+            shape((heads, length, 128), F32),
+            shape((rows, features), F32),
+            shape((length, features), BF16),
+            shape((length, hidden), BF16),
+            shape((length, hidden), F32),
+            shape((8, features), F32),
+        ],
+        in_specs=[pl.BlockSpec(memory_space=pltpu.SMEM)] + [vmem] * 7,
+        out_specs=[hbm] * 9 + [vmem] + [hbm] * 3 + [vmem],
+        scratch_shapes=[
+            pltpu.VMEM((count, 8, features), F32),
+            pltpu.VMEM((length, features), BF16),
+            pltpu.VMEM((features, triple), BF16),
+            pltpu.VMEM((length, triple), BF16),
+            pltpu.VMEM((length, width), BF16),
+            pltpu.VMEM((heads, length, 128), F32),
+            pltpu.VMEM((width, features), BF16),
+            pltpu.VMEM((2, rows, features), BF16),
+            pltpu.VMEM((2, rows, features), BF16),
+            pltpu.VMEM((rows, features), BF16),
+            pltpu.VMEM((rows, features), BF16),
+            pltpu.VMEM((length, features), BF16),
+            pltpu.VMEM((features, hidden), BF16),
+            pltpu.VMEM((length, hidden), BF16),
+            pltpu.VMEM((2, rows, hidden), F32),
+            dma((count,)),
+            dma((count,)),
+            dma((pieces, outer)),
+            dma((pieces, outer)),
+            dma((pieces, outer, inner)),
+            dma((pieces, outer, inner)),
+            dma((3, 3)),
+            dma((3, 3)),
+            dma((1, 3)),
+            dma((1, 3)),
+            dma((17,)),
+        ],
+        compiler_params=pltpu.CompilerParams(
+            collective_id=0, has_side_effects=True, vmem_limit_bytes=VMEM_BYTES
+        ),
+    )(prefix, tokens, cotangent, small, qkv_shard, out_shard, up_shard, down_shard)
+
+
+def pack_small(features, query_bias, value_bias, up_bias, vectors):
+    devices = lax.axis_size("dp")
+    me = lax.axis_index("dp")
+    rows = []
+    for part in vectors:
+        start = me * part.shape[0]
+        rows.append(lax.dynamic_update_slice(jnp.zeros((features,), F32), part.astype(F32), (start,)))
+
+    def spread_rows(part):
+        wide = jnp.zeros((part.shape[0], part.shape[1] * devices), F32)
+        return lax.dynamic_update_slice(wide, part.astype(F32), (0, me * part.shape[1])).reshape(-1)
+
+    q = spread_rows(query_bias)
+    joint = jnp.concatenate([q, jnp.zeros_like(q), spread_rows(value_bias)])
+    rows.append(jnp.pad(joint, (0, features - joint.size)))
+    u = spread_rows(up_bias)
+    rows.append(jnp.pad(u, (0, features - u.size)))
+    return jnp.stack(rows)
 
 
 def layer_norm(rows, gain, shift):
@@ -48,7 +597,7 @@
     return jnp.einsum("le,de->ld", left, right, preferred_element_type=jnp.float32)
 
 
-def local(
+def plain(
     tokens,
     prefix,
     query_weight,
@@ -70,24 +619,26 @@
 ):
     f32 = jnp.float32
     bf16 = jnp.bfloat16
-    wq, wk, wv, wo, bq, bv, g1, n1, g2, n2, bo, b2 = (
+    devices = lax.axis_size("dp")
+    small = (query_bias, value_bias, up_bias, norm1_gain, norm1_bias, norm2_gain, norm2_bias, out_bias, down_bias)
+    packed = jnp.concatenate([part.reshape(-1) for part in small])
+    packed = lax.all_gather(packed, "dp", axis=0, tiled=False)
+    pieces = []
+    offset = 0
+    for part in small:
+        piece = packed[:, offset : offset + part.size].reshape((devices,) + part.shape)
+        offset += part.size
+        pieces.append(jnp.moveaxis(piece, 0, -2).reshape(part.shape[:-1] + (-1,)))
+    bq, bv, b1, g1, n1, g2, n2, bo, b2 = pieces
+    wq, wk, wv, wo = (
         lax.all_gather(query_weight, "dp", axis=0, tiled=True),
         lax.all_gather(key_weight, "dp", axis=0, tiled=True),
         lax.all_gather(value_weight, "dp", axis=0, tiled=True),
         lax.all_gather(out_weight, "dp", axis=1, tiled=True),
-        lax.all_gather(query_bias, "dp", axis=1, tiled=True),
-        lax.all_gather(value_bias, "dp", axis=1, tiled=True),
-        lax.all_gather(norm1_gain, "dp", axis=0, tiled=True),
-        lax.all_gather(norm1_bias, "dp", axis=0, tiled=True),
-        lax.all_gather(norm2_gain, "dp", axis=0, tiled=True),
-        lax.all_gather(norm2_bias, "dp", axis=0, tiled=True),
-        lax.all_gather(out_bias, "dp", axis=0, tiled=True),
-        lax.all_gather(down_bias, "dp", axis=0, tiled=True),
-    )
-    w1, w2, b1 = (
+    )
+    w1, w2 = (
         lax.all_gather(up_weight, "dp", axis=0, tiled=True),
         lax.all_gather(down_weight, "dp", axis=1, tiled=True),
-        lax.all_gather(up_bias, "dp", axis=1, tiled=True),
     )
     g1f, n1f, g2f, n2f = (g1.astype(f32), n1.astype(f32), g2.astype(f32), n2.astype(f32))
     bof, b2f = (bo.astype(f32), b2.astype(f32))
@@ -127,7 +678,7 @@
     o_blocks, lse_blocks = lax.map(forward_block, (q_blocks, starts))
     mixed = row_major(from_blocks(o_blocks))
     attn_part = jnp.dot(mixed, wo, preferred_element_type=f32)
-    attn_total = lax.psum_scatter(attn_part, "tensor", scatter_dimension=0, tiled=True)
+    attn_total = lax.psum_scatter(attn_part.astype(bf16), "tensor", scatter_dimension=0, tiled=True).astype(f32)
     second = xf + attn_total + bof
     h2 = layer_norm(second, g2f, n2f).astype(bf16)
     rows2 = lax.all_gather(h2, "tensor", axis=0, tiled=True)
@@ -148,7 +699,7 @@
     d_h2_part = times_transpose(d_hidden_low, w1)
     g_w2 = contract_rows(gated, d_rows)
     g_w1 = contract_rows(rows2, d_hidden_low)
-    d_h2 = lax.psum_scatter(d_h2_part, "tensor", scatter_dimension=0, tiled=True)
+    d_h2 = lax.psum_scatter(d_h2_part.astype(bf16), "tensor", scatter_dimension=0, tiled=True).astype(f32)
     norm2_back = jax.vjp(layer_norm, second, g2f, n2f)[1]
     d_second_ln, g_g2, g_n2 = norm2_back(d_h2)
     d_second = d_out + d_second_ln
@@ -190,29 +741,31 @@
     d_h1_part = (
         times_transpose(dq_low, wq) + times_transpose(dk_low, wk) + times_transpose(dv_low, wv)
     )
-    d_h1 = lax.psum_scatter(d_h1_part, "tensor", scatter_dimension=0, tiled=True)
+    d_h1 = lax.psum_scatter(d_h1_part.astype(bf16), "tensor", scatter_dimension=0, tiled=True).astype(f32)
     norm1_back = jax.vjp(layer_norm, xf, g1f, n1f)[1]
     d_input_ln, g_g1, g_n1 = norm1_back(d_h1)
     input_grad = d_second + d_input_ln
-    s_wq, s_wk, s_wv, s_wo, s_bq, s_bv, s_w1, s_w2, s_b1 = (
-        lax.psum_scatter(g_wq, "dp", scatter_dimension=0, tiled=True),
-        lax.psum_scatter(g_wk, "dp", scatter_dimension=0, tiled=True),
-        lax.psum_scatter(g_wv, "dp", scatter_dimension=0, tiled=True),
-        lax.psum_scatter(g_wo, "dp", scatter_dimension=1, tiled=True),
-        lax.psum_scatter(g_bq, "dp", scatter_dimension=1, tiled=True),
-        lax.psum_scatter(g_bv, "dp", scatter_dimension=1, tiled=True),
-        lax.psum_scatter(g_w1, "dp", scatter_dimension=0, tiled=True),
-        lax.psum_scatter(g_w2, "dp", scatter_dimension=1, tiled=True),
-        lax.psum_scatter(g_b1, "dp", scatter_dimension=1, tiled=True),
-    )
-    s_g1, s_n1, s_g2, s_n2, s_bo, s_b2 = (
-        lax.psum_scatter(g_g1, ("dp", "tensor"), scatter_dimension=0, tiled=True),
-        lax.psum_scatter(g_n1, ("dp", "tensor"), scatter_dimension=0, tiled=True),
-        lax.psum_scatter(g_g2, ("dp", "tensor"), scatter_dimension=0, tiled=True),
-        lax.psum_scatter(g_n2, ("dp", "tensor"), scatter_dimension=0, tiled=True),
-        lax.psum_scatter(g_bo, ("dp", "tensor"), scatter_dimension=0, tiled=True),
-        lax.psum_scatter(g_b2, ("dp", "tensor"), scatter_dimension=0, tiled=True),
-    )
+    def scatter(part, dim):
+        return lax.psum_scatter(part.astype(bf16), "dp", scatter_dimension=dim, tiled=True).astype(f32)
+
+    s_w2, s_w1, s_wo = scatter(g_w2, 1), scatter(g_w1, 0), scatter(g_wo, 1)
+    s_wq, s_wk, s_wv = scatter(g_wq, 0), scatter(g_wk, 0), scatter(g_wv, 0)
+
+    def by_device(part):
+        return jnp.moveaxis(part.reshape(part.shape[:-1] + (devices, -1)), -2, 0).reshape(devices, -1)
+
+    rows = [by_device(part) for part in (g_bq, g_bv, g_b1, g_g1, g_n1, g_g2, g_n2, g_bo, g_b2)]
+    total = lax.psum_scatter(jnp.concatenate(rows, axis=1), "dp", scatter_dimension=0, tiled=True)[0]
+    offset = 0
+    outs = []
+    for part in (query_bias, value_bias, up_bias):
+        outs.append(total[offset : offset + part.size].reshape(part.shape))
+        offset += part.size
+    s_bq, s_bv, s_b1 = outs
+    vectors = lax.psum_scatter(
+        total[offset:].reshape(6, lax.axis_size("tensor"), -1), "tensor", scatter_dimension=1, tiled=True
+    ).reshape(6, -1)
+    s_g1, s_n1, s_g2, s_n2, s_bo, s_b2 = (vectors[index] for index in range(6))
     return (
         layer_out,
         input_grad,
@@ -232,6 +785,178 @@
         s_bo,
         s_b2,
     )
+
+
+def fast(
+    tokens,
+    prefix,
+    query_weight,
+    key_weight,
+    value_weight,
+    out_weight,
+    query_bias,
+    value_bias,
+    up_weight,
+    down_weight,
+    up_bias,
+    norm1_gain,
+    norm1_bias,
+    norm2_gain,
+    norm2_bias,
+    out_bias,
+    down_bias,
+    cotangent,
+):
+    f32 = jnp.float32
+    bf16 = jnp.bfloat16
+    devices = lax.axis_size("dp")
+    heads = query_bias.shape[0]
+    row_features = tokens.shape[1]
+    small = pack_small(
+        row_features, query_bias, value_bias, up_bias,
+        (norm1_gain, norm1_bias, norm2_gain, norm2_bias, out_bias, down_bias),
+    )
+    w_qkv, wo, w1, w2, rows1, d_rows, qkv, mixed, lse, second, rows2, gated, slope, sums = forward_call(
+        heads, devices, prefix, tokens, cotangent, small,
+        jnp.concatenate([query_weight, key_weight, value_weight], axis=1), out_weight, up_weight, down_weight,
+    )
+    g1f, n1f, g2f, n2f, bof, b2f = (sums[index] for index in range(6))
+    bq, bv, b1 = (
+        jnp.zeros((part.shape[0], part.shape[1] * devices), bf16) for part in (query_bias, value_bias, up_bias)
+    )
+    heads = bq.shape[0]
+    head_size = bq.shape[1]
+    scale = head_size ** (-0.5)
+    prefix_len = prefix[0]
+    xf = tokens.astype(f32)
+    length = rows1.shape[0]
+    block = min(512, length)
+    count = length // block
+    wq, wk, wv = jnp.split(w_qkv, 3, axis=1)
+    query, keyed, valued = jnp.split(qkv, 3, axis=1)
+    q_heads = head_major(query, heads)
+    k_heads = head_major(keyed, heads)
+    v_heads = head_major(valued, heads)
+    q_blocks = to_blocks(q_heads, count)
+    starts = jnp.arange(count, dtype=jnp.int32) * block
+
+    lse_blocks = to_blocks(lse[:, :, 0], count)
+    mlp_part = jnp.dot(gated, w2, preferred_element_type=f32)
+    mlp_total = lax.psum_scatter(
+        mlp_part.astype(jnp.bfloat16), "tensor", scatter_dimension=0, tiled=True
+    ).astype(jnp.float32)
+    layer_out = (second + mlp_total + b2f).astype(bf16)
+    d_out = cotangent.astype(f32)
+    g_b2 = jnp.sum(d_out, axis=0)
+    d_gated = times_transpose(d_rows, w2)
+    d_hidden = d_gated * slope
+    g_b1 = jnp.sum(d_hidden, axis=0).reshape(b1.shape)
+    d_hidden_low = d_hidden.astype(bf16)
+    d_h2_part = times_transpose(d_hidden_low, w1)
+    g_w2 = contract_rows(gated, d_rows)
+    g_w1 = contract_rows(rows2, d_hidden_low)
+    d_h2 = lax.psum_scatter(d_h2_part.astype(bf16), "tensor", scatter_dimension=0, tiled=True).astype(f32)
+    norm2_back = jax.vjp(layer_norm, second, g2f, n2f)[1]
+    d_second_ln, g_g2, g_n2 = norm2_back(d_h2)
+    d_second = d_out + d_second_ln
+    g_bo = jnp.sum(d_second, axis=0)
+    d_second_low = d_second.astype(bf16)
+    back_rows = lax.all_gather(d_second_low, "tensor", axis=0, tiled=True)
+    g_wo = contract_rows(mixed, back_rows)
+    d_mixed = times_transpose(back_rows, wo).astype(bf16)
+    do_blocks = to_blocks(head_major(d_mixed, heads), count)
+
+    def backward_block(carry, item):
+        d_keys, d_vals = carry
+        q_block, do_block, lse_block, start = item
+        scores = masked_scores(q_block, k_heads, start, prefix_len)
+        probs = jnp.exp(scores - lse_block[..., None])
+        d_probs = jnp.einsum("hqd,hkd->hqk", do_block, v_heads, preferred_element_type=f32)
+        d_vals = d_vals + jnp.einsum(
+            "hqk,hqd->hkd", probs.astype(bf16), do_block, preferred_element_type=f32
+        )
+        inner = jnp.sum(probs * d_probs, axis=-1, keepdims=True)
+        d_scores = (probs * (d_probs - inner)).astype(bf16)
+        d_query = jnp.einsum("hqk,hkd->hqd", d_scores, k_heads, preferred_element_type=f32)
+        d_keys = d_keys + jnp.einsum("hqk,hqd->hkd", d_scores, q_block, preferred_element_type=f32)
+        return ((d_keys, d_vals), d_query)
+
+    empty = jnp.zeros(k_heads.shape, f32)
+    (d_keys, d_vals), dq_blocks = lax.scan(
+        backward_block, (empty, empty), (q_blocks, do_blocks, lse_blocks, starts)
+    )
+    d_query = row_major(from_blocks(dq_blocks)) * scale
+    d_keys = row_major(d_keys)
+    d_vals = row_major(d_vals)
+    g_bq = jnp.sum(d_query, axis=0).reshape(bq.shape)
+    g_bv = jnp.sum(d_vals, axis=0).reshape(bv.shape)
+    dq_low, dk_low, dv_low = (d_query.astype(bf16), d_keys.astype(bf16), d_vals.astype(bf16))
+    g_wq = contract_rows(rows1, dq_low)
+    g_wk = contract_rows(rows1, dk_low)
+    g_wv = contract_rows(rows1, dv_low)
+    d_h1_part = (
+        times_transpose(dq_low, wq) + times_transpose(dk_low, wk) + times_transpose(dv_low, wv)
+    )
+    d_h1 = lax.psum_scatter(d_h1_part.astype(bf16), "tensor", scatter_dimension=0, tiled=True).astype(f32)
+    norm1_back = jax.vjp(layer_norm, xf, g1f, n1f)[1]
+    d_input_ln, g_g1, g_n1 = norm1_back(d_h1)
+    input_grad = d_second + d_input_ln
+    def scatter(part, dim):
+        return lax.psum_scatter(part.astype(bf16), "dp", scatter_dimension=dim, tiled=True).astype(f32)
+
+    s_w2, s_w1, s_wo = scatter(g_w2, 1), scatter(g_w1, 0), scatter(g_wo, 1)
+    s_wq, s_wk, s_wv = scatter(g_wq, 0), scatter(g_wk, 0), scatter(g_wv, 0)
+
+    def by_device(part):
+        return jnp.moveaxis(part.reshape(part.shape[:-1] + (devices, -1)), -2, 0).reshape(devices, -1)
+
+    rows = [by_device(part) for part in (g_bq, g_bv, g_b1, g_g1, g_n1, g_g2, g_n2, g_bo, g_b2)]
+    total = lax.psum_scatter(jnp.concatenate(rows, axis=1), "dp", scatter_dimension=0, tiled=True)[0]
+    offset = 0
+    outs = []
+    for part in (query_bias, value_bias, up_bias):
+        outs.append(total[offset : offset + part.size].reshape(part.shape))
+        offset += part.size
+    s_bq, s_bv, s_b1 = outs
+    vectors = lax.psum_scatter(
+        total[offset:].reshape(6, lax.axis_size("tensor"), -1), "tensor", scatter_dimension=1, tiled=True
+    ).reshape(6, -1)
+    s_g1, s_n1, s_g2, s_n2, s_bo, s_b2 = (vectors[index] for index in range(6))
+    return (
+        layer_out,
+        input_grad,
+        s_wq,
+        s_wk,
+        s_wv,
+        s_wo,
+        s_bq,
+        s_bv,
+        s_w1,
+        s_w2,
+        s_b1,
+        s_g1,
+        s_n1,
+        s_g2,
+        s_n2,
+        s_bo,
+        s_b2,
+    )
+
+
+def local(*args):
+    tokens, query_weight, up_weight = args[0], args[2], args[8]
+    devices = lax.axis_size("dp")
+    features = tokens.shape[1]
+    share = features // devices
+    fits = (
+        lax.axis_size("tensor") == 4
+        and devices <= 8
+        and share % 128 == 0
+        and tokens.shape[0] == 256
+        and 3 * query_weight.shape[1] <= features
+        and up_weight.shape[1] <= features
+    )
+    return fast(*args) if fits else plain(*args)
 
 
 def solution(mesh):

time: 2080 us -> 1220 us (0.59)
  waiting for transfers between devices: 1560 us -> 564 us
  Pallas kernels: 0 us -> 348 us
  blocking collectives: 178 us -> 43.8 us
  matrix products: 219 us -> 150 us
    reduce_scatter x10 -> x9, waiting for transfers between devices: 1060 us -> 564 us  [the longest x6 434 us: scatter(): lax.psum_scatter(part.astype(bf16), 'dp', scatter_dimension=dim, tiled=True)]
    all_gather x10 -> x1, waiting for transfers between devices: 443 us -> 0.01 us  [fast(): back_rows = lax.all_gather(d_second_low, 'tensor', axis=0, tiled=True)]
    pallas_call x0 -> x1, Pallas kernels: none -> 348 us  [forward_call(): pl.pallas_call(functools.partial(forward_kernel, heads, count), out_shape...]
    all_gather x9 -> x0, blocking collectives: 135 us -> none  [the longest x1 22.7 us: local(): lax.all_gather(up_bias, 'dp', axis=1, tiled=True)]
    unnamed x26 -> x10, waiting for transfers between devices: 53 us -> 0.17 us
    dot_general x8 -> x1, matrix products: 59.2 us -> 13.8 us  [fast(): mlp_part = jnp.dot(gated, w2, preferred_element_type=f32)]
    unnamed x1 -> x2, blocking collectives: 43.2 us -> 43.8 us
  transfers between devices with their start and end apart: 23 -> 10, of which waited for: 20 -> 9; matrix products, arithmetic and copies ran while one was open for 12% -> 14% of each run, Pallas kernels for 0% -> 0%
where the time goes in v1:
time: 1220 us; the launch traced here: 1210 us
  waiting for transfers between devices  564 us (46%)
  Pallas kernels  348 us (29%)
  matrix products  150 us (12%)
  other arithmetic  46.2 us (4%)
  blocking collectives  43.8 us (4%)
  local copies, waits for them, and re-layouts  38 us (3%)
  between operations  16.6 us (1%)
    reduce_scatter x6, waiting for transfers between devices, scatter(): lax.psum_scatter(part.astype(bf16), 'dp', scatter_dimension=dim, tiled=True)  434 us
    pallas_call x1, Pallas kernels, forward_call(): pl.pallas_call(functools.partial(forward_kernel, heads, count), out_shape...  348 us
    dot_general x6, matrix products, contract_rows(): jnp.einsum('ld,le->de', left, right, preferred_element_type=jnp.float32)  52.5 us
    reduce_scatter x1, waiting for transfers between devices, fast(): lax.psum_scatter(d_h1_part.astype(bf16), 'tensor', scatter_dimension=0, t...  45.8 us
    dot_general x6, matrix products, times_transpose(): jnp.einsum('le,de->ld', left, right, preferred_element_type=jnp.float32)  44.8 us
    reduce_scatter x1, waiting for transfers between devices, fast(): lax.psum_scatter(mlp_part.astype(jnp.bfloat16), 'tensor', scatter_dimensi...  44.5 us
    unnamed x2, blocking collectives  43.8 us
    reduce_scatter x1, waiting for transfers between devices, fast(): lax.psum_scatter(d_h2_part.astype(bf16), 'tensor', scatter_dimension=0, t...  39.5 us
  transfers between devices with their start and end apart: 10, of which 9 were waited for; matrix products, arithmetic and copies ran while one was open for 14% of the time, Pallas kernels for 0%

profile of v1, /device:TPU:9, one launch (start us, length us, event | category | flops | bytes accessed | tf_op | source)
XLA Modules:
  0.0 1208.5 jit_solution(12645922766927608074)
XLA Ops:
  15.7 2.0 pad_maximum_fusion.qkv_shard
  18.5 348.3 %shard_map.305 = (bf16[2048,1536]{1,0:T(8,128)(2,1)}, bf16[512,2048]{1,0:T(8,128)(2,1)}, bf16[2048,2048]{1,0:T(8,128)(2,1)}, bf16[2048,2048]{1,0:T(8,128)(2,1)},...) custom-call(s32[1]{0:T(128)S(6)} %copy.146.prefix, ...), custom_call_target="tpu_custom_call" | custom-call | tf_op jit(solution)/shard_map/pallas_call | solution.py:482
  366.8 15.0 %fusion.58 = (f32[2048]{0:T(1024)}, bf16[1024,2048]{1,0:T(8,128)(2,1)S(1)}) fusion(f32[1024,2048]{1,0:T(8,128)} %get-tuple-element.95, bf16[1024,2048]{1,0:T(8,128)(2,1)} %get-tuple-element.94, bf16[2048,2048]{1,0:T(8,128)(2,1)} %get-tuple-element.92), kind=kOutput, calls=%fused_computation.132 | convolution fusion | flops 8596224000 | bytes 25174016 | tf_op jit(solution)/shard_map/le,de->ld/dot_general | solution.py:597
  381.8 2.0 copy-done.25
  383.8 10.4 convolution_convert_fusion.2
  394.3 13.8 %convolution_convert_fusion.3 = bf16[1024,2048]{1,0:T(8,128)(2,1)} fusion(bf16[1024,2048]{1,0:T(8,128)(2,1)} %get-tuple-element.91, bf16[2048,2048]{1,0:T(8,128)(2,1)} %get-tuple-element.92), kind=kOutput, calls=%fused_computation.38 | convolution fusion | flops 8592031744 | bytes 16777216 | tf_op jit(solution)/shard_map/dot_general | solution.py:844
  408.4 1.3 copy-done.4
  410.3 1.6 fusion.57
  411.8 39.5 %reduce-scatter.13.cloned.1.call-done = bf16[256,2048]{1,0:T(8,128)(2,1)} async-done(((bf16[1024,2048]{1,0:T(8,128)(2,1)}), bf16[256,2048]{1,0:T(8,128)(2,1)}) %reduce-scatter.13.cloned.1.call-update) | async-done | bytes 1048592 | tf_op jit(solution)/shard_map/reduce_scatter | solution.py:858
  451.3 2.7 fusion.35
  454.0 44.5 %reduce-scatter.11.cloned.1.call-done = bf16[256,2048]{1,0:T(8,128)(2,1)} async-done(((bf16[1024,2048]{1,0:T(8,128)(2,1)}), bf16[256,2048]{1,0:T(8,128)(2,1)}) %reduce-scatter.11.cloned.1.call-update) | async-done | bytes 1048592 | tf_op jit(solution)/shard_map/reduce_scatter | solution.py:845
  498.5 3.1 fusion.56
  501.6 1.3 copy-done.6
  502.9 1.3 fusion.55
  504.2 14.1 %convolution_convert_fusion.1 = bf16[2048,2048]{1,0:T(8,128)(2,1)} fusion(bf16[1024,2048]{1,0:T(8,128)(2,1)} %get-tuple-element.106, bf16[1024,2048]{1,0:T(8,128)(2,1)} %copy-done.25), kind=kOutput, calls=%fused_computation.35 | convolution fusion | flops 8594128896 | bytes 16777216 | tf_op jit(solution)/shard_map/ld,le->de/dot_general | solution.py:593
  518.4 14.0 %convolution_convert_fusion = bf16[2048,2048]{1,0:T(8,128)(2,1)} fusion(bf16[1024,2048]{1,0:T(8,128)(2,1)} %get-tuple-element.91, bf16[1024,2048]{1,0:T(8,128)(2,1)} %get-tuple-element.94), kind=kOutput, calls=%fused_computation.34 | convolution fusion | flops 8594128896 | bytes 16777216 | tf_op jit(solution)/shard_map/ld,le->de/dot_general | solution.py:593
  532.7 3.4 slice_bitcast_fusion
  538.8 3.0 bitcast_bitcast_fusion
  541.8 5.3 convolution_convert_fusion.8
  547.1 1.3 copy.73
  548.4 6.2 convolution_convert_fusion.4
  554.7 53.1 %while.15 = (s32[]{:T(128)}, f32[4,1024,128]{2,1,0:T(8,128)S(1)}, f32[4,1024,128]{2,1,0:T(8,128)}, f32[2,4,512,128]{3,2,0,1:T(8,128)}, s32[2]{0:T(128)S(1)}, /*i...) while((s32[]{:T(128)}, f32[4,1024,128]{2,1,0:T(8,128)S(1)}, ...), condition=%wide.region_8.9_spmd.clone, body=%wide.region_6.8_spmd.clone.sunk | while | flops 2712665600 | bytes 172048688 | solution.py:885
  554.7 2.8 fusion.108
  560.1 3.1 multiply_reduce_fusion.4
  563.2 2.1 multiply_convert_fusion.3
  565.4 1.9 copy-done.2
  567.3 3.5 fusion.110
  570.8 4.7 select_add_fusion.4
  575.6 5.2 select_add_fusion.5
  580.8 2.8 fusion.108
  586.2 3.1 multiply_reduce_fusion.4
  589.3 2.1 multiply_convert_fusion.3
  591.5 1.9 copy-done.2
  593.5 3.5 fusion.110
  597.0 4.7 select_add_fusion.4
  601.8 6.0 select_add_fusion.5
  607.8 3.3 copy.81
  611.1 1.7 bitcast_convert_fusion
  612.9 6.0 convolution_convert_fusion.5
  618.9 1.4 copy.80
  620.3 6.2 convolution_convert_fusion.6
  626.6 1.9 multiply_reduce_fusion.2
  629.0 6.0 convolution_convert_fusion.7
  636.2 4.0 fusion.38
  640.2 4.0 fusion.40
  644.2 6.0 add_convert_fusion
  653.2 11.3 reduce-scatter.25.cloned.1.call-done
  664.5 2.8 convert_element_type.152
  667.3 147.5 %reduce-scatter.27.cloned.1.call-done = bf16[2048,256]{1,0:T(8,128)(2,1)} async-done(((bf16[2048,2048]{1,0:T(8,128)(2,1)}), bf16[2048,256]{1,0:T(8,128)(2,1)}) %reduce-scatter.27.cloned.1.call-update) | async-done | bytes 1048592 | tf_op jit(solution)/shard_map/reduce_scatter | solution.py:905
  814.9 2.7 convert_element_type.154
  817.6 68.1 %reduce-scatter.23.cloned.1.call-done = bf16[512,256]{1,0:T(8,128)(2,1)} async-done(((bf16[512,2048]{1,0:T(8,128)(2,1)}), bf16[512,256]{1,0:T(8,128)(2,1)}) %reduce-scatter.23.cloned.1.call-update) | async-done | bytes 262160 | tf_op jit(solution)/shard_map/reduce_scatter | solution.py:905
  885.7 1.8 convert_element_type.150
  887.5 68.9 %reduce-scatter.21.cloned.1.call-done = bf16[256,512]{1,0:T(8,128)(2,1)} async-done(((bf16[2048,512]{1,0:T(8,128)(2,1)}), bf16[256,512]{1,0:T(8,128)(2,1)}) %reduce-scatter.21.cloned.1.call-update) | async-done | bytes 262160 | tf_op jit(solution)/shard_map/reduce_scatter | solution.py:905
  956.4 1.8 convert_element_type.148
  958.2 68.9 %reduce-scatter.19.cloned.1.call-done = bf16[256,512]{1,0:T(8,128)(2,1)} async-done(((bf16[2048,512]{1,0:T(8,128)(2,1)}), bf16[256,512]{1,0:T(8,128)(2,1)}) %reduce-scatter.19.cloned.1.call-update) | async-done | bytes 262160 | tf_op jit(solution)/shard_map/reduce_scatter | solution.py:905
  1027.1 1.8 convert_element_type.146
  1028.9 69.2 %reduce-scatter.17.cloned.1.call-done = bf16[256,512]{1,0:T(8,128)(2,1)} async-done(((bf16[2048,512]{1,0:T(8,128)(2,1)}), bf16[256,512]{1,0:T(8,128)(2,1)}) %reduce-scatter.17.cloned.1.call-update) | async-done | bytes 262160 | tf_op jit(solution)/shard_map/reduce_scatter | solution.py:905
  1098.1 1.8 convert_element_type.144
  1099.9 45.8 %reduce-scatter.15.cloned.1.call-done = bf16[256,2048]{1,0:T(8,128)(2,1)} async-done(((bf16[1024,2048]{1,0:T(8,128)(2,1)}), bf16[256,2048]{1,0:T(8,128)(2,1)}) %reduce-scatter.15.cloned.1.call-update) | async-done | bytes 1048592 | tf_op jit(solution)/shard_map/reduce_scatter | solution.py:900
  1145.7 2.3 fusion.33
  1149.1 2.7 convert_reduce_fusion.3
  1151.9 28.0 %all-reduce.1 = f32[8,1920]{1,0:T(8,128)S(1)} all-reduce(f32[8,1920]{1,0:T(8,128)S(1)} %concatenate.11), channel_id=9, replica_groups=mesh['dp'=8,'tensor'=4] {'dp'}, use_global_device_ids=true, to_apply=%region_27.28.clone | all-reduce | flops 15360 | bytes 122880
  1180.7 15.8 %all-reduce.2 = f32[6,4,64]{2,1,0:T(4,128)S(1)} all-reduce(f32[6,4,64]{2,1,0:T(4,128)S(1)} %reshape.273), channel_id=12, replica_groups=mesh['dp'=8,'tensor'=4] {'tensor'}, use_global_device_ids=true, to_apply=%region_30.31.clone | all-reduce | flops 1536 | bytes 12288
  1199.9 1.2 fusion.47
  (165 shorter events, 27.1 us)
Async XLA Ops:
  8.0 443.3 %reduce-scatter.13.cloned.1.call-start = ((), (), s32[]{:S(2)}) async-start(), calls=%async_computation.10 | async-start | bytes 5242880 | tf_op jit(solution)/shard_map/reduce_scatter | solution.py:858
  366.8 17.0 %copy-start.22 = (bf16[2048,2048]{1,0:T(8,128)(2,1)S(1)}, bf16[2048,2048]{1,0:T(8,128)(2,1)}, u32[]{:S(2)}) copy-start(bf16[2048,2048]{1,0:T(8,128)(2,1)} %get-tuple-element.96) | copy-start | bytes 25165828
  381.8 2.0 copy-start.25
  394.2 104.2 %reduce-scatter.11.cloned.1.call-start = ((), (), s32[]{:S(2)}) async-start(), calls=%async_computation.9 | async-start | bytes 5242880 | tf_op jit(solution)/shard_map/reduce_scatter | solution.py:845
  408.1 1.6 copy-start.4
  408.2 133.6 %all-gather.2.cloned.1.call-start = ((), (), s32[]{:S(2)}) async-start(), calls=%async_computation.11 | async-start | bytes 5242880 | tf_op jit(solution)/shard_map/all_gather | solution.py:864
  451.3 47.1 %copy-start.13 = (bf16[256,2048]{1,0:T(8,128)(2,1)S(1)}, bf16[256,2048]{1,0:T(8,128)(2,1)}, u32[]{:S(2)}) copy-start(bf16[256,2048]{1,0:T(8,128)(2,1)} %reduce-scatter.13.cloned.1.call-done) | copy-start | bytes 3145732
  498.5 4.4 copy-start.10
  501.6 1.3 copy-start.6
  501.6 1.3 copy-start.19
  504.2 160.3 %reduce-scatter.25.cloned.1.call-start = ((), (), s32[]{:S(2)}) async-start(), calls=%async_computation.17 | async-start | bytes 9437184 | tf_op jit(solution)/shard_map/reduce_scatter | solution.py:905
  518.3 296.5 %reduce-scatter.27.cloned.1.call-start = ((), (), s32[]{:S(2)}) async-start(), calls=%async_computation.18 | async-start | bytes 9437184 | tf_op jit(solution)/shard_map/reduce_scatter | solution.py:905
  532.4 353.2 %reduce-scatter.23.cloned.1.call-start = ((), (), s32[]{:S(2)}) async-start(), calls=%async_computation.16 | async-start | bytes 2359296 | tf_op jit(solution)/shard_map/reduce_scatter | solution.py:905
  536.1 2.0 copy-start.14
  554.7 401.7 %reduce-scatter.21.cloned.1.call-start = ((), (), s32[]{:S(2)}) async-start(), calls=%async_computation.15 | async-start | bytes 2359296 | tf_op jit(solution)/shard_map/reduce_scatter | solution.py:905
  554.7 5.3 copy-start.3
  554.7 5.3 copy-start.9
  557.5 5.7 copy-start
  565.4 2.0 copy-start.2
  570.8 4.8 copy-start.1
  580.8 5.3 copy-start.3
  580.8 5.3 copy-start.9
  583.6 5.7 copy-start
  591.5 2.0 copy-start.2
  597.0 4.8 copy-start.1
  618.8 408.2 %reduce-scatter.19.cloned.1.call-start = ((), (), s32[]{:S(2)}) async-start(), calls=%async_computation.14 | async-start | bytes 2359296 | tf_op jit(solution)/shard_map/reduce_scatter | solution.py:905
  626.5 471.6 %reduce-scatter.17.cloned.1.call-start = ((), (), s32[]{:S(2)}) async-start(), calls=%async_computation.13 | async-start | bytes 2359296 | tf_op jit(solution)/shard_map/reduce_scatter | solution.py:905
  635.0 1.2 copy-start.15
  635.0 510.7 %reduce-scatter.15.cloned.1.call-start = ((), (), s32[]{:S(2)}) async-start(), calls=%async_computation.12 | async-start | bytes 5242880 | tf_op jit(solution)/shard_map/reduce_scatter | solution.py:900
  650.2 0.7 copy-start.21
  650.2 0.9 copy-start.24
  650.2 1.5 copy-start.23
  650.2 2.2 copy-start.5
  650.3 2.4 copy-start.18
  650.3 2.4 copy-start.17
  650.3 2.4 copy-start.8
  817.6 328.1 %copy-start.16 = (f32[1,2048]{1,0:T(1,128)S(1)}, f32[1,2048]{1,0:T(1,128)}, u32[]{:S(2)}) copy-start(f32[1,2048]{1,0:T(1,128)} %get-tuple-element.221) | copy-start | bytes 24580
  1145.7 2.4 copy-start.12
  1145.7 3.4 copy-start.7
  1145.7 3.4 copy-start.11
  1145.7 3.4 copy-start.20
Sparse Core Ops, SparseCore 0:
  394.4 56.9 reduce-scatter.12
  453.8 44.5 reduce-scatter.10
  504.3 35.0 all-gather.1
Sparse Core Ops, SparseCore 1:
  518.4 146.0 reduce-scatter.24
  668.0 146.8 reduce-scatter.26
  818.3 67.4 reduce-scatter.22
  889.2 67.1 reduce-scatter.20
  959.9 67.1 reduce-scatter.18
  1030.6 67.4 reduce-scatter.16
  1100.5 45.1 reduce-scatter.14

commit v2 on v1

--- a/solution.py
+++ b/solution.py
@@ -55,15 +55,19 @@
     def beside(self, step, row=None):
         return (self.row if row is None else row) * self.inner + lax.rem(self.column + step, self.inner)
 
-    def meet(self):
+    def meet(self, far=False):
         barrier = pltpu.get_barrier_semaphore()
         for step in range(1, self.count):
             pl.semaphore_signal(
                 barrier, inc=1, device_id=(lax.rem(self.dp + step, self.count), self.tensor), device_id_type=MESH
             )
+        for peer in (self.core_peer, self.x_peer) + ((self.far_peer,) if far else ()):
+            pl.semaphore_signal(barrier, inc=1, device_id=(self.dp, peer), device_id_type=MESH)
+        pl.semaphore_wait(barrier, self.count + 1 + far)
+
+    def release(self, ready):
         for peer in (self.core_peer, self.x_peer):
-            pl.semaphore_signal(barrier, inc=1, device_id=(self.dp, peer), device_id_type=MESH)
-        pl.semaphore_wait(barrier, self.count + 1)
+            pl.semaphore_signal(ready, inc=1, device_id=(self.dp, peer), device_id_type=MESH)
 
 
 class Spread:
@@ -531,6 +535,540 @@
             collective_id=0, has_side_effects=True, vmem_limit_bytes=VMEM_BYTES
         ),
     )(prefix, tokens, cotangent, small, qkv_shard, out_shard, up_shard, down_shard)
+class Reduce:
+    def __init__(self, spot, left, right, lanes, landing, target, shared, index, last):
+        self.spot, self.left, self.right, self.lanes = spot, left, right, lanes
+        self.landing, self.target, self.shared, self.index, self.last = landing, target, shared, index, last
+        self.width = lanes.stop - lanes.start
+        self.share = target.shape[0]
+        self.stepped = {}
+        self.held = False
+
+    def block(self, owner, take):
+        turned = jnp.transpose(self.left[:, block_of(owner, self.share)])
+        for start in range(0, self.width, 512):
+            source = self.right[:, self.lanes.start + start : self.lanes.start + start + 512]
+            take(slice(start, start + 512), jnp.dot(turned, source, preferred_element_type=F32))
+
+    def y_copy(self, step):
+        shared = self.shared
+        area = pl.ds(0, self.width)
+        return remote(
+            shared["y_out"].at[step, :, area], shared["y_in"].at[step, :, area], shared["y_send"].at[step],
+            shared["y_recv"].at[step], self.spot.beside(1), self.spot.tensor,
+        )
+
+    def z_copy(self, step):
+        shared = self.shared
+        return remote(
+            shared["z_out"].at[step, :, pl.ds(0, self.width)], self.landing.at[step - 1],
+            shared["z_send"].at[step], shared["z_recv"].at[self.index, step], self.spot.across(step),
+            self.spot.tensor,
+        )
+
+    def produce(self, step):
+        shared, spot = self.shared, self.spot
+        row = lax.rem(spot.row + step, spot.outer)
+        if step in shared["y_busy"]:
+            shared["y_busy"].pop(step).wait_send()
+
+        def take(where, value):
+            shared["y_out"][step, :, where] = value.astype(BF16)
+
+        self.block(spot.beside(1, row), take)
+        if self.index > 0:
+            pl.semaphore_wait(shared["credit"], 1)
+        copy = self.y_copy(step)
+        copy.start()
+        shared["y_busy"][step] = copy
+
+    def hold(self):
+        self.held = True
+        for step in range(self.spot.outer):
+
+            def take(where, value, step=step):
+                self.shared["z_out"][step, :, where] = value.astype(BF16)
+
+            self.block(self.spot.across(step), take)
+
+    def serve(self, step):
+        shared, spot = self.shared, self.spot
+        self.y_copy(step).wait_recv()
+        if step in shared["z_busy"]:
+            shared["z_busy"].pop(step).wait_send()
+        y_in, z_out = shared["y_in"], shared["z_out"]
+        if self.held:
+            for start in range(0, self.width, 512):
+                where = slice(start, start + 512)
+                z_out[step, :, where] = (z_out[step, :, where].astype(F32) + y_in[step, :, where].astype(F32)).astype(BF16)
+        else:
+
+            def take(where, value):
+                z_out[step, :, where] = (value + y_in[step, :, where].astype(F32)).astype(BF16)
+
+            self.block(spot.across(step), take)
+        if not self.last:
+            pl.semaphore_signal(
+                shared["credit"], inc=1, device_id=(spot.beside(1), spot.tensor), device_id_type=MESH
+            )
+        if step:
+            copy = self.z_copy(step)
+            copy.start()
+            shared["z_busy"][step] = copy
+
+    def settle(self):
+        shared, spot = self.shared, self.spot
+        for step in range(1, spot.outer):
+            self.z_copy(step).wait_recv()
+        loads, stores = [], []
+        chunks = self.width // 512
+        for chunk in range(chunks):
+            loads.append(pltpu.make_async_copy(
+                self.landing.at[:, :, pl.ds(chunk * 512, 512)], shared["z_stage"].at[chunk % 2],
+                shared["stage_sem"].at[chunk % 2],
+            ))
+            stores.append(pltpu.make_async_copy(
+                shared["o_stage"].at[chunk % 2], self.target.at[:, pl.ds(chunk * 512, 512)],
+                shared["stage_sem"].at[2 + chunk % 2],
+            ))
+        loads[0].start()
+        for chunk in range(chunks):
+            loads[chunk].wait()
+            if chunk + 1 < chunks:
+                loads[chunk + 1].start()
+            if chunk >= 2:
+                stores[chunk - 2].wait()
+            total = shared["z_out"][0, :, chunk * 512 : (chunk + 1) * 512].astype(F32)
+            for step in range(spot.outer - 1):
+                total = total + shared["z_stage"][chunk % 2, step].astype(F32)
+            shared["o_stage"][chunk % 2] = total
+            stores[chunk].start()
+        for store in stores[-2:]:
+            store.wait()
+
+
+def row_dot(left, right):
+    return lax.dot_general(left, right, (((1,), (1,)), ((), ())), preferred_element_type=F32)
+
+
+def backward_kernel(
+    heads,
+    count,
+    prefix,
+    sums,
+    tokens,
+    cotangent,
+    wqkv,
+    wo,
+    w1,
+    w2,
+    h1_all,
+    d_rows,
+    qkv_all,
+    mixed_all,
+    lse_v,
+    second,
+    h2_all,
+    gated_all,
+    slope_all,
+    layer_out,
+    input_grad,
+    grad_down,
+    grad_up,
+    grad_out,
+    grad_qkv,
+    vector_sums,
+    bias_sums,
+    land_down,
+    land_up,
+    land_out,
+    land_qkv,
+    weight_v,
+    buf1,
+    buf2,
+    buf3,
+    buf4,
+    buf5,
+    core_send,
+    core_recv,
+    x_send,
+    x_recv,
+    y_in,
+    y_out,
+    z_out,
+    z_stage,
+    o_stage,
+    spare,
+    line,
+    dk_sum,
+    dv_sum,
+    vectors,
+    biases,
+    vector_in,
+    bias_in,
+    part_sum,
+    part_in,
+    y_send,
+    y_recv,
+    z_send,
+    z_recv,
+    g_send,
+    g_recv,
+    s_send,
+    s_recv,
+    v_send,
+    v_recv,
+    b_send,
+    b_recv,
+    t_send,
+    t_recv,
+    stage_sem,
+    load_sem,
+    credit,
+    ready,
+):
+    spot = Spot(count)
+    rows, features = line.shape
+    length = buf1.shape[0]
+    width = wo.shape[0]
+    hidden = w1.shape[1]
+    triple = 3 * width
+    size = width // heads
+    scale = size ** -0.5
+    tail = slice(triple, triple + width)
+    shared = {
+        "y_in": y_in, "y_out": y_out, "z_out": z_out, "z_stage": z_stage, "o_stage": o_stage, "y_send": y_send,
+        "y_recv": y_recv, "z_send": z_send, "z_recv": z_recv, "credit": credit, "stage_sem": stage_sem,
+        "y_busy": {}, "z_busy": {},
+    }
+    down = Reduce(spot, buf1, buf2, slice(0, hidden), land_down, grad_down, shared, 0, False)
+    up = Reduce(spot, buf4, buf3, slice(0, hidden), land_up, grad_up, shared, 1, False)
+    out = Reduce(spot, buf1, buf2, tail, land_out, grad_out, shared, 2, False)
+    qkv = Reduce(spot, buf4, buf5, slice(0, triple), land_qkv, grad_qkv, shared, 3, True)
+
+    def fetch(source, target, slot):
+        copy = pltpu.make_async_copy(source, target, load_sem.at[slot])
+        copy.start()
+        return copy
+
+    load_a = fetch(d_rows, buf1, 0)
+    load_b = fetch(gated_all, buf2, 1)
+    load_w = fetch(w2, weight_v, 2)
+    slopes = [fetch(slope_all.at[pl.ds(part * rows, rows)], (spare, input_grad)[part % 2], 3 + part % 2) for part in range(2)]
+    load_h = fetch(h2_all, buf4, 5)
+    load_c = fetch(cotangent, line, 6)
+    spot.meet(True)
+    vectors[...] = jnp.zeros_like(vectors)
+    biases[...] = jnp.zeros_like(biases)
+    load_a.wait()
+    load_b.wait()
+    order = list(range(1, spot.outer)) + [0]
+    for step in order:
+        down.produce(step)
+    load_w.wait()
+    for part in range(length // rows):
+        held = (spare, input_grad)[part % 2]
+        slopes[part].wait()
+
+        def lower(index, carry, part=part, held=held):
+            where = block_of(index, 512)
+            span = slice(part * rows, (part + 1) * rows)
+            du = row_dot(buf1[span, :], weight_v[where, :]) * held[:, where]
+            biases[pl.ds(index, 1), :] += jnp.sum(du, axis=0, keepdims=True)
+            buf3[span, where] = du.astype(BF16)
+            return carry
+
+        lax.fori_loop(0, hidden // 512, lower, 0)
+        if part + 2 < length // rows:
+            slopes.append(fetch(slope_all.at[pl.ds((part + 2) * rows, rows)], held, 3 + part % 2))
+    load_w = fetch(w1, weight_v, 2)
+    load_s = fetch(second, spare, 3)
+    down.hold()
+    load_q = fetch(qkv_all, buf2.at[:, pl.ds(0, triple)], 0)
+    load_m = fetch(mixed_all, buf2.at[:, pl.ds(triple, width)], 1)
+    load_w.wait()
+    load_h.wait()
+
+    def h2_part(rank, index):
+        return row_dot(buf3[block_of(rank, rows), :], weight_v[block_of(index, 512), :])
+
+    def take_h2(index, total):
+        input_grad[:, block_of(index, 512)] = total
+
+    tensor = (core_send, core_recv, x_send, x_recv)
+    end = tensor_sum(spot, h2_part, *tensor, s_send, s_recv, take_h2)
+    down.serve(1)
+    up.produce(1)
+    down.serve(2)
+    up.produce(2)
+    end()
+    spot.release(ready)
+    load_o = fetch(wo, weight_v.at[pl.ds(0, width)], 2)
+    load_s.wait()
+    load_c.wait()
+    strip = 32
+    base = spot.tensor * rows
+
+    def norm_back(rows_of, gain, grads, keep, first):
+        center, inverse = normal_parts(rows_of)
+        normal = center * inverse
+        vectors[first : first + 1, :] += jnp.sum(grads * normal, axis=0, keepdims=True)
+        vectors[first + 1 : first + 2, :] += jnp.sum(grads, axis=0, keepdims=True)
+        scaled = grads * gain
+        mean = jnp.mean(scaled, axis=-1, keepdims=True)
+        slope = jnp.mean(scaled * normal, axis=-1, keepdims=True)
+        return keep + inverse * (scaled - mean - normal * slope)
+
+    def back2(index, carry):
+        where = block_of(index, strip)
+        dy = line[where, :].astype(F32)
+        dx = norm_back(spare[where, :], sums[2:3, :], input_grad[where, :], dy, 2)
+        vectors[4:5, :] += jnp.sum(dx, axis=0, keepdims=True)
+        vectors[5:6, :] += jnp.sum(dy, axis=0, keepdims=True)
+        input_grad[where, :] = dx
+        buf1[pl.ds(pl.multiple_of(base + index * strip, strip), strip), :] = dx.astype(BF16)
+        return carry
+
+    lax.fori_loop(0, rows // strip, back2, 0)
+    gather = TensorGather(spot, buf1.at[block_of(spot.tensor, rows)], buf1, rows, g_send, g_recv)
+    load_t = fetch(tokens, line, 6)
+    down.serve(3)
+    up.produce(3)
+    gather.pass_on()
+    load_o.wait()
+    gather.finish()
+    load_q.wait()
+    load_m.wait()
+
+    def mix_back(index, carry):
+        where = block_of(index, rows)
+        buf5[where, tail] = row_dot(buf1[where, :], weight_v[0:width, :]).astype(BF16)
+        return carry
+
+    lax.fori_loop(0, length // rows, mix_back, 0)
+    load_w = fetch(wqkv, weight_v.at[:, pl.ds(0, triple)], 2)
+    limit = prefix[0]
+    bench = 256
+
+    def attend(head, carry):
+        q_at = block_of(head, size)
+        k_at = pl.ds(pl.multiple_of(width + head * size, size), size)
+        v_at = pl.ds(pl.multiple_of(2 * width + head * size, size), size)
+        o_at = pl.ds(pl.multiple_of(triple + head * size, size), size)
+        dk_sum[...] = jnp.zeros_like(dk_sum)
+        dv_sum[...] = jnp.zeros_like(dv_sum)
+        for block in range(length // bench):
+            reach = min(length, max((block + 1) * bench, PREFIX_TOP))
+            span = slice(block * bench, (block + 1) * bench)
+            row_of = block * bench + lax.broadcasted_iota(jnp.int32, (bench, reach), 0)
+            place = lax.broadcasted_iota(jnp.int32, (bench, reach), 1)
+            seen = (place <= row_of) | (place < limit)
+            q = buf2[span, q_at]
+            k = buf2[0:reach, k_at]
+            v = buf2[0:reach, v_at]
+            do = buf5[span, o_at]
+            scores = jnp.where(seen, row_dot(q, k), -1e30)
+            probs = jnp.exp(scores - lse_v[head, span, 0:1])
+            d_probs = row_dot(do, v)
+            inner = jnp.sum(probs * d_probs, axis=-1, keepdims=True)
+            d_scores = (probs * (d_probs - inner)).astype(BF16)
+            flip = (((0,), (0,)), ((), ()))
+            dv_sum[0:reach, :] += lax.dot_general(probs.astype(BF16), do, flip, preferred_element_type=F32)
+            dk_sum[0:reach, :] += lax.dot_general(d_scores, q, flip, preferred_element_type=F32)
+            dq = jnp.dot(d_scores, k, preferred_element_type=F32) * scale
+            biases[4:5, q_at] += jnp.sum(dq, axis=0, keepdims=True)
+            buf5[span, q_at] = dq.astype(BF16)
+        buf5[:, k_at] = dk_sum[...].astype(BF16)
+        buf5[:, v_at] = dv_sum[...].astype(BF16)
+        biases[5:6, q_at] += jnp.sum(dv_sum[...], axis=0, keepdims=True)
+        return carry
+
+    half = heads // 2
+    lax.fori_loop(0, half, attend, 0)
+    down.serve(0)
+    up.produce(0)
+    lax.fori_loop(half, heads, attend, 0)
+    load_w.wait()
+
+    def h1_part(rank, index):
+        return row_dot(buf5[block_of(rank, rows), 0:triple], weight_v[block_of(index, 512), 0:triple])
+
+    def take_h1(index, total):
+        spare[:, block_of(index, 512)] = total
+
+    pl.semaphore_wait(ready, 2)
+    end = tensor_sum(spot, h1_part, *tensor, s_send, s_recv, take_h1)
+    up.serve(1)
+    out.produce(1)
+    end()
+    spot.release(ready)
+    load_w = fetch(w2, weight_v, 2)
+    load_t.wait()
+
+    def back1(index, carry):
+        where = block_of(index, strip)
+        dx = norm_back(line[where, :].astype(F32), sums[0:1, :], spare[where, :], input_grad[where, :], 0)
+        input_grad[where, :] = dx
+        return carry
+
+    lax.fori_loop(0, rows // strip, back1, 0)
+    load_s = fetch(second, spare, 3)
+    share = grad_up.shape[0]
+    vector_copies, bias_copies = [], []
+    for step in range(1, count):
+        peer = lax.rem(spot.dp + step, count)
+        vector_copies.append(remote(
+            vectors.at[:, block_of(peer, share)], vector_in.at[spot.dp], v_send.at[step], v_recv.at[step], peer,
+            spot.tensor,
+        ))
+        bias_copies.append(remote(biases, bias_in.at[spot.dp], b_send.at[step], b_recv.at[step], peer, spot.tensor))
+    for copy in vector_copies + bias_copies:
+        copy.start()
+    vector_in[spot.dp] = vectors[:, block_of(spot.dp, share)]
+    bias_in[spot.dp] = biases[...]
+    up.serve(2)
+    out.produce(2)
+    down.settle()
+    up.serve(3)
+    out.produce(3)
+    for copy in vector_copies + bias_copies:
+        copy.wait_recv()
+    total, bias_total = vector_in[0], bias_in[0]
+    for index in range(1, count):
+        total = total + vector_in[index]
+        bias_total = bias_total + bias_in[index]
+    part_sum[...] = total
+    bias_sums[...] = bias_total
+    part_copies = [
+        remote(part_sum, part_in.at[spot.tensor], t_send.at[slot], t_recv.at[slot], spot.dp, peer)
+        for slot, peer in enumerate((spot.x_peer, spot.core_peer, spot.far_peer))
+    ]
+    for copy in part_copies:
+        copy.start()
+    part_in[spot.tensor] = part_sum[...]
+    up.serve(0)
+    out.produce(0)
+    load_b = fetch(gated_all, buf3, 0)
+    load_h = fetch(h1_all, buf4, 1)
+    for copy in part_copies:
+        copy.wait_recv()
+    vector_sums[...] = part_in[0] + part_in[1] + part_in[2] + part_in[3]
+    load_h.wait()
+    load_b.wait()
+    load_w.wait()
+    load_s.wait()
+    out.serve(1)
+    qkv.produce(1)
+    out.serve(2)
+    qkv.produce(2)
+    out.serve(3)
+    qkv.produce(3)
+    up.settle()
+    out.serve(0)
+    qkv.produce(0)
+
+    def down_part(rank, index):
+        return jnp.dot(buf3[block_of(rank, rows), :], weight_v[:, block_of(index, 512)], preferred_element_type=F32)
+
+    def take_out(index, total):
+        where = block_of(index, 512)
+        layer_out[:, where] = (spare[:, where] + total + sums[5:6, where]).astype(BF16)
+
+    pl.semaphore_wait(ready, 2)
+    end = tensor_sum(spot, down_part, *tensor, s_send, s_recv, take_out)
+    out.settle()
+    qkv.serve(1)
+    end()
+    qkv.serve(2)
+    qkv.serve(3)
+    qkv.serve(0)
+    for copy in vector_copies + bias_copies + part_copies:
+        copy.wait_send()
+    qkv.settle()
+    for copy in list(shared["y_busy"].values()) + list(shared["z_busy"].values()):
+        copy.wait_send()
+
+
+def backward_call(heads, count, prefix, sums, tokens, cotangent, weights, saved):
+    rows, features = tokens.shape
+    length = rows * 4
+    share = features // count
+    wqkv, wo, w1, w2 = weights
+    width, hidden, triple = wo.shape[0], w1.shape[1], wqkv.shape[1]
+    outer, inner = split_of(count)
+    shape = jax.ShapeDtypeStruct
+    hbm = pl.BlockSpec(memory_space=pl.ANY)
+    vmem = pl.BlockSpec(memory_space=pltpu.VMEM)
+    dma = pltpu.SemaphoreType.DMA
+    regular = pltpu.SemaphoreType.REGULAR
+    wide = (length, features)
+    return pl.pallas_call(
+        functools.partial(backward_kernel, heads, count),
+        out_shape=[
+            shape((rows, features), BF16),
+            shape((rows, features), F32),
+            shape((share, hidden), F32),
+            shape((share, hidden), F32),
+            shape((share, width), F32),
+            shape((share, triple), F32),
+            shape((8, share), F32),
+            shape((8, 512), F32),
+            shape((outer - 1, share, hidden), BF16),
+            shape((outer - 1, share, hidden), BF16),
+            shape((outer - 1, share, width), BF16),
+            shape((outer - 1, share, triple), BF16),
+        ],
+        in_specs=[pl.BlockSpec(memory_space=pltpu.SMEM), vmem] + [hbm] * 10 + [vmem] + [hbm] * 4,
+        out_specs=[vmem] * 2 + [hbm] * 4 + [vmem] * 2 + [hbm] * 4,
+        scratch_shapes=[
+            pltpu.VMEM((hidden, features), BF16),
+            pltpu.VMEM(wide, BF16),
+            pltpu.VMEM(wide, BF16),
+            pltpu.VMEM(wide, BF16),
+            pltpu.VMEM(wide, BF16),
+            pltpu.VMEM(wide, BF16),
+            pltpu.VMEM((2, rows, features), BF16),
+            pltpu.VMEM((2, rows, features), BF16),
+            pltpu.VMEM((rows, features), BF16),
+            pltpu.VMEM((rows, features), BF16),
+            pltpu.VMEM((outer, share, hidden), BF16),
+            pltpu.VMEM((outer, share, hidden), BF16),
+            pltpu.VMEM((outer, share, hidden), BF16),
+            pltpu.VMEM((2, outer - 1, share, 512), BF16),
+            pltpu.VMEM((2, share, 512), F32),
+            pltpu.VMEM((rows, features), F32),
+            pltpu.VMEM((rows, features), BF16),
+            pltpu.VMEM((length, width // heads), F32),
+            pltpu.VMEM((length, width // heads), F32),
+            pltpu.VMEM((8, features), F32),
+            pltpu.VMEM((8, 512), F32),
+            pltpu.VMEM((count, 8, share), F32),
+            pltpu.VMEM((count, 8, 512), F32),
+            pltpu.VMEM((8, share), F32),
+            pltpu.VMEM((4, 8, share), F32),
+            dma((outer,)),
+            dma((outer,)),
+            dma((outer,)),
+            dma((4, outer)),
+            dma((3,)),
+            dma((3,)),
+            dma((3,)),
+            dma((3,)),
+            dma((count,)),
+            dma((count,)),
+            dma((count,)),
+            dma((count,)),
+            dma((3,)),
+            dma((3,)),
+            dma((4,)),
+            dma((7,)),
+            regular,
+            regular,
+        ],
+        compiler_params=pltpu.CompilerParams(
+            collective_id=1, has_side_effects=True, vmem_limit_bytes=VMEM_BYTES
+        ),
+    )(prefix, sums, tokens, cotangent, wqkv, wo, w1, w2, *saved)
 
 
 def pack_small(features, query_bias, value_bias, up_bias, vectors):
@@ -807,139 +1345,36 @@
     down_bias,
     cotangent,
 ):
-    f32 = jnp.float32
-    bf16 = jnp.bfloat16
     devices = lax.axis_size("dp")
+    me = lax.axis_index("dp")
     heads = query_bias.shape[0]
-    row_features = tokens.shape[1]
     small = pack_small(
-        row_features, query_bias, value_bias, up_bias,
+        tokens.shape[1], query_bias, value_bias, up_bias,
         (norm1_gain, norm1_bias, norm2_gain, norm2_bias, out_bias, down_bias),
     )
-    w_qkv, wo, w1, w2, rows1, d_rows, qkv, mixed, lse, second, rows2, gated, slope, sums = forward_call(
+    results = forward_call(
         heads, devices, prefix, tokens, cotangent, small,
         jnp.concatenate([query_weight, key_weight, value_weight], axis=1), out_weight, up_weight, down_weight,
     )
-    g1f, n1f, g2f, n2f, bof, b2f = (sums[index] for index in range(6))
-    bq, bv, b1 = (
-        jnp.zeros((part.shape[0], part.shape[1] * devices), bf16) for part in (query_bias, value_bias, up_bias)
+    layer_out, input_grad, g_w2, g_w1, g_wo, g_qkv, vectors, biases, *_ = backward_call(
+        heads, devices, prefix, results[-1], tokens, cotangent, results[:4], results[4:-1]
     )
-    heads = bq.shape[0]
-    head_size = bq.shape[1]
-    scale = head_size ** (-0.5)
-    prefix_len = prefix[0]
-    xf = tokens.astype(f32)
-    length = rows1.shape[0]
-    block = min(512, length)
-    count = length // block
-    wq, wk, wv = jnp.split(w_qkv, 3, axis=1)
-    query, keyed, valued = jnp.split(qkv, 3, axis=1)
-    q_heads = head_major(query, heads)
-    k_heads = head_major(keyed, heads)
-    v_heads = head_major(valued, heads)
-    q_blocks = to_blocks(q_heads, count)
-    starts = jnp.arange(count, dtype=jnp.int32) * block
-
-    lse_blocks = to_blocks(lse[:, :, 0], count)
-    mlp_part = jnp.dot(gated, w2, preferred_element_type=f32)
-    mlp_total = lax.psum_scatter(
-        mlp_part.astype(jnp.bfloat16), "tensor", scatter_dimension=0, tiled=True
-    ).astype(jnp.float32)
-    layer_out = (second + mlp_total + b2f).astype(bf16)
-    d_out = cotangent.astype(f32)
-    g_b2 = jnp.sum(d_out, axis=0)
-    d_gated = times_transpose(d_rows, w2)
-    d_hidden = d_gated * slope
-    g_b1 = jnp.sum(d_hidden, axis=0).reshape(b1.shape)
-    d_hidden_low = d_hidden.astype(bf16)
-    d_h2_part = times_transpose(d_hidden_low, w1)
-    g_w2 = contract_rows(gated, d_rows)
-    g_w1 = contract_rows(rows2, d_hidden_low)
-    d_h2 = lax.psum_scatter(d_h2_part.astype(bf16), "tensor", scatter_dimension=0, tiled=True).astype(f32)
-    norm2_back = jax.vjp(layer_norm, second, g2f, n2f)[1]
-    d_second_ln, g_g2, g_n2 = norm2_back(d_h2)
-    d_second = d_out + d_second_ln
-    g_bo = jnp.sum(d_second, axis=0)
-    d_second_low = d_second.astype(bf16)
-    back_rows = lax.all_gather(d_second_low, "tensor", axis=0, tiled=True)
-    g_wo = contract_rows(mixed, back_rows)
-    d_mixed = times_transpose(back_rows, wo).astype(bf16)
-    do_blocks = to_blocks(head_major(d_mixed, heads), count)
-
-    def backward_block(carry, item):
-        d_keys, d_vals = carry
-        q_block, do_block, lse_block, start = item
-        scores = masked_scores(q_block, k_heads, start, prefix_len)
-        probs = jnp.exp(scores - lse_block[..., None])
-        d_probs = jnp.einsum("hqd,hkd->hqk", do_block, v_heads, preferred_element_type=f32)
-        d_vals = d_vals + jnp.einsum(
-            "hqk,hqd->hkd", probs.astype(bf16), do_block, preferred_element_type=f32
-        )
-        inner = jnp.sum(probs * d_probs, axis=-1, keepdims=True)
-        d_scores = (probs * (d_probs - inner)).astype(bf16)
-        d_query = jnp.einsum("hqk,hkd->hqd", d_scores, k_heads, preferred_element_type=f32)
-        d_keys = d_keys + jnp.einsum("hqk,hqd->hkd", d_scores, q_block, preferred_element_type=f32)
-        return ((d_keys, d_vals), d_query)
-
-    empty = jnp.zeros(k_heads.shape, f32)
-    (d_keys, d_vals), dq_blocks = lax.scan(
-        backward_block, (empty, empty), (q_blocks, do_blocks, lse_blocks, starts)
-    )
-    d_query = row_major(from_blocks(dq_blocks)) * scale
-    d_keys = row_major(d_keys)
-    d_vals = row_major(d_vals)
-    g_bq = jnp.sum(d_query, axis=0).reshape(bq.shape)
-    g_bv = jnp.sum(d_vals, axis=0).reshape(bv.shape)
-    dq_low, dk_low, dv_low = (d_query.astype(bf16), d_keys.astype(bf16), d_vals.astype(bf16))
-    g_wq = contract_rows(rows1, dq_low)
-    g_wk = contract_rows(rows1, dk_low)
-    g_wv = contract_rows(rows1, dv_low)
-    d_h1_part = (
-        times_transpose(dq_low, wq) + times_transpose(dk_low, wk) + times_transpose(dv_low, wv)
-    )
-    d_h1 = lax.psum_scatter(d_h1_part.astype(bf16), "tensor", scatter_dimension=0, tiled=True).astype(f32)
-    norm1_back = jax.vjp(layer_norm, xf, g1f, n1f)[1]
-    d_input_ln, g_g1, g_n1 = norm1_back(d_h1)
-    input_grad = d_second + d_input_ln
-    def scatter(part, dim):
-        return lax.psum_scatter(part.astype(bf16), "dp", scatter_dimension=dim, tiled=True).astype(f32)
-
-    s_w2, s_w1, s_wo = scatter(g_w2, 1), scatter(g_w1, 0), scatter(g_wo, 1)
-    s_wq, s_wk, s_wv = scatter(g_wq, 0), scatter(g_wk, 0), scatter(g_wv, 0)
-
-    def by_device(part):
-        return jnp.moveaxis(part.reshape(part.shape[:-1] + (devices, -1)), -2, 0).reshape(devices, -1)
-
-    rows = [by_device(part) for part in (g_bq, g_bv, g_b1, g_g1, g_n1, g_g2, g_n2, g_bo, g_b2)]
-    total = lax.psum_scatter(jnp.concatenate(rows, axis=1), "dp", scatter_dimension=0, tiled=True)[0]
-    offset = 0
-    outs = []
-    for part in (query_bias, value_bias, up_bias):
-        outs.append(total[offset : offset + part.size].reshape(part.shape))
-        offset += part.size
-    s_bq, s_bv, s_b1 = outs
-    vectors = lax.psum_scatter(
-        total[offset:].reshape(6, lax.axis_size("tensor"), -1), "tensor", scatter_dimension=1, tiled=True
-    ).reshape(6, -1)
-    s_g1, s_n1, s_g2, s_n2, s_bo, s_b2 = (vectors[index] for index in range(6))
+    g_wq, g_wk, g_wv = jnp.split(g_qkv, 3, axis=1)
+    vectors = vectors.reshape(8, lax.axis_size("tensor"), -1)
+    vectors = lax.dynamic_index_in_dim(vectors, lax.axis_index("tensor"), axis=1, keepdims=False)
+
+    def own(flat, part):
+        whole = flat.reshape(part.shape[0], -1)
+        return lax.dynamic_slice_in_dim(whole, me * part.shape[1], part.shape[1], axis=1)
+
+    width = out_weight.shape[0]
+    up_size = up_bias.size * devices
+    g_b1 = own(biases[: up_size // 512].reshape(-1), up_bias)
+    g_bq = own(biases[4, :width], query_bias)
+    g_bv = own(biases[5, :width], value_bias)
     return (
-        layer_out,
-        input_grad,
-        s_wq,
-        s_wk,
-        s_wv,
-        s_wo,
-        s_bq,
-        s_bv,
-        s_w1,
-        s_w2,
-        s_b1,
-        s_g1,
-        s_n1,
-        s_g2,
-        s_n2,
-        s_bo,
-        s_b2,
+        layer_out, input_grad, g_wq, g_wk, g_wv, g_wo.T, g_bq, g_bv, g_w1, g_w2.T, g_b1,
+        vectors[0], vectors[1], vectors[2], vectors[3], vectors[4], vectors[5],
     )
 
 
@@ -950,11 +1385,12 @@
     share = features // devices
     fits = (
         lax.axis_size("tensor") == 4
-        and devices <= 8
+        and devices == 8
         and share % 128 == 0
         and tokens.shape[0] == 256
-        and 3 * query_weight.shape[1] <= features
-        and up_weight.shape[1] <= features
+        and query_weight.shape[1] == 512
+        and features == 2048
+        and up_weight.shape[1] == 2048
     )
     return fast(*args) if fits else plain(*args)
 

time: 1220 us -> 739 us (0.61)
  waiting for transfers between devices: 564 us -> 0 us
  Pallas kernels: 348 us -> 699 us
  matrix products: 150 us -> 0 us
  blocking collectives: 43.8 us -> 0 us
  other arithmetic: 46.2 us -> 8.05 us
  local copies, waits for them, and re-layouts: 38 us -> 22.8 us
  between operations: 16.6 us -> 1.61 us
    reduce_scatter x9 -> x0, waiting for transfers between devices: 564 us -> none  [the longest x6 434 us: scatter(): lax.psum_scatter(part.astype(bf16), 'dp', scatter_dimension=dim, tiled=True)]
    pallas_call x0 -> x1, Pallas kernels: none -> 351 us  [backward_call(): pl.pallas_call(functools.partial(backward_kernel, heads, count), out_shap...]
    dot_general x23 -> x0, matrix products: 150 us -> none  [the longest x6 52.5 us: contract_rows(): jnp.einsum('ld,le->de', left, right, preferred_element_type=jnp.float32)]
    unnamed x2 -> x0, blocking collectives: 43.8 us -> none
    convert_element_type x10 -> x0, other arithmetic: 20 us -> none  [the longest x6 12.7 us: scatter(): lax.psum_scatter(part.astype(bf16), 'dp', scatter_dimension=dim, tiled=True)]
    reduce_sum x10 -> x0, other arithmetic: 14.6 us -> none  [the longest x2 3.69 us: layer_norm(): return center * lax.rsqrt(spread + 1e-05) * gain + shift]
  transfers between devices with their start and end apart: 10 -> 0, of which waited for: 9 -> 0; matrix products, arithmetic and copies ran while one was open for 14% -> 0% of each run, Pallas kernels for 0% -> 0%
where the time goes in v2:
time: 739 us; the launch traced here: 732 us
  Pallas kernels  699 us (95%)
  local copies, waits for them, and re-layouts  22.8 us (3%)
  other arithmetic  8.05 us (1%)
    pallas_call x1, Pallas kernels, backward_call(): pl.pallas_call(functools.partial(backward_kernel, heads, count), out_shap...  351 us
    pallas_call x1, Pallas kernels, forward_call(): pl.pallas_call(functools.partial(forward_kernel, heads, count), out_shape...  348 us

profile of v2, /device:TPU:9, one launch (start us, length us, event | category | flops | bytes accessed | tf_op | source)
XLA Modules:
  0.0 731.7 jit_solution(4485994970651764864)
XLA Ops:
  0.7 0.7 convert_element_type.7
  1.3 0.2 dynamic_update_slice.39
  1.5 0.7 convert_element_type.8
  2.2 0.2 dynamic_update_slice.40
  2.4 0.7 stack.62
  3.1 0.6 stack.41.clone.5
  3.7 0.6 constant_dynamic-update-slice_fusion
  4.3 0.7 stack.61
  4.9 0.6 stack.41.clone.4
  5.5 0.6 constant_dynamic-update-slice_fusion.1
  6.1 0.7 stack.60
  6.7 0.6 stack.41.clone.3
  7.4 0.6 constant_dynamic-update-slice_fusion.2
  7.9 0.7 stack.59
  8.6 0.6 stack.41.clone.2
  9.2 0.6 constant_dynamic-update-slice_fusion.3
  9.7 0.7 stack.58
  10.4 0.6 stack.41.clone.1
  11.0 0.6 constant_dynamic-update-slice_fusion.4
  11.6 0.7 stack.57
  12.2 0.6 stack.41.clone
  12.8 0.6 constant_dynamic-update-slice_fusion.5
  13.4 0.7 convert_element_type.10
  14.1 0.2 dynamic_update_slice.41
  14.2 1.5 stack.56.small
  16.4 2.0 pad_maximum_fusion.qkv_shard
  18.4 348.1 %shard_map.305 = (bf16[2048,1536]{1,0:T(8,128)(2,1)}, bf16[512,2048]{1,0:T(8,128)(2,1)}, bf16[2048,2048]{1,0:T(8,128)(2,1)}, bf16[2048,2048]{1,0:T(8,128)(2,1)},...) custom-call(s32[1]{0:T(128)S(6)} %copy.49.prefix, ...), custom_call_target="tpu_custom_call" | custom-call | tf_op jit(solution)/shard_map/pallas_call | solution.py:486
  366.6 351.1 %shard_map.306 = (bf16[256,2048]{1,0:T(8,128)(2,1)}, f32[256,2048]{1,0:T(8,128)}, f32[256,2048]{1,0:T(8,128)}, f32[256,2048]{1,0:T(8,128)}, f32[256,512]{1,0:T(8...) custom-call(s32[1]{0:T(128)S(6)} %copy.49.prefix, ...), custom_call_target="tpu_custom_call" | custom-call | tf_op jit(solution)/shard_map/pallas_call | solution.py:1005
  717.7 0.8 fusion.7
  718.5 0.7 constant_dynamic-slice_fusion.7
  719.1 0.0 copy-start.2
  719.1 3.0 copy.36
  722.1 0.0 copy-done.2
  722.1 0.0 copy-start.4
  722.1 0.0 copy-start.5
  722.2 0.0 copy-start.3
  722.2 1.2 fusion.6
  723.3 0.0 copy-start.1
  723.3 2.2 copy.35
  725.5 0.0 copy-done.4
  725.5 0.7 constant_dynamic-slice_fusion.6
  726.2 0.0 copy-done.5
  726.2 0.1 reshape.77
  726.3 0.5 fusion
  726.8 0.0 copy-done.3
  726.8 1.0 copy.50
  727.8 0.0 copy-done.1
  727.8 0.0 copy-start
  727.8 1.3 copy.51
  729.1 1.0 copy-done
  730.2 1.3 copy.52
  (7 shorter events, 0.0 us)
Async XLA Ops:
  719.1 3.0 copy-start.2
  722.1 3.4 copy-start.4
  722.1 4.1 copy-start.5
  722.2 4.7 copy-start.3
  723.3 4.5 copy-start.1
  727.8 2.3 copy-start

commit v3 on v2

--- a/solution.py
+++ b/solution.py
@@ -71,70 +71,110 @@
 
 
 class Spread:
-    def __init__(self, spot, pieces, z_send, z_recv, y_send, y_recv):
-        self.spot, self.pieces = spot, pieces
-        self.sems = (z_send, z_recv, y_send, y_recv)
+    AHEAD = 3
+
+    def __init__(self, spot, pieces, late, own_at, sems):
+        self.spot, self.pieces, self.late, self.sems = spot, pieces, late, sems
+        self.flows = [(piece, 0) for piece in range(len(pieces)) if piece != late] + [(late, 0), (late, 1)]
+        self.own_at = own_at
+        self.order = (2, jnp.where(spot.row == 0, 3, 1), jnp.where(spot.row == 0, 1, 3))
         self.sent = []
-        self.todo = [(piece, step) for piece in range(len(pieces)) for step in range(1, spot.outer)]
-        self.own_next = 0
-
-    def send_rows(self, piece):
+        self.todo = [(flow, place) for flow in range(len(self.flows)) for place in range(3)]
+        for piece in own_at[None]:
+            self.send_own(piece)
+        for flow in range(self.AHEAD):
+            self.send_rows(flow)
+
+    def owner(self, row, side):
+        return row * 2 + lax.rem(self.spot.column + side, 2)
+
+    def launch(self, condition, copy):
+        if condition is None:
+            copy().start()
+        else:
+            pl.when(condition)(lambda: copy().start())
+        self.sent.append((condition, copy))
+
+    def along(self, flow, step, source_row, target_row, send_slot):
+        piece, side = self.flows[flow]
         source, target = self.pieces[piece]
-        for step in range(1, self.spot.outer):
-            copy = remote(
-                source, target(self.spot.dp), self.sems[0].at[piece, step], self.sems[1].at[piece, step],
-                self.spot.across(step), self.spot.tensor,
+        place = target(self.owner(source_row, side))
+        if source_row is not self.spot.row or side:
+            source = place
+        return remote(
+            source, place, self.sems[0].at[flow, send_slot], self.sems[1].at[flow, step],
+            target_row * 2 + self.spot.column, self.spot.tensor,
+        )
+
+    def send_rows(self, flow):
+        row = self.spot.row
+        if self.flows[flow][1]:
+            self.beside(self.late, 0, row).wait_recv()
+        for step, condition in ((2, None), (1, row != 3), (3, row != 0)):
+            self.launch(
+                condition,
+                functools.partial(self.along, flow, step, row, lax.rem(row + step, 4), step),
             )
-            copy.start()
-            self.sent.append(copy)
-
-    def y_copies(self, piece, step):
+
+    def hand_over(self, flow):
+        row = self.spot.row
+        self.launch(
+            (row == 1) | (row == 2),
+            lambda: self.along(flow, 2 * row - 1, lax.rem(row + 2, 4), (row - 1) * 3, 0),
+        )
+
+    def beside(self, piece, step, source_row):
         spot = self.spot
         source, target = self.pieces[piece]
-        owner = spot.across(spot.outer - step) if step else spot.dp
-        if step:
-            source = target(owner)
-        copies = []
-        for side in range(1, spot.inner):
-            copies.append(remote(
-                source, target(owner), self.sems[2].at[piece, step, side], self.sems[3].at[piece, step, side],
-                spot.beside(side), spot.tensor,
-            ))
-        return copies
-
-    def send_own(self, upto):
-        while self.own_next < min(upto, len(self.pieces)):
-            for copy in self.y_copies(self.own_next, 0):
-                copy.start()
-                self.sent.append(copy)
-            self.own_next += 1
+        place = target(self.owner(source_row, 0))
+        if source_row is not spot.row:
+            source = place
+        return remote(
+            source, place, self.sems[2].at[piece, step], self.sems[3].at[piece, step], spot.beside(1), spot.tensor
+        )
+
+    def beside_arrival(self, piece, step, source_row):
+        source, target = self.pieces[piece]
+        return remote(
+            source, target(self.owner(source_row, 1)), self.sems[2].at[piece, step], self.sems[3].at[piece, step],
+            self.spot.beside(1), self.spot.tensor,
+        )
+
+    def send_own(self, piece):
+        self.launch(None, functools.partial(self.beside, piece, 0, self.spot.row))
 
     def forward(self, count):
         for _ in range(count):
             if not self.todo:
                 return
-            piece, step = self.todo.pop(0)
-            source, target = self.pieces[piece]
-            remote(
-                source, target(self.spot.across(self.spot.outer - step)), self.sems[0].at[piece, step],
-                self.sems[1].at[piece, step], self.spot.across(step), self.spot.tensor,
-            ).wait_recv()
-            for copy in self.y_copies(piece, step):
-                copy.start()
-                self.sent.append(copy)
-            if step == self.spot.outer - 1:
-                self.send_own(piece + 4)
+            flow, place = self.todo.pop(0)
+            step = self.order[place]
+            row = lax.rem(self.spot.row + 4 - step, 4)
+            self.along(flow, step, row, self.spot.row, 0).wait_recv()
+            if place == 0:
+                self.hand_over(flow)
+            piece = self.flows[flow][0]
+            if piece != self.late:
+                self.launch(None, functools.partial(self.beside, piece, step, row))
+            if place == 2:
+                if flow + self.AHEAD < len(self.flows):
+                    self.send_rows(flow + self.AHEAD)
+                for own in self.own_at.get(flow, ()):
+                    self.send_own(own)
 
     def arrived(self, piece):
-        while self.todo and self.todo[0][0] <= piece:
+        while self.todo and self.flows[self.todo[0][0]][0] <= piece:
             self.forward(1)
-        for step in range(self.spot.outer):
-            for copy in self.y_copies(piece, step):
-                copy.wait_recv()
+        if piece != self.late:
+            for step in range(4):
+                self.beside_arrival(piece, step, lax.rem(self.spot.row + 4 - step, 4)).wait_recv()
 
     def finish(self):
-        for copy in self.sent:
-            copy.wait_send()
+        for condition, copy in self.sent:
+            if condition is None:
+                copy().wait_send()
+            else:
+                pl.when(condition)(lambda copy=copy: copy().wait_send())
 
 
 class TensorGather:
@@ -281,8 +321,8 @@
     ]
     pieces.append((out_shard, lambda owner: wo.at[:, block_of(owner, depth)]))
     pieces += [
-        (up_shard.at[pl.ds(part * half, half)],
-         lambda owner, part=part: w1.at[block_of(owner * 2 + part, half)])
+        (up_shard.at[:, pl.ds(part * tall, tall)],
+         lambda owner, part=part: w1.at[block_of(owner, depth), pl.ds(part * tall, tall)])
         for part in range(2)
     ]
     pieces += [
@@ -290,7 +330,6 @@
          lambda owner, part=part: w2.at[pl.ds(part * tall, tall), block_of(owner, depth)])
         for part in range(2)
     ]
-    spread = Spread(spot, pieces, z_send, z_recv, y_send, y_recv)
     locals_ = []
 
     def keep(source, target):
@@ -307,21 +346,32 @@
         )
         copy.start()
         small_copies.append(copy)
-    for piece in range(len(pieces)):
-        spread.send_rows(piece)
-    spread.send_own(4)
+    spread = Spread(
+        spot, pieces, 6, {None: (0, 1, 2, 3), 0: (4,), 1: (6,), 2: (5,)}, (z_send, z_recv, y_send, y_recv)
+    )
     for source, target in pieces:
         keep(source, target(spot.dp))
     smalls[spot.dp] = small[...]
-    for step, copy in enumerate(small_copies):
+    for step in range(1, count):
+        owner = lax.rem(spot.dp + count - step, count)
         remote(
-            small, smalls.at[lax.rem(spot.dp + count - step - 1, count)], small_send.at[step + 1],
-            small_recv.at[step + 1], spot.dp, spot.core_peer,
+            small, smalls.at[owner], small_send.at[step], small_recv.at[step], spot.dp, spot.core_peer
         ).wait_recv()
-    total = smalls[0]
+    sums[...] = jnp.zeros_like(sums)
+    joint = smalls[0, 0:24, :]
     for index in range(1, count):
-        total = total + smalls[index]
-    sums[...] = total
+        joint = joint + smalls[index, 0:24, :]
+    lanes = 128
+    for head in range(heads):
+        sums[6:7, head * lanes : (head + 1) * lanes] = joint[head : head + 1, :]
+        start = 2 * width + head * lanes
+        sums[6:7, start : start + lanes] = joint[4 + head : 5 + head, :]
+    for line in range(hidden // lanes):
+        sums[7:8, line * lanes : (line + 1) * lanes] = joint[8 + line : 9 + line, :]
+    for owner in range(count):
+        for part in range(2):
+            start = owner * depth + part * lanes
+            sums[0:6, start : start + lanes] = smalls[owner, 24 + 8 * part : 30 + 8 * part, :]
 
     strip = 32
     base = spot.tensor * rows
@@ -338,19 +388,19 @@
     gather1 = TensorGather(spot, h1v.at[block_of(spot.tensor, rows)], h1v, rows, g_send.at[0], g_recv.at[0])
     gather_d = TensorGather(spot, cotangent, d_rows, rows, g_send.at[1], g_recv.at[1])
     keep(cotangent, d_rows.at[block_of(spot.tensor, rows)])
-    spread.forward(spot.outer - 1)
+    spread.forward(1)
     gather1.pass_on()
-    spread.forward(spot.outer - 1)
+    spread.forward(2)
+    gather_d.pass_on()
     gather1.finish()
     keep(h1v, h1_all)
-    gather_d.pass_on()
+    spread.forward(6)
     spread.arrived(0)
     spread.arrived(1)
     for copy in locals_[:2]:
         copy.wait()
     load = pltpu.make_async_copy(wqkv, wqkv_v, local_sem.at[14])
     load.start()
-    spread.forward(1)
     load.wait()
 
     def project(index, carry):
@@ -365,7 +415,7 @@
 
     lax.fori_loop(0, length // rows, project, 0)
     keep(qkv_v, qkv_all)
-    spread.forward(2)
+    spread.forward(3)
     size = width // heads
     limit = prefix[0]
     bench = 256
@@ -392,10 +442,11 @@
             return carry
 
         lax.fori_loop(0, heads, attend, 0)
-        if block % 2 == 1:
-            spread.forward(1)
+        if block == 2:
+            spread.forward(2)
     keep(mixed_v, mixed_all)
     keep(lse_v, lse_all)
+    spread.forward(1)
     spread.arrived(2)
     locals_[2].wait()
     load = pltpu.make_async_copy(wo, wo_v, local_sem.at[14])
@@ -412,7 +463,6 @@
     end = tensor_sum(
         spot, out_part, core_send, core_recv, x_send, x_recv, s_send.at[0], s_recv.at[0], take_second
     )
-    spread.forward(spot.outer - 1)
     end()
 
     def norm2(index, carry):
@@ -425,45 +475,45 @@
 
     lax.fori_loop(0, rows // strip, norm2, 0)
     gather2 = TensorGather(spot, h2v.at[block_of(spot.tensor, rows)], h2v, rows, g_send.at[2], g_recv.at[2])
-    spread.forward(spot.outer - 1)
     gather2.pass_on()
+    spread.forward(3)
     gather2.finish()
     gather_d.finish()
     keep(h2v, h2_all)
-    spread.arrived(3)
-    spread.arrived(4)
-    for copy in locals_[3:5]:
-        copy.wait()
-    load = pltpu.make_async_copy(w1, w1_v, local_sem.at[14])
-    load.start()
-    spread.forward(1)
-    load.wait()
     stored = []
-    for block in range(length // rows):
-        slot = block % 2
-        if block >= 2:
-            stored[block - 2].wait()
-
-        def lift(index, carry, block=block, slot=slot):
-            where = block_of(index, 512)
-            u = jnp.dot(
-                h2v[block * rows : (block + 1) * rows, :], w1_v[:, where], preferred_element_type=F32
-            ) + sums[7:8, where]
-            below = 0.5 * (1.0 + lax.erf(u * 0.7071067811865476))
-            gated_v[block * rows : (block + 1) * rows, where] = (u * below).astype(BF16)
-            slope_v[slot, :, where] = below + u * (0.3989422804014327 * jnp.exp(-0.5 * u * u))
-            return carry
-
-        lax.fori_loop(0, hidden // 512, lift, 0)
-        copy = pltpu.make_async_copy(
-            slope_v.at[slot], slope_all.at[pl.ds(block * rows, rows)], local_sem.at[15 + slot]
-        )
-        copy.start()
-        stored.append(copy)
-        spread.forward(1)
+    for part in range(2):
+        spread.arrived(3 + part)
+        locals_[3 + part].wait()
+        lanes_of = pl.ds(part * tall, tall)
+        load = pltpu.make_async_copy(w1.at[:, lanes_of], w1_v.at[:, lanes_of], local_sem.at[14])
+        load.start()
+        load.wait()
+        for block in range(length // rows):
+            slot = block % 2
+            if len(stored) >= 2:
+                stored[-2].wait()
+
+            def lift(index, carry, block=block, slot=slot, part=part):
+                where = block_of(part * (tall // 512) + index, 512)
+                u = jnp.dot(
+                    h2v[block * rows : (block + 1) * rows, :], w1_v[:, where], preferred_element_type=F32
+                ) + sums[7:8, where]
+                below = 0.5 * (1.0 + lax.erf(u * 0.7071067811865476))
+                gated_v[block * rows : (block + 1) * rows, where] = (u * below).astype(BF16)
+                slope_v[slot, :, block_of(index, 512)] = below + u * (0.3989422804014327 * jnp.exp(-0.5 * u * u))
+                return carry
+
+            lax.fori_loop(0, tall // 512, lift, 0)
+            copy = pltpu.make_async_copy(
+                slope_v.at[slot], slope_all.at[pl.ds(block * rows, rows), lanes_of], local_sem.at[15 + slot]
+            )
+            copy.start()
+            stored.append(copy)
+        if part == 0:
+            spread.forward(3)
     keep(gated_v, gated_all)
+    spread.arrived(6)
     spread.arrived(5)
-    spread.arrived(6)
     spread.finish()
     for copy in small_copies:
         copy.wait_send()
@@ -504,7 +554,7 @@
         in_specs=[pl.BlockSpec(memory_space=pltpu.SMEM)] + [vmem] * 7,
         out_specs=[hbm] * 9 + [vmem] + [hbm] * 3 + [vmem],
         scratch_shapes=[
-            pltpu.VMEM((count, 8, features), F32),
+            pltpu.VMEM((count, 40, 128), F32),
             pltpu.VMEM((length, features), BF16),
             pltpu.VMEM((features, triple), BF16),
             pltpu.VMEM((length, triple), BF16),
@@ -518,13 +568,13 @@
             pltpu.VMEM((length, features), BF16),
             pltpu.VMEM((features, hidden), BF16),
             pltpu.VMEM((length, hidden), BF16),
-            pltpu.VMEM((2, rows, hidden), F32),
+            pltpu.VMEM((2, rows, hidden // 2), F32),
             dma((count,)),
             dma((count,)),
+            dma((pieces + 1, outer)),
+            dma((pieces + 1, outer)),
             dma((pieces, outer)),
             dma((pieces, outer)),
-            dma((pieces, outer, inner)),
-            dma((pieces, outer, inner)),
             dma((3, 3)),
             dma((3, 3)),
             dma((1, 3)),
@@ -1071,24 +1121,13 @@
     )(prefix, sums, tokens, cotangent, wqkv, wo, w1, w2, *saved)
 
 
-def pack_small(features, query_bias, value_bias, up_bias, vectors):
+def pack_small(biases, vectors):
     devices = lax.axis_size("dp")
-    me = lax.axis_index("dp")
-    rows = []
-    for part in vectors:
-        start = me * part.shape[0]
-        rows.append(lax.dynamic_update_slice(jnp.zeros((features,), F32), part.astype(F32), (start,)))
-
-    def spread_rows(part):
-        wide = jnp.zeros((part.shape[0], part.shape[1] * devices), F32)
-        return lax.dynamic_update_slice(wide, part.astype(F32), (0, me * part.shape[1])).reshape(-1)
-
-    q = spread_rows(query_bias)
-    joint = jnp.concatenate([q, jnp.zeros_like(q), spread_rows(value_bias)])
-    rows.append(jnp.pad(joint, (0, features - joint.size)))
-    u = spread_rows(up_bias)
-    rows.append(jnp.pad(u, (0, features - u.size)))
-    return jnp.stack(rows)
+    parts = jnp.concatenate(biases, axis=0)
+    lane = lax.broadcasted_iota(jnp.int32, (parts.shape[0], parts.shape[1] * devices), 1)
+    wide = jnp.where(lane // parts.shape[1] == lax.axis_index("dp"), jnp.tile(parts, (1, devices)), 0)
+    halves = jnp.pad(jnp.stack(vectors), ((0, 2), (0, 0)))
+    return jnp.concatenate([wide, halves[:, :128], halves[:, 128:]], axis=0).astype(F32)
 
 
 def layer_norm(rows, gain, shift):
@@ -1349,8 +1388,7 @@
     me = lax.axis_index("dp")
     heads = query_bias.shape[0]
     small = pack_small(
-        tokens.shape[1], query_bias, value_bias, up_bias,
-        (norm1_gain, norm1_bias, norm2_gain, norm2_bias, out_bias, down_bias),
+        (query_bias, value_bias, up_bias), (norm1_gain, norm1_bias, norm2_gain, norm2_bias, out_bias, down_bias)
     )
     results = forward_call(
         heads, devices, prefix, tokens, cotangent, small,
@@ -1389,6 +1427,7 @@
         and share % 128 == 0
         and tokens.shape[0] == 256
         and query_weight.shape[1] == 512
+        and args[6].shape[0] == 4
         and features == 2048
         and up_weight.shape[1] == 2048
     )

time: 739 us -> 658 us (0.89)
  Pallas kernels: 699 us -> 627 us
    pallas_call x1, Pallas kernels: 348 us -> 272 us  [forward_call(): pl.pallas_call(functools.partial(forward_kernel, heads, count), out_shape...]
where the time goes in v3:
time: 658 us; the launch traced here: 650 us
  Pallas kernels  627 us (95%)
  local copies, waits for them, and re-layouts  17.7 us (3%)
    pallas_call x1, Pallas kernels, backward_call(): pl.pallas_call(functools.partial(backward_kernel, heads, count), out_shap...  356 us
    pallas_call x1, Pallas kernels, forward_call(): pl.pallas_call(functools.partial(forward_kernel, heads, count), out_shape...  272 us

profile of v3, /device:TPU:9, one launch (start us, length us, event | category | flops | bytes accessed | tf_op | source)
XLA Modules:
  0.0 650.3 jit_solution(4506476546585378315)
XLA Ops:
  0.7 0.7 pad_maximum_fusion.1
  1.4 0.1 tile.10
  1.5 0.7 stack.21
  2.2 0.7 stack.22
  2.9 0.7 stack.23
  3.5 0.7 stack.24
  4.2 0.7 stack.25
  4.8 0.7 stack.26
  5.5 0.6 maximum_convert_fusion.small
  6.8 2.0 pad_maximum_fusion.qkv_shard
  8.8 271.6 %shard_map.305 = (bf16[2048,1536]{1,0:T(8,128)(2,1)}, bf16[512,2048]{1,0:T(8,128)(2,1)}, bf16[2048,2048]{1,0:T(8,128)(2,1)}, bf16[2048,2048]{1,0:T(8,128)(2,1)},...) custom-call(s32[1]{0:T(128)S(6)} %copy.42.prefix, ...), custom_call_target="tpu_custom_call" | custom-call | tf_op jit(solution)/shard_map/pallas_call | solution.py:536
  280.4 355.7 %shard_map.306 = (bf16[256,2048]{1,0:T(8,128)(2,1)}, f32[256,2048]{1,0:T(8,128)}, f32[256,2048]{1,0:T(8,128)}, f32[256,2048]{1,0:T(8,128)}, f32[256,512]{1,0:T(8...) custom-call(s32[1]{0:T(128)S(6)} %copy.42.prefix, ...), custom_call_target="tpu_custom_call" | custom-call | tf_op jit(solution)/shard_map/pallas_call | solution.py:1055
  636.1 0.0 copy-start.2
  636.2 3.0 copy.38
  639.2 0.0 copy-done.2
  639.2 0.0 copy-start.4
  639.2 0.0 copy-start.5
  639.2 0.0 copy-start.3
  639.2 1.2 fusion.7
  640.4 0.0 copy-start.1
  640.4 2.2 copy.37
  642.5 0.0 copy-done.4
  642.6 0.7 constant_dynamic-slice_fusion.6
  643.2 0.0 copy-done.5
  643.2 0.1 reshape.53
  643.3 0.5 fusion.1
  643.9 0.7 constant_dynamic-slice_fusion.7
  644.5 0.6 constant_dynamic-slice_fusion.8
  645.2 0.0 copy-done.3
  645.2 1.0 copy.43
  646.1 0.0 copy-done.1
  646.1 0.0 copy-start
  646.1 1.3 copy.44
  647.5 1.0 copy-done
  648.5 1.3 copy.45
  (9 shorter events, 0.1 us)
Async XLA Ops:
  636.1 3.0 copy-start.2
  639.2 3.4 copy-start.4
  639.2 4.1 copy-start.5
  639.2 6.0 copy-start.3
  640.4 5.8 copy-start.1
  646.1 2.3 copy-start

commit v4 on v3

--- a/solution.py
+++ b/solution.py
@@ -202,7 +202,7 @@
             copy.wait_send()
 
 
-def tensor_sum(spot, product, core_send, core_recv, x_send, x_recv, send, recv, finish):
+def tensor_sum(spot, product, core_send, core_recv, x_send, x_recv, send, recv, finish, between=None):
     width = core_send.shape[2]
     chunk = 512
     count = width // chunk
@@ -220,6 +220,8 @@
         copy = remote(core_send.at[slot], core_recv.at[slot], send.at[slot], recv.at[slot], spot.dp, spot.core_peer)
         copy.start()
         copies.append(copy)
+    if between is not None:
+        between()
     copies[0].wait_recv()
 
     def join(index, carry):
@@ -592,7 +594,7 @@
         self.width = lanes.stop - lanes.start
         self.share = target.shape[0]
         self.stepped = {}
-        self.held = False
+        self.held = ()
 
     def block(self, owner, take):
         turned = jnp.transpose(self.left[:, block_of(owner, self.share)])
@@ -632,9 +634,9 @@
         copy.start()
         shared["y_busy"][step] = copy
 
-    def hold(self):
-        self.held = True
-        for step in range(self.spot.outer):
+    def hold(self, steps):
+        self.held = steps
+        for step in steps:
 
             def take(where, value, step=step):
                 self.shared["z_out"][step, :, where] = value.astype(BF16)
@@ -647,7 +649,7 @@
         if step in shared["z_busy"]:
             shared["z_busy"].pop(step).wait_send()
         y_in, z_out = shared["y_in"], shared["z_out"]
-        if self.held:
+        if step in self.held:
             for start in range(0, self.width, 512):
                 where = slice(start, start + 512)
                 z_out[step, :, where] = (z_out[step, :, where].astype(F32) + y_in[step, :, where].astype(F32)).astype(BF16)
@@ -671,29 +673,29 @@
         for step in range(1, spot.outer):
             self.z_copy(step).wait_recv()
         loads, stores = [], []
-        chunks = self.width // 512
+        chunks = self.width // 128
         for chunk in range(chunks):
+            slot = chunk % 4
             loads.append(pltpu.make_async_copy(
-                self.landing.at[:, :, pl.ds(chunk * 512, 512)], shared["z_stage"].at[chunk % 2],
-                shared["stage_sem"].at[chunk % 2],
+                self.landing.at[:, :, pl.ds(chunk * 128, 128)], shared["z_stage"].at[slot], shared["stage_sem"].at[slot]
             ))
             stores.append(pltpu.make_async_copy(
-                shared["o_stage"].at[chunk % 2], self.target.at[:, pl.ds(chunk * 512, 512)],
-                shared["stage_sem"].at[2 + chunk % 2],
+                shared["o_stage"].at[slot], self.target.at[:, pl.ds(chunk * 128, 128)], shared["stage_sem"].at[4 + slot]
             ))
-        loads[0].start()
+        for load in loads[:3]:
+            load.start()
         for chunk in range(chunks):
             loads[chunk].wait()
-            if chunk + 1 < chunks:
-                loads[chunk + 1].start()
-            if chunk >= 2:
-                stores[chunk - 2].wait()
-            total = shared["z_out"][0, :, chunk * 512 : (chunk + 1) * 512].astype(F32)
+            if chunk + 3 < chunks:
+                loads[chunk + 3].start()
+            if chunk >= 4:
+                stores[chunk - 4].wait()
+            total = shared["z_out"][0, :, chunk * 128 : (chunk + 1) * 128].astype(F32)
             for step in range(spot.outer - 1):
-                total = total + shared["z_stage"][chunk % 2, step].astype(F32)
-            shared["o_stage"][chunk % 2] = total
+                total = total + shared["z_stage"][chunk % 4, step].astype(F32)
+            shared["o_stage"][chunk % 4] = total
             stores[chunk].start()
-        for store in stores[-2:]:
+        for store in stores[-4:]:
             store.wait()
 
 
@@ -739,6 +741,7 @@
     buf3,
     buf4,
     buf5,
+    buf6,
     core_send,
     core_recv,
     x_send,
@@ -793,8 +796,8 @@
     }
     down = Reduce(spot, buf1, buf2, slice(0, hidden), land_down, grad_down, shared, 0, False)
     up = Reduce(spot, buf4, buf3, slice(0, hidden), land_up, grad_up, shared, 1, False)
-    out = Reduce(spot, buf1, buf2, tail, land_out, grad_out, shared, 2, False)
-    qkv = Reduce(spot, buf4, buf5, slice(0, triple), land_qkv, grad_qkv, shared, 3, True)
+    qkv = Reduce(spot, buf6, buf5, slice(0, triple), land_qkv, grad_qkv, shared, 2, False)
+    out = Reduce(spot, buf1, buf2, tail, land_out, grad_out, shared, 3, True)
 
     def fetch(source, target, slot):
         copy = pltpu.make_async_copy(source, target, load_sem.at[slot])
@@ -807,6 +810,7 @@
     slopes = [fetch(slope_all.at[pl.ds(part * rows, rows)], (spare, input_grad)[part % 2], 3 + part % 2) for part in range(2)]
     load_h = fetch(h2_all, buf4, 5)
     load_c = fetch(cotangent, line, 6)
+    load_n = fetch(h1_all, buf6, 7)
     spot.meet(True)
     vectors[...] = jnp.zeros_like(vectors)
     biases[...] = jnp.zeros_like(biases)
@@ -816,6 +820,18 @@
     for step in order:
         down.produce(step)
     load_w.wait()
+    tensor = (core_send, core_recv, x_send, x_recv)
+
+    def down_part(rank, index):
+        return jnp.dot(buf2[block_of(rank, rows), :], weight_v[:, block_of(index, 512)], preferred_element_type=F32)
+
+    def take_out(index, total):
+        where = block_of(index, 512)
+        layer_out[:, where] = (spare[:, where] + total + sums[5:6, where]).astype(BF16)
+
+    end = tensor_sum(
+        spot, down_part, *tensor, s_send, s_recv, take_out, between=lambda: down.serve(1)
+    )
     for part in range(length // rows):
         held = (spare, input_grad)[part % 2]
         slopes[part].wait()
@@ -831,13 +847,22 @@
         lax.fori_loop(0, hidden // 512, lower, 0)
         if part + 2 < length // rows:
             slopes.append(fetch(slope_all.at[pl.ds((part + 2) * rows, rows)], held, 3 + part % 2))
+        if part == 1:
+            down.serve(2)
+    load_s = fetch(second, spare, 3)
+    load_s.wait()
+    end()
+    spot.release(ready)
     load_w = fetch(w1, weight_v, 2)
-    load_s = fetch(second, spare, 3)
-    down.hold()
+    load_h.wait()
+    down.serve(3)
+    down.hold((0,))
     load_q = fetch(qkv_all, buf2.at[:, pl.ds(0, triple)], 0)
     load_m = fetch(mixed_all, buf2.at[:, pl.ds(triple, width)], 1)
+    up.produce(1)
+    up.produce(2)
+    up.produce(3)
     load_w.wait()
-    load_h.wait()
 
     def h2_part(rank, index):
         return row_dot(buf3[block_of(rank, rows), :], weight_v[block_of(index, 512), :])
@@ -845,16 +870,14 @@
     def take_h2(index, total):
         input_grad[:, block_of(index, 512)] = total
 
-    tensor = (core_send, core_recv, x_send, x_recv)
+    pl.semaphore_wait(ready, 2)
     end = tensor_sum(spot, h2_part, *tensor, s_send, s_recv, take_h2)
-    down.serve(1)
-    up.produce(1)
-    down.serve(2)
-    up.produce(2)
+    down.serve(0)
+    up.produce(0)
+    up.serve(1)
     end()
     spot.release(ready)
     load_o = fetch(wo, weight_v.at[pl.ds(0, width)], 2)
-    load_s.wait()
     load_c.wait()
     strip = 32
     base = spot.tensor * rows
@@ -882,8 +905,8 @@
     lax.fori_loop(0, rows // strip, back2, 0)
     gather = TensorGather(spot, buf1.at[block_of(spot.tensor, rows)], buf1, rows, g_send, g_recv)
     load_t = fetch(tokens, line, 6)
-    down.serve(3)
-    up.produce(3)
+    up.serve(2)
+    down.settle()
     gather.pass_on()
     load_o.wait()
     gather.finish()
@@ -933,11 +956,12 @@
         biases[5:6, q_at] += jnp.sum(dv_sum[...], axis=0, keepdims=True)
         return carry
 
-    half = heads // 2
-    lax.fori_loop(0, half, attend, 0)
-    down.serve(0)
-    up.produce(0)
-    lax.fori_loop(half, heads, attend, 0)
+    lax.fori_loop(0, heads, attend, 0)
+    load_n.wait()
+    qkv.produce(1)
+    qkv.produce(2)
+    up.serve(3)
+    qkv.produce(3)
     load_w.wait()
 
     def h1_part(rank, index):
@@ -948,11 +972,11 @@
 
     pl.semaphore_wait(ready, 2)
     end = tensor_sum(spot, h1_part, *tensor, s_send, s_recv, take_h1)
-    up.serve(1)
+    up.serve(0)
+    qkv.produce(0)
+    qkv.serve(1)
     out.produce(1)
     end()
-    spot.release(ready)
-    load_w = fetch(w2, weight_v, 2)
     load_t.wait()
 
     def back1(index, carry):
@@ -962,7 +986,6 @@
         return carry
 
     lax.fori_loop(0, rows // strip, back1, 0)
-    load_s = fetch(second, spare, 3)
     share = grad_up.shape[0]
     vector_copies, bias_copies = [], []
     for step in range(1, count):
@@ -976,11 +999,9 @@
         copy.start()
     vector_in[spot.dp] = vectors[:, block_of(spot.dp, share)]
     bias_in[spot.dp] = biases[...]
-    up.serve(2)
+    up.settle()
+    qkv.serve(2)
     out.produce(2)
-    down.settle()
-    up.serve(3)
-    out.produce(3)
     for copy in vector_copies + bias_copies:
         copy.wait_recv()
     total, bias_total = vector_in[0], bias_in[0]
@@ -996,45 +1017,21 @@
     for copy in part_copies:
         copy.start()
     part_in[spot.tensor] = part_sum[...]
-    up.serve(0)
-    out.produce(0)
-    load_b = fetch(gated_all, buf3, 0)
-    load_h = fetch(h1_all, buf4, 1)
+    qkv.serve(3)
+    out.produce(3)
     for copy in part_copies:
         copy.wait_recv()
     vector_sums[...] = part_in[0] + part_in[1] + part_in[2] + part_in[3]
-    load_h.wait()
-    load_b.wait()
-    load_w.wait()
-    load_s.wait()
+    qkv.serve(0)
+    out.produce(0)
     out.serve(1)
-    qkv.produce(1)
     out.serve(2)
-    qkv.produce(2)
     out.serve(3)
-    qkv.produce(3)
-    up.settle()
-    out.serve(0)
-    qkv.produce(0)
-
-    def down_part(rank, index):
-        return jnp.dot(buf3[block_of(rank, rows), :], weight_v[:, block_of(index, 512)], preferred_element_type=F32)
-
-    def take_out(index, total):
-        where = block_of(index, 512)
-        layer_out[:, where] = (spare[:, where] + total + sums[5:6, where]).astype(BF16)
-
-    pl.semaphore_wait(ready, 2)
-    end = tensor_sum(spot, down_part, *tensor, s_send, s_recv, take_out)
-    out.settle()
-    qkv.serve(1)
-    end()
-    qkv.serve(2)
-    qkv.serve(3)
-    qkv.serve(0)
     for copy in vector_copies + bias_copies + part_copies:
         copy.wait_send()
     qkv.settle()
+    out.serve(0)
+    out.settle()
     for copy in list(shared["y_busy"].values()) + list(shared["z_busy"].values()):
         copy.wait_send()
 
@@ -1077,6 +1074,7 @@
             pltpu.VMEM(wide, BF16),
             pltpu.VMEM(wide, BF16),
             pltpu.VMEM(wide, BF16),
+            pltpu.VMEM(wide, BF16),
             pltpu.VMEM((2, rows, features), BF16),
             pltpu.VMEM((2, rows, features), BF16),
             pltpu.VMEM((rows, features), BF16),
@@ -1084,8 +1082,8 @@
             pltpu.VMEM((outer, share, hidden), BF16),
             pltpu.VMEM((outer, share, hidden), BF16),
             pltpu.VMEM((outer, share, hidden), BF16),
-            pltpu.VMEM((2, outer - 1, share, 512), BF16),
-            pltpu.VMEM((2, share, 512), F32),
+            pltpu.VMEM((4, outer - 1, share, 128), BF16),
+            pltpu.VMEM((4, share, 128), F32),
             pltpu.VMEM((rows, features), F32),
             pltpu.VMEM((rows, features), BF16),
             pltpu.VMEM((length, width // heads), F32),
@@ -1110,8 +1108,8 @@
             dma((count,)),
             dma((3,)),
             dma((3,)),
-            dma((4,)),
-            dma((7,)),
+            dma((8,)),
+            dma((8,)),
             regular,
             regular,
         ],

time: 658 us -> 628 us (0.954)
  Pallas kernels: 627 us -> 593 us
    pallas_call x1, Pallas kernels: 356 us -> 322 us  [backward_call(): pl.pallas_call(functools.partial(backward_kernel, heads, count), out_shap...]
where the time goes in v4:
time: 628 us; the launch traced here: 616 us
  Pallas kernels  593 us (94%)
  local copies, waits for them, and re-layouts  17.7 us (3%)
    pallas_call x1, Pallas kernels, backward_call(): pl.pallas_call(functools.partial(backward_kernel, heads, count), out_shap...  322 us
    pallas_call x1, Pallas kernels, forward_call(): pl.pallas_call(functools.partial(forward_kernel, heads, count), out_shape...  272 us

profile of v4, /device:TPU:9, one launch (start us, length us, event | category | flops | bytes accessed | tf_op | source)
XLA Modules:
  0.0 616.1 jit_solution(13518301238505166766)
XLA Ops:
  0.7 0.7 pad_maximum_fusion.1
  1.4 0.1 tile.10
  1.5 0.7 stack.21
  2.2 0.7 stack.22
  2.9 0.7 stack.23
  3.5 0.7 stack.24
  4.2 0.7 stack.25
  4.8 0.7 stack.26
  5.5 0.6 maximum_convert_fusion.small
  6.8 2.0 pad_maximum_fusion.qkv_shard
  8.8 271.6 %shard_map.305 = (bf16[2048,1536]{1,0:T(8,128)(2,1)}, bf16[512,2048]{1,0:T(8,128)(2,1)}, bf16[2048,2048]{1,0:T(8,128)(2,1)}, bf16[2048,2048]{1,0:T(8,128)(2,1)},...) custom-call(s32[1]{0:T(128)S(6)} %copy.42.prefix, ...), custom_call_target="tpu_custom_call" | custom-call | tf_op jit(solution)/shard_map/pallas_call | solution.py:538
  280.4 321.6 %shard_map.306 = (bf16[256,2048]{1,0:T(8,128)(2,1)}, f32[256,2048]{1,0:T(8,128)}, f32[256,2048]{1,0:T(8,128)}, f32[256,2048]{1,0:T(8,128)}, f32[256,512]{1,0:T(8...) custom-call(s32[1]{0:T(128)S(6)} %copy.42.prefix, ...), custom_call_target="tpu_custom_call" | custom-call | tf_op jit(solution)/shard_map/pallas_call | solution.py:1052
  602.0 0.0 copy-start.2
  602.0 3.0 copy.38
  605.0 0.0 copy-done.2
  605.0 0.0 copy-start.4
  605.0 0.0 copy-start.5
  605.1 0.0 copy-start.3
  605.1 1.2 fusion.7
  606.2 0.0 copy-start.1
  606.2 2.2 copy.37
  608.4 0.0 copy-done.4
  608.4 0.7 constant_dynamic-slice_fusion.6
  609.1 0.0 copy-done.5
  609.1 0.1 reshape.53
  609.2 0.5 fusion.1
  609.7 0.7 constant_dynamic-slice_fusion.7
  610.4 0.6 constant_dynamic-slice_fusion.8
  611.0 0.0 copy-done.3
  611.1 1.0 copy.43
  612.0 0.0 copy-done.1
  612.0 0.0 copy-start
  612.0 1.3 copy.44
  613.3 1.0 copy-done
  614.4 1.3 copy.45
  (9 shorter events, 0.1 us)
Async XLA Ops:
  602.0 3.0 copy-start.2
  605.0 3.4 copy-start.4
  605.0 4.1 copy-start.5
  605.1 6.0 copy-start.3
  606.2 5.8 copy-start.1
  612.0 2.3 copy-start

commit v5 on v4

--- a/solution.py
+++ b/solution.py
@@ -595,6 +595,11 @@
         self.share = target.shape[0]
         self.stepped = {}
         self.held = ()
+        row = spot.row
+        self.inner = (row == 1) | (row == 2)
+        self.steps = (
+            jnp.where(row == 0, 3, 1), jnp.where(self.inner, 3, 2), jnp.where(row == 0, 1, jnp.where(row == 3, 3, 2)), 0
+        )
 
     def block(self, owner, take):
         turned = jnp.transpose(self.left[:, block_of(owner, self.share)])
@@ -610,68 +615,116 @@
             shared["y_recv"].at[step], self.spot.beside(1), self.spot.tensor,
         )
 
-    def z_copy(self, step):
-        shared = self.shared
+    def z_copy(self, place):
+        shared, step = self.shared, self.steps[place]
         return remote(
-            shared["z_out"].at[step, :, pl.ds(0, self.width)], self.landing.at[step - 1],
-            shared["z_send"].at[step], shared["z_recv"].at[self.index, step], self.spot.across(step),
+            shared["z_out"].at[place, :, pl.ds(0, self.width)], self.landing.at[step - 1],
+            shared["z_send"].at[place], shared["z_recv"].at[self.index, step], self.spot.across(step),
             self.spot.tensor,
         )
 
-    def produce(self, step):
+    def near_copy(self):
         shared, spot = self.shared, self.spot
-        row = lax.rem(spot.row + step, spot.outer)
-        if step in shared["y_busy"]:
-            shared["y_busy"].pop(step).wait_send()
+        area = pl.ds(0, self.width)
+        return remote(
+            shared["z_out"].at[0, :, area], shared["near"].at[:, area], shared["z_send"].at[0], shared["near_recv"].at[0],
+            jnp.where(spot.row == 0, 1, 2) * spot.inner + spot.column, spot.tensor,
+        )
+
+    def produce(self, place):
+        shared, spot = self.shared, self.spot
+        row = lax.rem(spot.row + self.steps[place], spot.outer)
+        if place in shared["y_busy"]:
+            shared["y_busy"].pop(place).wait_send()
 
         def take(where, value):
-            shared["y_out"][step, :, where] = value.astype(BF16)
+            shared["y_out"][place, :, where] = value.astype(BF16)
 
         self.block(spot.beside(1, row), take)
         if self.index > 0:
             pl.semaphore_wait(shared["credit"], 1)
-        copy = self.y_copy(step)
+        copy = self.y_copy(place)
         copy.start()
-        shared["y_busy"][step] = copy
-
-    def hold(self, steps):
-        self.held = steps
-        for step in steps:
-
-            def take(where, value, step=step):
-                self.shared["z_out"][step, :, where] = value.astype(BF16)
-
-            self.block(self.spot.across(step), take)
-
-    def serve(self, step):
+        shared["y_busy"][place] = copy
+
+    def hold(self, places):
+        self.held = places
+        for place in places:
+
+            def take(where, value, place=place):
+                self.shared["z_out"][place, :, where] = value.astype(BF16)
+
+            self.block(self.spot.across(self.steps[place]), take)
+
+    def serve(self, place):
         shared, spot = self.shared, self.spot
-        self.y_copy(step).wait_recv()
-        if step in shared["z_busy"]:
-            shared["z_busy"].pop(step).wait_send()
+        self.y_copy(place).wait_recv()
+        if place in shared["z_busy"]:
+            shared["z_busy"].pop(place).wait_send()
         y_in, z_out = shared["y_in"], shared["z_out"]
-        if step in self.held:
+        if place in self.held:
             for start in range(0, self.width, 512):
                 where = slice(start, start + 512)
-                z_out[step, :, where] = (z_out[step, :, where].astype(F32) + y_in[step, :, where].astype(F32)).astype(BF16)
+                z_out[place, :, where] = (
+                    z_out[place, :, where].astype(F32) + y_in[place, :, where].astype(F32)
+                ).astype(BF16)
         else:
 
             def take(where, value):
-                z_out[step, :, where] = (value + y_in[step, :, where].astype(F32)).astype(BF16)
-
-            self.block(spot.across(step), take)
+                z_out[place, :, where] = (value + y_in[place, :, where].astype(F32)).astype(BF16)
+
+            self.block(spot.across(self.steps[place]), take)
         if not self.last:
             pl.semaphore_signal(
                 shared["credit"], inc=1, device_id=(spot.beside(1), spot.tensor), device_id_type=MESH
             )
-        if step:
-            copy = self.z_copy(step)
-            copy.start()
-            shared["z_busy"][step] = copy
+        if place == 3:
+            return
+        if place == 0:
+
+            @pl.when(jnp.logical_not(self.inner))
+            def _():
+                if self.index > 0:
+                    pl.semaphore_wait(shared["near_free"], 1)
+                self.near_copy().start()
+
+            @pl.when(self.inner)
+            def _():
+                self.z_copy(0).start()
+
+        else:
+            if place == 2:
+
+                @pl.when(self.inner)
+                def _():
+                    self.near_copy().wait_recv()
+                    for start in range(0, self.width, 512):
+                        where = slice(start, start + 512)
+                        z_out[2, :, where] = (
+                            z_out[2, :, where].astype(F32) + shared["near"][:, where].astype(F32)
+                        ).astype(BF16)
+                    if not self.last:
+                        pl.semaphore_signal(
+                            shared["near_free"], inc=1,
+                            device_id=(jnp.where(spot.row == 1, 0, 3) * spot.inner + spot.column, spot.tensor),
+                            device_id_type=MESH,
+                        )
+
+            self.z_copy(place).start()
+        shared["z_busy"][place] = self.z_copy(place)
+
+    def landed(self, step):
+        shared = self.shared
+        remote(
+            shared["z_out"].at[0, :, pl.ds(0, self.width)], self.landing.at[step - 1], shared["z_send"].at[0],
+            shared["z_recv"].at[self.index, step], self.spot.across(1), self.spot.tensor,
+        ).wait_recv()
 
     def settle(self):
         shared, spot = self.shared, self.spot
-        for step in range(1, spot.outer):
-            self.z_copy(step).wait_recv()
+        pl.when(spot.row != 0)(lambda: self.landed(1))
+        self.landed(2)
+        pl.when(spot.row != 3)(lambda: self.landed(3))
         loads, stores = [], []
         chunks = self.width // 128
         for chunk in range(chunks):
@@ -690,9 +743,12 @@
                 loads[chunk + 3].start()
             if chunk >= 4:
                 stores[chunk - 4].wait()
-            total = shared["z_out"][0, :, chunk * 128 : (chunk + 1) * 128].astype(F32)
+            total = shared["z_out"][3, :, chunk * 128 : (chunk + 1) * 128].astype(F32)
             for step in range(spot.outer - 1):
-                total = total + shared["z_stage"][chunk % 4, step].astype(F32)
+                part = shared["z_stage"][chunk % 4, step].astype(F32)
+                if step != 1:
+                    part = jnp.where(spot.row == (0 if step == 0 else 3), 0.0, part)
+                total = total + part
             shared["o_stage"][chunk % 4] = total
             stores[chunk].start()
         for store in stores[-4:]:
@@ -742,6 +798,7 @@
     buf4,
     buf5,
     buf6,
+    near,
     core_send,
     core_recv,
     x_send,
@@ -777,8 +834,10 @@
     t_recv,
     stage_sem,
     load_sem,
+    near_recv,
     credit,
     ready,
+    near_free,
 ):
     spot = Spot(count)
     rows, features = line.shape
@@ -792,7 +851,7 @@
     shared = {
         "y_in": y_in, "y_out": y_out, "z_out": z_out, "z_stage": z_stage, "o_stage": o_stage, "y_send": y_send,
         "y_recv": y_recv, "z_send": z_send, "z_recv": z_recv, "credit": credit, "stage_sem": stage_sem,
-        "y_busy": {}, "z_busy": {},
+        "y_busy": {}, "z_busy": {}, "near": near, "near_recv": near_recv, "near_free": near_free,
     }
     down = Reduce(spot, buf1, buf2, slice(0, hidden), land_down, grad_down, shared, 0, False)
     up = Reduce(spot, buf4, buf3, slice(0, hidden), land_up, grad_up, shared, 1, False)
@@ -810,15 +869,13 @@
     slopes = [fetch(slope_all.at[pl.ds(part * rows, rows)], (spare, input_grad)[part % 2], 3 + part % 2) for part in range(2)]
     load_h = fetch(h2_all, buf4, 5)
     load_c = fetch(cotangent, line, 6)
-    load_n = fetch(h1_all, buf6, 7)
     spot.meet(True)
     vectors[...] = jnp.zeros_like(vectors)
     biases[...] = jnp.zeros_like(biases)
     load_a.wait()
     load_b.wait()
-    order = list(range(1, spot.outer)) + [0]
-    for step in order:
-        down.produce(step)
+    for place in range(spot.outer):
+        down.produce(place)
     load_w.wait()
     tensor = (core_send, core_recv, x_send, x_recv)
 
@@ -827,10 +884,10 @@
 
     def take_out(index, total):
         where = block_of(index, 512)
-        layer_out[:, where] = (spare[:, where] + total + sums[5:6, where]).astype(BF16)
+        buf6[0:rows, where] = (spare[:, where] + total + sums[5:6, where]).astype(BF16)
 
     end = tensor_sum(
-        spot, down_part, *tensor, s_send, s_recv, take_out, between=lambda: down.serve(1)
+        spot, down_part, *tensor, s_send, s_recv, take_out, between=lambda: down.serve(0)
     )
     for part in range(length // rows):
         held = (spare, input_grad)[part % 2]
@@ -848,20 +905,21 @@
         if part + 2 < length // rows:
             slopes.append(fetch(slope_all.at[pl.ds((part + 2) * rows, rows)], held, 3 + part % 2))
         if part == 1:
-            down.serve(2)
+            down.serve(1)
     load_s = fetch(second, spare, 3)
     load_s.wait()
     end()
     spot.release(ready)
+    store_l = fetch(buf6.at[pl.ds(0, rows)], layer_out, 7)
     load_w = fetch(w1, weight_v, 2)
     load_h.wait()
-    down.serve(3)
-    down.hold((0,))
+    down.serve(2)
+    down.hold((3,))
     load_q = fetch(qkv_all, buf2.at[:, pl.ds(0, triple)], 0)
     load_m = fetch(mixed_all, buf2.at[:, pl.ds(triple, width)], 1)
+    up.produce(0)
     up.produce(1)
     up.produce(2)
-    up.produce(3)
     load_w.wait()
 
     def h2_part(rank, index):
@@ -872,11 +930,13 @@
 
     pl.semaphore_wait(ready, 2)
     end = tensor_sum(spot, h2_part, *tensor, s_send, s_recv, take_h2)
-    down.serve(0)
-    up.produce(0)
-    up.serve(1)
+    down.serve(3)
+    up.produce(3)
+    up.serve(0)
     end()
     spot.release(ready)
+    store_l.wait()
+    load_n = fetch(h1_all, buf6, 7)
     load_o = fetch(wo, weight_v.at[pl.ds(0, width)], 2)
     load_c.wait()
     strip = 32
@@ -905,7 +965,7 @@
     lax.fori_loop(0, rows // strip, back2, 0)
     gather = TensorGather(spot, buf1.at[block_of(spot.tensor, rows)], buf1, rows, g_send, g_recv)
     load_t = fetch(tokens, line, 6)
-    up.serve(2)
+    up.serve(1)
     down.settle()
     gather.pass_on()
     load_o.wait()
@@ -958,24 +1018,24 @@
 
     lax.fori_loop(0, heads, attend, 0)
     load_n.wait()
+    qkv.produce(0)
     qkv.produce(1)
+    up.serve(2)
     qkv.produce(2)
+    load_w.wait()
+
+    def h1_part(rank, index):
+        return row_dot(buf5[block_of(rank, rows), 0:triple], weight_v[block_of(index, 512), 0:triple])
+
+    def take_h1(index, total):
+        spare[:, block_of(index, 512)] = total
+
+    pl.semaphore_wait(ready, 2)
+    end = tensor_sum(spot, h1_part, *tensor, s_send, s_recv, take_h1)
     up.serve(3)
     qkv.produce(3)
-    load_w.wait()
-
-    def h1_part(rank, index):
-        return row_dot(buf5[block_of(rank, rows), 0:triple], weight_v[block_of(index, 512), 0:triple])
-
-    def take_h1(index, total):
-        spare[:, block_of(index, 512)] = total
-
-    pl.semaphore_wait(ready, 2)
-    end = tensor_sum(spot, h1_part, *tensor, s_send, s_recv, take_h1)
-    up.serve(0)
-    qkv.produce(0)
-    qkv.serve(1)
-    out.produce(1)
+    qkv.serve(0)
+    out.produce(0)
     end()
     load_t.wait()
 
@@ -1000,8 +1060,8 @@
     vector_in[spot.dp] = vectors[:, block_of(spot.dp, share)]
     bias_in[spot.dp] = biases[...]
     up.settle()
-    qkv.serve(2)
-    out.produce(2)
+    qkv.serve(1)
+    out.produce(1)
     for copy in vector_copies + bias_copies:
         copy.wait_recv()
     total, bias_total = vector_in[0], bias_in[0]
@@ -1017,20 +1077,20 @@
     for copy in part_copies:
         copy.start()
     part_in[spot.tensor] = part_sum[...]
-    qkv.serve(3)
-    out.produce(3)
+    qkv.serve(2)
+    out.produce(2)
     for copy in part_copies:
         copy.wait_recv()
     vector_sums[...] = part_in[0] + part_in[1] + part_in[2] + part_in[3]
-    qkv.serve(0)
-    out.produce(0)
+    qkv.serve(3)
+    out.produce(3)
+    out.serve(0)
     out.serve(1)
     out.serve(2)
-    out.serve(3)
     for copy in vector_copies + bias_copies + part_copies:
         copy.wait_send()
     qkv.settle()
-    out.serve(0)
+    out.serve(3)
     out.settle()
     for copy in list(shared["y_busy"].values()) + list(shared["z_busy"].values()):
         copy.wait_send()
@@ -1066,7 +1126,7 @@
             shape((outer - 1, share, triple), BF16),
         ],
         in_specs=[pl.BlockSpec(memory_space=pltpu.SMEM), vmem] + [hbm] * 10 + [vmem] + [hbm] * 4,
-        out_specs=[vmem] * 2 + [hbm] * 4 + [vmem] * 2 + [hbm] * 4,
+        out_specs=[hbm, vmem] + [hbm] * 4 + [vmem] * 2 + [hbm] * 4,
         scratch_shapes=[
             pltpu.VMEM((hidden, features), BF16),
             pltpu.VMEM(wide, BF16),
@@ -1075,6 +1135,7 @@
             pltpu.VMEM(wide, BF16),
             pltpu.VMEM(wide, BF16),
             pltpu.VMEM(wide, BF16),
+            pltpu.VMEM((share, hidden), BF16),
             pltpu.VMEM((2, rows, features), BF16),
             pltpu.VMEM((2, rows, features), BF16),
             pltpu.VMEM((rows, features), BF16),
@@ -1110,6 +1171,8 @@
             dma((3,)),
             dma((8,)),
             dma((8,)),
+            dma((1,)),
+            regular,
             regular,
             regular,
         ],

time: 628 us -> 614 us (0.978)
  Pallas kernels: 593 us -> 582 us
    pallas_call x1, Pallas kernels: 322 us -> 310 us  [backward_call(): pl.pallas_call(functools.partial(backward_kernel, heads, count), out_shap...]
where the time goes in v5:
time: 614 us; the launch traced here: 605 us
  Pallas kernels  582 us (95%)
  local copies, waits for them, and re-layouts  17.7 us (3%)
    pallas_call x1, Pallas kernels, backward_call(): pl.pallas_call(functools.partial(backward_kernel, heads, count), out_shap...  310 us
    pallas_call x1, Pallas kernels, forward_call(): pl.pallas_call(functools.partial(forward_kernel, heads, count), out_shape...  272 us

profile of v5, /device:TPU:9, one launch (start us, length us, event | category | flops | bytes accessed | tf_op | source)
XLA Modules:
  0.0 604.6 jit_solution(12555426526157292225)
XLA Ops:
  0.7 0.7 pad_maximum_fusion.1
  1.4 0.1 tile.10
  1.5 0.7 stack.21
  2.2 0.7 stack.22
  2.9 0.7 stack.23
  3.5 0.7 stack.24
  4.2 0.7 stack.25
  4.8 0.7 stack.26
  5.5 0.6 maximum_convert_fusion.small
  6.8 2.0 pad_maximum_fusion.qkv_shard
  8.8 271.6 %shard_map.305 = (bf16[2048,1536]{1,0:T(8,128)(2,1)}, bf16[512,2048]{1,0:T(8,128)(2,1)}, bf16[2048,2048]{1,0:T(8,128)(2,1)}, bf16[2048,2048]{1,0:T(8,128)(2,1)},...) custom-call(s32[1]{0:T(128)S(6)} %copy.42.prefix, ...), custom_call_target="tpu_custom_call" | custom-call | tf_op jit(solution)/shard_map/pallas_call | solution.py:538
  280.4 310.1 %shard_map.306 = (bf16[256,2048]{1,0:T(8,128)(2,1)}, f32[256,2048]{1,0:T(8,128)}, f32[256,2048]{1,0:T(8,128)}, f32[256,2048]{1,0:T(8,128)}, f32[256,512]{1,0:T(8...) custom-call(s32[1]{0:T(128)S(6)} %copy.42.prefix, ...), custom_call_target="tpu_custom_call" | custom-call | tf_op jit(solution)/shard_map/pallas_call | solution.py:1112
  590.5 0.0 copy-start.2
  590.5 3.0 copy.38
  593.5 0.0 copy-done.2
  593.5 0.0 copy-start.4
  593.5 0.0 copy-start.5
  593.5 0.0 copy-start.3
  593.6 1.2 fusion.7
  594.7 0.0 copy-start.1
  594.7 2.2 copy.37
  596.9 0.0 copy-done.4
  596.9 0.7 constant_dynamic-slice_fusion.6
  597.6 0.0 copy-done.5
  597.6 0.1 reshape.53
  597.7 0.5 fusion.1
  598.2 0.7 constant_dynamic-slice_fusion.7
  598.9 0.6 constant_dynamic-slice_fusion.8
  599.5 0.0 copy-done.3
  599.5 1.0 copy.43
  600.5 0.0 copy-done.1
  600.5 0.0 copy-start
  600.5 1.3 copy.44
  601.8 1.0 copy-done
  602.9 1.3 copy.45
  (9 shorter events, 0.1 us)
Async XLA Ops:
  590.5 3.0 copy-start.2
  593.5 3.4 copy-start.4
  593.5 4.1 copy-start.5
  593.5 6.0 copy-start.3
  594.7 5.8 copy-start.1
  600.5 2.3 copy-start

commit v6 on v5

--- a/solution.py
+++ b/solution.py
@@ -482,7 +482,6 @@
     gather2.finish()
     gather_d.finish()
     keep(h2v, h2_all)
-    stored = []
     for part in range(2):
         spread.arrived(3 + part)
         locals_[3 + part].wait()
@@ -490,27 +489,35 @@
         load = pltpu.make_async_copy(w1.at[:, lanes_of], w1_v.at[:, lanes_of], local_sem.at[14])
         load.start()
         load.wait()
-        for block in range(length // rows):
-            slot = block % 2
-            if len(stored) >= 2:
-                stored[-2].wait()
-
-            def lift(index, carry, block=block, slot=slot, part=part):
+
+        def stored(block, lanes_of=lanes_of):
+            slot = lax.rem(block, 2)
+            return pltpu.make_async_copy(
+                slope_v.at[slot], slope_all.at[block_of(block, rows), lanes_of], local_sem.at[15 + slot]
+            )
+
+        def lift_rows(block, carry, part=part, stored=stored):
+            where_rows = block_of(block, rows)
+            if part == 0:
+                pl.when(block >= 2)(lambda: stored(block).wait())
+            else:
+                stored(block).wait()
+
+            def lift(index, carry):
                 where = block_of(part * (tall // 512) + index, 512)
-                u = jnp.dot(
-                    h2v[block * rows : (block + 1) * rows, :], w1_v[:, where], preferred_element_type=F32
-                ) + sums[7:8, where]
+                u = jnp.dot(h2v[where_rows, :], w1_v[:, where], preferred_element_type=F32) + sums[7:8, where]
                 below = 0.5 * (1.0 + lax.erf(u * 0.7071067811865476))
-                gated_v[block * rows : (block + 1) * rows, where] = (u * below).astype(BF16)
-                slope_v[slot, :, block_of(index, 512)] = below + u * (0.3989422804014327 * jnp.exp(-0.5 * u * u))
+                gated_v[where_rows, where] = (u * below).astype(BF16)
+                slope_v[lax.rem(block, 2), :, block_of(index, 512)] = (
+                    below + u * (0.3989422804014327 * jnp.exp(-0.5 * u * u))
+                )
                 return carry
 
             lax.fori_loop(0, tall // 512, lift, 0)
-            copy = pltpu.make_async_copy(
-                slope_v.at[slot], slope_all.at[pl.ds(block * rows, rows), lanes_of], local_sem.at[15 + slot]
-            )
-            copy.start()
-            stored.append(copy)
+            stored(block).start()
+            return carry
+
+        lax.fori_loop(0, length // rows, lift_rows, 0)
         if part == 0:
             spread.forward(3)
     keep(gated_v, gated_all)
@@ -519,7 +526,7 @@
     spread.finish()
     for copy in small_copies:
         copy.wait_send()
-    for copy in locals_[5:] + stored[-2:]:
+    for copy in locals_[5:] + [stored(jnp.int32(block)) for block in range(2)]:
         copy.wait()
 
 
@@ -603,9 +610,13 @@
 
     def block(self, owner, take):
         turned = jnp.transpose(self.left[:, block_of(owner, self.share)])
-        for start in range(0, self.width, 512):
-            source = self.right[:, self.lanes.start + start : self.lanes.start + start + 512]
-            take(slice(start, start + 512), jnp.dot(turned, source, preferred_element_type=F32))
+
+        def body(index, carry):
+            source = self.right[:, pl.ds(pl.multiple_of(self.lanes.start + index * 512, 512), 512)]
+            take(block_of(index, 512), jnp.dot(turned, source, preferred_element_type=F32))
+            return carry
+
+        lax.fori_loop(0, self.width // 512, body, 0)
 
     def y_copy(self, step):
         shared = self.shared
@@ -725,34 +736,40 @@
         pl.when(spot.row != 0)(lambda: self.landed(1))
         self.landed(2)
         pl.when(spot.row != 3)(lambda: self.landed(3))
-        loads, stores = [], []
         chunks = self.width // 128
-        for chunk in range(chunks):
-            slot = chunk % 4
-            loads.append(pltpu.make_async_copy(
-                self.landing.at[:, :, pl.ds(chunk * 128, 128)], shared["z_stage"].at[slot], shared["stage_sem"].at[slot]
-            ))
-            stores.append(pltpu.make_async_copy(
-                shared["o_stage"].at[slot], self.target.at[:, pl.ds(chunk * 128, 128)], shared["stage_sem"].at[4 + slot]
-            ))
-        for load in loads[:3]:
-            load.start()
-        for chunk in range(chunks):
-            loads[chunk].wait()
-            if chunk + 3 < chunks:
-                loads[chunk + 3].start()
-            if chunk >= 4:
-                stores[chunk - 4].wait()
-            total = shared["z_out"][3, :, chunk * 128 : (chunk + 1) * 128].astype(F32)
+
+        def load(chunk):
+            slot = lax.rem(chunk, 4)
+            return pltpu.make_async_copy(
+                self.landing.at[:, :, block_of(chunk, 128)], shared["z_stage"].at[slot], shared["stage_sem"].at[slot]
+            )
+
+        def store(chunk):
+            slot = lax.rem(chunk, 4)
+            return pltpu.make_async_copy(
+                shared["o_stage"].at[slot], self.target.at[:, block_of(chunk, 128)], shared["stage_sem"].at[4 + slot]
+            )
+
+        def add(chunk, carry):
+            slot = lax.rem(chunk, 4)
+            load(chunk).wait()
+            pl.when(chunk + 3 < chunks)(lambda: load(chunk + 3).start())
+            pl.when(chunk >= 4)(lambda: store(chunk - 4).wait())
+            total = shared["z_out"][3, :, block_of(chunk, 128)].astype(F32)
             for step in range(spot.outer - 1):
-                part = shared["z_stage"][chunk % 4, step].astype(F32)
+                part = shared["z_stage"][slot, step].astype(F32)
                 if step != 1:
                     part = jnp.where(spot.row == (0 if step == 0 else 3), 0.0, part)
                 total = total + part
-            shared["o_stage"][chunk % 4] = total
-            stores[chunk].start()
-        for store in stores[-4:]:
-            store.wait()
+            shared["o_stage"][slot] = total
+            store(chunk).start()
+            return carry
+
+        for chunk in range(3):
+            load(jnp.int32(chunk)).start()
+        lax.fori_loop(0, chunks, add, 0)
+        for chunk in range(chunks - 4, chunks):
+            store(jnp.int32(chunk)).wait()
 
 
 def row_dot(left, right):

time: 614 us -> 608 us (level); the launches traced: 605 us -> 606 us
  no operation moved by 1% of the time
where the time goes in v6:
time: 608 us; the launch traced here: 606 us
  Pallas kernels  583 us (96%)
  local copies, waits for them, and re-layouts  17.7 us (3%)
    pallas_call x1, Pallas kernels, backward_call(): pl.pallas_call(functools.partial(backward_kernel, heads, count), out_shap...  311 us
    pallas_call x1, Pallas kernels, forward_call(): pl.pallas_call(functools.partial(forward_kernel, heads, count), out_shape...  272 us

profile of v6, /device:TPU:9, one launch (start us, length us, event | category | flops | bytes accessed | tf_op | source)
XLA Modules:
  0.0 605.5 jit_solution(7199853258045236856)
XLA Ops:
  0.7 0.7 pad_maximum_fusion.1
  1.4 0.1 tile.10
  1.5 0.7 stack.21
  2.2 0.7 stack.22
  2.9 0.7 stack.23
  3.5 0.7 stack.24
  4.2 0.7 stack.25
  4.8 0.7 stack.26
  5.5 0.6 maximum_convert_fusion.small
  6.8 2.0 pad_maximum_fusion.qkv_shard
  8.8 271.6 %shard_map.305 = (bf16[2048,1536]{1,0:T(8,128)(2,1)}, bf16[512,2048]{1,0:T(8,128)(2,1)}, bf16[2048,2048]{1,0:T(8,128)(2,1)}, bf16[2048,2048]{1,0:T(8,128)(2,1)},...) custom-call(s32[1]{0:T(128)S(6)} %copy.42.prefix, ...), custom_call_target="tpu_custom_call" | custom-call | tf_op jit(solution)/shard_map/pallas_call | solution.py:545
  280.4 311.4 %shard_map.306 = (bf16[256,2048]{1,0:T(8,128)(2,1)}, f32[256,2048]{1,0:T(8,128)}, f32[256,2048]{1,0:T(8,128)}, f32[256,2048]{1,0:T(8,128)}, f32[256,512]{1,0:T(8...) custom-call(s32[1]{0:T(128)S(6)} %copy.42.prefix, ...), custom_call_target="tpu_custom_call" | custom-call | tf_op jit(solution)/shard_map/pallas_call | solution.py:1129
  591.9 0.0 copy-start.2
  591.9 3.0 copy.38
  594.9 0.0 copy-done.2
  594.9 0.0 copy-start.4
  594.9 0.0 copy-start.5
  594.9 0.0 copy-start.3
  594.9 1.2 fusion.7
  596.1 0.0 copy-start.1
  596.1 2.2 copy.37
  598.3 0.0 copy-done.4
  598.3 0.7 constant_dynamic-slice_fusion.6
  599.0 0.0 copy-done.5
  599.0 0.1 reshape.53
  599.1 0.5 fusion.1
  599.6 0.7 constant_dynamic-slice_fusion.7
  600.3 0.6 constant_dynamic-slice_fusion.8
  600.9 0.0 copy-done.3
  600.9 1.0 copy.43
  601.9 0.0 copy-done.1
  601.9 0.0 copy-start
  601.9 1.3 copy.44
  603.2 1.0 copy-done
  604.2 1.3 copy.45
  (9 shorter events, 0.1 us)
Async XLA Ops:
  591.9 3.0 copy-start.2
  594.9 3.4 copy-start.4
  594.9 4.1 copy-start.5
  594.9 6.0 copy-start.3
  596.1 5.8 copy-start.1
  601.9 2.3 copy-start

commit v7 on v6

--- a/solution.py
+++ b/solution.py
@@ -71,7 +71,7 @@
 
 
 class Spread:
-    AHEAD = 3
+    AHEAD = 2
 
     def __init__(self, spot, pieces, late, own_at, sems):
         self.spot, self.pieces, self.late, self.sems = spot, pieces, late, sems

time: 608 us -> 608 us (level)
    pallas_call x1, Pallas kernels: 311 us -> 303 us  [backward_call(): pl.pallas_call(functools.partial(backward_kernel, heads, count), out_shap...]
where the time goes in v7:
time: 608 us; the launch traced here: 601 us
  Pallas kernels  578 us (95%)
  local copies, waits for them, and re-layouts  17.7 us (3%)
    pallas_call x1, Pallas kernels, backward_call(): pl.pallas_call(functools.partial(backward_kernel, heads, count), out_shap...  303 us
    pallas_call x1, Pallas kernels, forward_call(): pl.pallas_call(functools.partial(forward_kernel, heads, count), out_shape...  275 us

profile of v7, /device:TPU:9, one launch (start us, length us, event | category | flops | bytes accessed | tf_op | source)
XLA Modules:
  0.0 600.8 jit_solution(8164848871173260696)
XLA Ops:
  0.7 0.7 pad_maximum_fusion.1
  1.4 0.1 tile.10
  1.5 0.7 stack.21
  2.2 0.7 stack.22
  2.9 0.7 stack.23
  3.5 0.7 stack.24
  4.2 0.7 stack.25
  4.8 0.7 stack.26
  5.5 0.6 maximum_convert_fusion.small
  6.8 2.0 pad_maximum_fusion.qkv_shard
  8.8 275.0 %shard_map.305 = (bf16[2048,1536]{1,0:T(8,128)(2,1)}, bf16[512,2048]{1,0:T(8,128)(2,1)}, bf16[2048,2048]{1,0:T(8,128)(2,1)}, bf16[2048,2048]{1,0:T(8,128)(2,1)},...) custom-call(s32[1]{0:T(128)S(6)} %copy.42.prefix, ...), custom_call_target="tpu_custom_call" | custom-call | tf_op jit(solution)/shard_map/pallas_call | solution.py:545
  283.8 303.3 %shard_map.306 = (bf16[256,2048]{1,0:T(8,128)(2,1)}, f32[256,2048]{1,0:T(8,128)}, f32[256,2048]{1,0:T(8,128)}, f32[256,2048]{1,0:T(8,128)}, f32[256,512]{1,0:T(8...) custom-call(s32[1]{0:T(128)S(6)} %copy.42.prefix, ...), custom_call_target="tpu_custom_call" | custom-call | tf_op jit(solution)/shard_map/pallas_call | solution.py:1129
  587.2 0.0 copy-start.2
  587.2 3.0 copy.38
  590.2 0.0 copy-done.2
  590.2 0.0 copy-start.4
  590.2 0.0 copy-start.5
  590.2 0.0 copy-start.3
  590.2 1.2 fusion.7
  591.4 0.0 copy-start.1
  591.4 2.2 copy.37
  593.6 0.0 copy-done.4
  593.6 0.7 constant_dynamic-slice_fusion.6
  594.3 0.0 copy-done.5
  594.3 0.1 reshape.53
  594.3 0.5 fusion.1
  594.9 0.7 constant_dynamic-slice_fusion.7
  595.5 0.6 constant_dynamic-slice_fusion.8
  596.2 0.0 copy-done.3
  596.2 1.0 copy.43
  597.2 0.0 copy-done.1
  597.2 0.0 copy-start
  597.2 1.3 copy.44
  598.5 1.0 copy-done
  599.5 1.3 copy.45
  (9 shorter events, 0.1 us)
Async XLA Ops:
  587.2 3.0 copy-start.2
  590.2 3.4 copy-start.4
  590.2 4.1 copy-start.5
  590.2 6.0 copy-start.3
  591.4 5.8 copy-start.1
  597.2 2.3 copy-start
